TPU v7x, 32 devices: a whole 2x2x4 slice. The times are simulated.
32 devices in a mesh: space: 16 (over z, y, x), rhs: 2 (over core).
Axes of the slice: x: 2, y: 2, z: 4, core: 2. Of those that a mesh axis runs over, the one named last changes fastest.
Arguments:
- positions: float32 [4096, 3, 128], P('space'), may hold values from -0.5 to 0.5
- point_counts: int32 [4096], P('space'), may hold values from 1 to 128
- charges: bfloat16 [4096, 8, 128], P('space', 'rhs'), may hold values from -1.1953125 to 1.1953125
- frequencies: float32 [3, 128], replicated, may hold values from -8 to 8
- octants: int32 [4096], P('space'), may hold values from 0 to 7, as said below
- child_shift: bfloat16 [8, 256, 256], replicated, may hold values from -0.125 to 0.125
- to_wave: bfloat16 [256, 256], replicated, may hold values from -0.375 to 0.375
- to_local: bfloat16 [256, 256], replicated, may hold values from -0.375 to 0.375
- translation: float32 [316, 256], replicated, may hold values from -0.3086067 to 0.3086067
- send_leaf: int32 [16, 8, 48], P('space'), may hold values from 0 to 255
- send_parent: int32 [16, 8, 16], P('space'), may hold values from 0 to 31
- leaf_pairs: int32 [4096, 2, 189], P('space'), may hold values from 0 to 799, as said below
- parent_pairs: int32 [512, 2, 189], P('space'), may hold values from 0 to 799, as said below
Outputs:
- leaf_locals: float32 [4096, 8, 256], P('space', 'rhs')
- parent_locals: float32 [512, 8, 256], P('space', 'rhs')
Inputs may be any that keep to these rules, and one draw needn't show every extreme that they name: `octants`: each aligned group of 8 leaves holds every octant 0 to 7 once. `leaf_pairs`: entries [., 0, .] are rows of the device's source table, entries [., 1, .] offset classes below 316. `parent_pairs`: entries [., 0, .] are rows of the device's source table, entries [., 1, .] offset classes below 316.
All inputs are finite; a program needn't handle non-finite values.
Results may differ from a plain program's by a relative error of at most 0.0056.
Values may be sent and summed in bfloat16 or wider, within the bound.
No kernel may reach another device: no remote copies, remote signals or barrier semaphores. Data moves between devices by JAX's collectives and lax.ppermute only.
A program may use at most 128 MiB of HBM per device.

v0:
```python
import jax
import jax.numpy as jnp
from jax import lax
from jax.sharding import PartitionSpec as P


def from_behind(value, axis, steps):
    count = lax.axis_size(axis)
    initial, last = (max(0, -steps), min(count, count - steps))
    return lax.ppermute(value, axis, [(source, source + steps) for source in range(initial, last)])


def plane_basis(positions, frequencies):
    phase = (
        positions[:, 0, :, None] * frequencies[0]
        + positions[:, 1, :, None] * frequencies[1]
        + positions[:, 2, :, None] * frequencies[2]
    )
    return jnp.concatenate([jnp.cos(phase), jnp.sin(phase)], axis=-1).astype(jnp.bfloat16)


def expand(positions, point_counts, charges, frequencies):
    basis = plane_basis(positions, frequencies)
    slot_ids = lax.broadcasted_iota(jnp.int32, (1, 1, charges.shape[2]), 2)
    masked = jnp.where(slot_ids < point_counts[:, None, None], charges, jnp.zeros_like(charges))
    product = jnp.einsum("brs,bsk->brk", masked, basis, preferred_element_type=jnp.float32)
    return product.astype(jnp.bfloat16)


def upward(multipole, octants, child_shift):
    leaf_count, width_r, width_k = multipole.shape
    children = multipole.reshape(leaf_count // 8, 8, width_r, width_k)
    octant_rows = octants.reshape(leaf_count // 8, 8)
    summed = jnp.zeros((leaf_count // 8 * width_r, child_shift.shape[2]), jnp.float32)
    for octant_id in range(8):
        chosen = jnp.where(
            (octant_rows == octant_id)[:, :, None, None], children, jnp.zeros_like(children)
        )
        chosen = jnp.sum(chosen, axis=1)
        summed = summed + jnp.dot(
            chosen.reshape(-1, width_k), child_shift[octant_id], preferred_element_type=jnp.float32
        )
    return summed.reshape(leaf_count // 8, width_r, -1).astype(jnp.bfloat16)


def apply_matrix(values, matrix):
    in_shape = values.shape
    flattened = jnp.dot(
        values.reshape(-1, in_shape[-1]), matrix, preferred_element_type=jnp.float32
    )
    return flattened.reshape(in_shape[:-1] + (matrix.shape[1],))


def interact(source_table, pairs, translation, block_size):
    row_total, width_r, width_k = source_table.shape
    half_width = width_k // 2
    flat_table = source_table.reshape(row_total, width_r * width_k)

    def one_block(block_pairs):
        list_len = block_pairs.shape[2]
        picked = jnp.take(flat_table, block_pairs[:, 0].reshape(-1), axis=0)
        picked = picked.reshape(block_pairs.shape[0], list_len, width_r, width_k).astype(
            jnp.float32
        )
        factor = jnp.take(translation, block_pairs[:, 1].reshape(-1), axis=0)
        factor = factor.reshape(block_pairs.shape[0], list_len, 1, width_k)
        wave_re = picked[..., :half_width]
        wave_im = picked[..., half_width:]
        factor_re = factor[..., :half_width]
        factor_im = factor[..., half_width:]
        real_part = jnp.sum(factor_re * wave_re - factor_im * wave_im, axis=1)
        imag_part = jnp.sum(factor_re * wave_im + factor_im * wave_re, axis=1)
        return jnp.concatenate([real_part, imag_part], axis=-1).astype(jnp.bfloat16)

    grouped = pairs.reshape((-1, block_size) + pairs.shape[1:])
    result = lax.map(one_block, grouped)
    return result.reshape((pairs.shape[0],) + result.shape[2:])


def shards(
    positions,
    point_counts,
    charges,
    frequencies,
    octants,
    child_shift,
    to_wave,
    to_local,
    translation,
    send_leaf,
    send_parent,
    leaf_pairs,
    parent_pairs,
):
    share_rows = positions.shape[0] // lax.axis_size("rhs")
    first_row = lax.axis_index("rhs") * share_rows
    gathered_charges = lax.all_to_all(charges, "rhs", split_axis=0, concat_axis=1, tiled=True)
    partial_value = expand(
        lax.dynamic_slice_in_dim(positions, first_row, share_rows, 0),
        lax.dynamic_slice_in_dim(point_counts, first_row, share_rows, 0),
        gathered_charges,
        frequencies,
    )
    multipole = lax.all_to_all(partial_value, "rhs", split_axis=1, concat_axis=0, tiled=True)
    parent = upward(multipole, octants, child_shift)
    leaf_wave = apply_matrix(multipole, to_wave).astype(jnp.bfloat16)
    parent_wave = apply_matrix(parent, to_wave).astype(jnp.bfloat16)
    leaf_buffers = leaf_wave[send_leaf[0]]
    parent_buffers = parent_wave[send_parent[0]]
    near_count = send_leaf.shape[1] // 2
    offset_list = list(range(-near_count, 0)) + list(range(1, near_count + 1))
    leaf_blocks = []
    parent_blocks = []
    for slot_id, offset in enumerate(offset_list):
        arrived = from_behind((leaf_buffers[slot_id], parent_buffers[slot_id]), "space", offset)
        leaf_blocks.append(arrived[0])
        parent_blocks.append(arrived[1])
    source_table = jnp.concatenate([leaf_wave, parent_wave] + leaf_blocks + parent_blocks, axis=0)
    all_pairs = jnp.concatenate([leaf_pairs, parent_pairs], axis=0)
    incoming = interact(source_table, all_pairs, translation, parent_pairs.shape[0])
    local_all = apply_matrix(incoming, to_local)
    leaf_count = leaf_pairs.shape[0]
    return (local_all[:leaf_count], local_all[leaf_count:])


def solution(mesh):
    in_specs = (
        P("space", None, None),
        P("space"),
        P("space", "rhs", None),
        P(),
        P("space"),
        P(),
        P(),
        P(),
        P(),
        P("space", None, None),
        P("space", None, None),
        P("space", None, None),
        P("space", None, None),
    )
    out_specs = (P("space", "rhs", None), P("space", "rhs", None))
    return jax.shard_map(shards, mesh=mesh, in_specs=in_specs, out_specs=out_specs, check_vma=False)
```

profile of v0, /device:TPU:0, one launch (start us, length us, event | category | flops | bytes accessed | tf_op | source)
XLA Modules:
  0.0 1248.3 jit_solution(7450243800679755685)
XLA Ops:
  7.7 32.3 %cosine_convert_fusion = (bf16[128,128,128]{2,1,0:T(8,128)(2,1)S(1)}, bf16[128,128,128]{2,1,0:T(8,128)(2,1)S(1)}) fusion(f32[128]{0:T(128)S(1)} %get-tuple-element.93, f32[128,128]{1,0:T(8,128)S(1)} %get-tuple-element.81, f32[128]{0:T(128)S(1)} %get-tuple-element.94, f32[128,128]{1,0:T(8,128)S(1)} %get-tuple-element.80, f32[128]{0:T(128)S(1)} %get-tuple-element.92, ...), kind=kLoop, calls=%fused_computation.27 | loop fusion | flops 14680064 | bytes 8586752 | tf_op jit(solution)/shard_map/convert.12
  131.7 1114.0 %while.10 = (s32[]{:T(128)}, bf16[9,32,4,256]{3,2,1,0:T(4,128)(2,1)S(1)}, s32[9,32,2,189]{3,1,0,2:T(8,128)S(1)}, f32[316,256]{1,0:T(8,128)S(1)}, bf16[800,1024]{1,0:T(8,128)(2,1)S(1)}, /*index=5*/s32[]{:T(128)}) while((s32[]{:T(128)}, bf16[9,32,4,256]{3,2,1,0:T(4,128)(2,1)S(1)}, s32[9,32,2,189]{3,1,0,2:T(8,128)S(1)}, ...), condition=%wide.region_11.12_spmd, body=%wide.region_8.11_spmd.sunk | while | flops 38926656 | bytes 267107840 | solution.py:76
  132.0 26.8 %gather_fusion = bf16[6048,1024]{1,0:T(8,128)(2,1)} fusion(bf16[800,1024]{1,0:T(8,128)(2,1)S(1)} %get-tuple-element.172, s32[6144]{0:T(1024)S(1)} %pad_clamp_fusion.6), kind=kCustom, calls=%fused_computation.1.clone.1 | custom fusion | bytes 24796800 | tf_op jit(solution)/shard_map/while/body/eval_jaxpr/jit(_take)/gather | solution.py:61
  158.8 23.2 %gather.34 = bf16[32,189,4,256]{3,2,1,0:T(4,128)(2,1)} reshape(bf16[6048,1024]{1,0:T(8,128)(2,1)} %gather_fusion) | data formatting | bytes 24772608 | tf_op jit(solution)/shard_map/while/body/eval_jaxpr/jit(_take)/gather | solution.py:61
  199.5 23.7 %gather_fusion.1 = f32[6048,256]{1,0:T(8,128)} fusion(f32[316,256]{1,0:T(8,128)S(1)} %get-tuple-element.171, s32[6144]{0:T(1024)S(1)} %pad_clamp_fusion.7), kind=kCustom, calls=%fused_computation.clone.1 | custom fusion | bytes 12410496 | tf_op jit(solution)/shard_map/while/body/eval_jaxpr/jit(_take)/gather | solution.py:65
  255.8 26.8 %gather_fusion = bf16[6048,1024]{1,0:T(8,128)(2,1)} fusion(bf16[800,1024]{1,0:T(8,128)(2,1)S(1)} %get-tuple-element.172, s32[6144]{0:T(1024)S(1)} %pad_clamp_fusion.6), kind=kCustom, calls=%fused_computation.1.clone.1 | custom fusion | bytes 24796800 | tf_op jit(solution)/shard_map/while/body/eval_jaxpr/jit(_take)/gather | solution.py:61
  282.5 23.2 %gather.34 = bf16[32,189,4,256]{3,2,1,0:T(4,128)(2,1)} reshape(bf16[6048,1024]{1,0:T(8,128)(2,1)} %gather_fusion) | data formatting | bytes 24772608 | tf_op jit(solution)/shard_map/while/body/eval_jaxpr/jit(_take)/gather | solution.py:61
  323.3 23.7 %gather_fusion.1 = f32[6048,256]{1,0:T(8,128)} fusion(f32[316,256]{1,0:T(8,128)S(1)} %get-tuple-element.171, s32[6144]{0:T(1024)S(1)} %pad_clamp_fusion.7), kind=kCustom, calls=%fused_computation.clone.1 | custom fusion | bytes 12410496 | tf_op jit(solution)/shard_map/while/body/eval_jaxpr/jit(_take)/gather | solution.py:65
  379.6 26.8 %gather_fusion = bf16[6048,1024]{1,0:T(8,128)(2,1)} fusion(bf16[800,1024]{1,0:T(8,128)(2,1)S(1)} %get-tuple-element.172, s32[6144]{0:T(1024)S(1)} %pad_clamp_fusion.6), kind=kCustom, calls=%fused_computation.1.clone.1 | custom fusion | bytes 24796800 | tf_op jit(solution)/shard_map/while/body/eval_jaxpr/jit(_take)/gather | solution.py:61
  406.3 23.2 %gather.34 = bf16[32,189,4,256]{3,2,1,0:T(4,128)(2,1)} reshape(bf16[6048,1024]{1,0:T(8,128)(2,1)} %gather_fusion) | data formatting | bytes 24772608 | tf_op jit(solution)/shard_map/while/body/eval_jaxpr/jit(_take)/gather | solution.py:61
  447.1 23.7 %gather_fusion.1 = f32[6048,256]{1,0:T(8,128)} fusion(f32[316,256]{1,0:T(8,128)S(1)} %get-tuple-element.171, s32[6144]{0:T(1024)S(1)} %pad_clamp_fusion.7), kind=kCustom, calls=%fused_computation.clone.1 | custom fusion | bytes 12410496 | tf_op jit(solution)/shard_map/while/body/eval_jaxpr/jit(_take)/gather | solution.py:65
  503.3 26.8 %gather_fusion = bf16[6048,1024]{1,0:T(8,128)(2,1)} fusion(bf16[800,1024]{1,0:T(8,128)(2,1)S(1)} %get-tuple-element.172, s32[6144]{0:T(1024)S(1)} %pad_clamp_fusion.6), kind=kCustom, calls=%fused_computation.1.clone.1 | custom fusion | bytes 24796800 | tf_op jit(solution)/shard_map/while/body/eval_jaxpr/jit(_take)/gather | solution.py:61
  530.1 23.2 %gather.34 = bf16[32,189,4,256]{3,2,1,0:T(4,128)(2,1)} reshape(bf16[6048,1024]{1,0:T(8,128)(2,1)} %gather_fusion) | data formatting | bytes 24772608 | tf_op jit(solution)/shard_map/while/body/eval_jaxpr/jit(_take)/gather | solution.py:61
  570.9 23.7 %gather_fusion.1 = f32[6048,256]{1,0:T(8,128)} fusion(f32[316,256]{1,0:T(8,128)S(1)} %get-tuple-element.171, s32[6144]{0:T(1024)S(1)} %pad_clamp_fusion.7), kind=kCustom, calls=%fused_computation.clone.1 | custom fusion | bytes 12410496 | tf_op jit(solution)/shard_map/while/body/eval_jaxpr/jit(_take)/gather | solution.py:65
  627.1 26.8 %gather_fusion = bf16[6048,1024]{1,0:T(8,128)(2,1)} fusion(bf16[800,1024]{1,0:T(8,128)(2,1)S(1)} %get-tuple-element.172, s32[6144]{0:T(1024)S(1)} %pad_clamp_fusion.6), kind=kCustom, calls=%fused_computation.1.clone.1 | custom fusion | bytes 24796800 | tf_op jit(solution)/shard_map/while/body/eval_jaxpr/jit(_take)/gather | solution.py:61
  694.6 23.7 %gather_fusion.1 = f32[6048,256]{1,0:T(8,128)} fusion(f32[316,256]{1,0:T(8,128)S(1)} %get-tuple-element.171, s32[6144]{0:T(1024)S(1)} %pad_clamp_fusion.7), kind=kCustom, calls=%fused_computation.clone.1 | custom fusion | bytes 12410496 | tf_op jit(solution)/shard_map/while/body/eval_jaxpr/jit(_take)/gather | solution.py:65
  750.9 26.8 %gather_fusion = bf16[6048,1024]{1,0:T(8,128)(2,1)} fusion(bf16[800,1024]{1,0:T(8,128)(2,1)S(1)} %get-tuple-element.172, s32[6144]{0:T(1024)S(1)} %pad_clamp_fusion.6), kind=kCustom, calls=%fused_computation.1.clone.1 | custom fusion | bytes 24796800 | tf_op jit(solution)/shard_map/while/body/eval_jaxpr/jit(_take)/gather | solution.py:61
  818.4 23.7 %gather_fusion.1 = f32[6048,256]{1,0:T(8,128)} fusion(f32[316,256]{1,0:T(8,128)S(1)} %get-tuple-element.171, s32[6144]{0:T(1024)S(1)} %pad_clamp_fusion.7), kind=kCustom, calls=%fused_computation.clone.1 | custom fusion | bytes 12410496 | tf_op jit(solution)/shard_map/while/body/eval_jaxpr/jit(_take)/gather | solution.py:65
  874.7 26.8 %gather_fusion = bf16[6048,1024]{1,0:T(8,128)(2,1)} fusion(bf16[800,1024]{1,0:T(8,128)(2,1)S(1)} %get-tuple-element.172, s32[6144]{0:T(1024)S(1)} %pad_clamp_fusion.6), kind=kCustom, calls=%fused_computation.1.clone.1 | custom fusion | bytes 24796800 | tf_op jit(solution)/shard_map/while/body/eval_jaxpr/jit(_take)/gather | solution.py:61
  942.2 23.7 %gather_fusion.1 = f32[6048,256]{1,0:T(8,128)} fusion(f32[316,256]{1,0:T(8,128)S(1)} %get-tuple-element.171, s32[6144]{0:T(1024)S(1)} %pad_clamp_fusion.7), kind=kCustom, calls=%fused_computation.clone.1 | custom fusion | bytes 12410496 | tf_op jit(solution)/shard_map/while/body/eval_jaxpr/jit(_take)/gather | solution.py:65
  998.5 26.8 %gather_fusion = bf16[6048,1024]{1,0:T(8,128)(2,1)} fusion(bf16[800,1024]{1,0:T(8,128)(2,1)S(1)} %get-tuple-element.172, s32[6144]{0:T(1024)S(1)} %pad_clamp_fusion.6), kind=kCustom, calls=%fused_computation.1.clone.1 | custom fusion | bytes 24796800 | tf_op jit(solution)/shard_map/while/body/eval_jaxpr/jit(_take)/gather | solution.py:61
  1066.0 23.7 %gather_fusion.1 = f32[6048,256]{1,0:T(8,128)} fusion(f32[316,256]{1,0:T(8,128)S(1)} %get-tuple-element.171, s32[6144]{0:T(1024)S(1)} %pad_clamp_fusion.7), kind=kCustom, calls=%fused_computation.clone.1 | custom fusion | bytes 12410496 | tf_op jit(solution)/shard_map/while/body/eval_jaxpr/jit(_take)/gather | solution.py:65
  1122.2 26.8 %gather_fusion = bf16[6048,1024]{1,0:T(8,128)(2,1)} fusion(bf16[800,1024]{1,0:T(8,128)(2,1)S(1)} %get-tuple-element.172, s32[6144]{0:T(1024)S(1)} %pad_clamp_fusion.6), kind=kCustom, calls=%fused_computation.1.clone.1 | custom fusion | bytes 24796800 | tf_op jit(solution)/shard_map/while/body/eval_jaxpr/jit(_take)/gather | solution.py:61
  1189.8 23.7 %gather_fusion.1 = f32[6048,256]{1,0:T(8,128)} fusion(f32[316,256]{1,0:T(8,128)S(1)} %get-tuple-element.171, s32[6144]{0:T(1024)S(1)} %pad_clamp_fusion.7), kind=kCustom, calls=%fused_computation.clone.1 | custom fusion | bytes 12410496 | tf_op jit(solution)/shard_map/while/body/eval_jaxpr/jit(_take)/gather | solution.py:65
  (310 shorter events, 666.9 us)
Async XLA Ops:
  0.6 45.0 %copy-start = (bf16[256,256]{1,0:T(8,128)(2,1)S(1)}, bf16[256,256]{1,0:T(8,128)(2,1)}, u32[]{:S(2)}) copy-start(bf16[256,256]{1,0:T(8,128)(2,1)} %param.21) | copy-start | bytes 393220
  0.6 5.1 all-to-all-start
  46.7 18.6 %copy-start.9 = (s32[256]{0:T(256)S(1)}, s32[256]{0:T(256)}, u32[]{:S(2)}) copy-start(s32[256]{0:T(256)} %param.19) | copy-start | bytes 3076
  49.7 19.5 %copy-start.4 = (bf16[8,256,256]{2,1,0:T(8,128)(2,1)S(1)}, bf16[8,256,256]{2,1,0:T(8,128)(2,1)}, u32[]{:S(2)}) copy-start(bf16[8,256,256]{2,1,0:T(8,128)(2,1)} %param.20) | copy-start | bytes 3145732
  50.7 22.0 %collective-permute-start = (bf16[48,4,256]{2,0,1:T(8,128)(2,1)}, bf16[48,4,256]{2,0,1:T(8,128)(2,1)}, u32[]{:S(2)}, u32[]{:S(2)}) collective-permute-start(bf16[48,4,256]{2,0,1:T(8,128)(2,1)} %copy.105), channel_id=1, source_target_pairs={{8,0},{10,2},{12,4},{14,6},{16,8},{18,10},{20,12},{22,14},{24,16},... | collective-permute-start | bytes 294920 | tf_op jit(solution)/shard_map/ppermute | solution.py:10
  52.6 26.4 %collective-permute-start.1 = (bf16[48,4,256]{2,0,1:T(8,128)(2,1)}, bf16[48,4,256]{2,0,1:T(8,128)(2,1)}, u32[]{:S(2)}, u32[]{:S(2)}) collective-permute-start(bf16[48,4,256]{2,0,1:T(8,128)(2,1)} %copy.106), channel_id=1, source_target_pairs={{6,0},{8,2},{10,4},{12,6},{14,8},{16,10},{18,12},{20,14},{22,16},{... | collective-permute-start | bytes 294920 | tf_op jit(solution)/shard_map/ppermute | solution.py:10
  54.5 33.2 %collective-permute-start.2 = (bf16[48,4,256]{2,0,1:T(8,128)(2,1)}, bf16[48,4,256]{2,0,1:T(8,128)(2,1)}, u32[]{:S(2)}, u32[]{:S(2)}) collective-permute-start(bf16[48,4,256]{2,0,1:T(8,128)(2,1)} %copy.107), channel_id=1, source_target_pairs={{4,0},{6,2},{8,4},{10,6},{12,8},{14,10},{16,12},{18,14},{20,16},{2... | collective-permute-start | bytes 294920 | tf_op jit(solution)/shard_map/ppermute | solution.py:10
  56.5 37.4 %collective-permute-start.3 = (bf16[48,4,256]{2,0,1:T(8,128)(2,1)}, bf16[48,4,256]{2,0,1:T(8,128)(2,1)}, u32[]{:S(2)}, u32[]{:S(2)}) collective-permute-start(bf16[48,4,256]{2,0,1:T(8,128)(2,1)} %copy.108), channel_id=1, source_target_pairs={{2,0},{4,2},{6,4},{8,6},{10,8},{12,10},{14,12},{16,14},{18,16},{20... | collective-permute-start | bytes 294920 | tf_op jit(solution)/shard_map/ppermute | solution.py:10
  57.8 38.9 %collective-permute-start.4 = (bf16[48,4,256]{2,0,1:T(8,128)(2,1)S(1)}, bf16[48,4,256]{2,0,1:T(8,128)(2,1)S(1)}, u32[]{:S(2)}, u32[]{:S(2)}) collective-permute-start(bf16[48,4,256]{2,0,1:T(8,128)(2,1)S(1)} %copy.109), channel_id=1, source_target_pairs={{0,2},{2,4},{4,6},{6,8},{8,10},{10,12},{12,14},{14,16},{16,18},{18... | collective-permute-start | bytes 294920 | tf_op jit(solution)/shard_map/ppermute | solution.py:10
  72.6 59.2 %copy-start.2 = (f32[316,256]{1,0:T(8,128)S(1)}, f32[316,256]{1,0:T(8,128)}, u32[]{:S(2)}) copy-start(f32[316,256]{1,0:T(8,128)} %param.23) | copy-start | bytes 970756
  72.6 59.1 %copy-start.5 = (bf16[9,32,4,256]{3,2,1,0:T(4,128)(2,1)S(1)}, bf16[9,32,4,256]{3,2,1,0:T(4,128)(2,1)}, u32[]{:S(2)}) copy-start(bf16[9,32,4,256]{3,2,1,0:T(4,128)(2,1)} %custom-call.9) | copy-start | bytes 1769476
  72.6 26.0 %collective-permute-start.5 = (bf16[48,4,256]{2,0,1:T(8,128)(2,1)S(1)}, bf16[48,4,256]{2,0,1:T(8,128)(2,1)S(1)}, u32[]{:S(2)}, u32[]{:S(2)}) collective-permute-start(bf16[48,4,256]{2,0,1:T(8,128)(2,1)S(1)} %copy.110), channel_id=1, source_target_pairs={{0,4},{2,6},{4,8},{6,10},{8,12},{10,14},{12,16},{14,18},{16,20},{1... | collective-permute-start | bytes 294920 | tf_op jit(solution)/shard_map/ppermute | solution.py:10
  79.0 21.5 %collective-permute-start.6 = (bf16[48,4,256]{2,0,1:T(8,128)(2,1)S(1)}, bf16[48,4,256]{2,0,1:T(8,128)(2,1)S(1)}, u32[]{:S(2)}, u32[]{:S(2)}) collective-permute-start(bf16[48,4,256]{2,0,1:T(8,128)(2,1)S(1)} %copy.111), channel_id=1, source_target_pairs={{0,6},{2,8},{4,10},{6,12},{8,14},{10,16},{12,18},{14,20},{16,22},{... | collective-permute-start | bytes 294920 | tf_op jit(solution)/shard_map/ppermute | solution.py:10
  87.7 14.8 %collective-permute-start.7 = (bf16[48,4,256]{2,0,1:T(8,128)(2,1)S(1)}, bf16[48,4,256]{2,0,1:T(8,128)(2,1)S(1)}, u32[]{:S(2)}, u32[]{:S(2)}) collective-permute-start(bf16[48,4,256]{2,0,1:T(8,128)(2,1)S(1)} %copy.112), channel_id=1, source_target_pairs={{0,8},{2,10},{4,12},{6,14},{8,16},{10,18},{12,20},{14,22},{16,24},... | collective-permute-start | bytes 294920 | tf_op jit(solution)/shard_map/ppermute | solution.py:10
  93.8 13.9 %collective-permute-start.8 = (bf16[16,4,256]{2,0,1:T(8,128)(2,1)S(1)}, bf16[16,4,256]{2,0,1:T(8,128)(2,1)S(1)}, u32[]{:S(2)}, u32[]{:S(2)}) collective-permute-start(bf16[16,4,256]{2,0,1:T(8,128)(2,1)S(1)} %copy.113), channel_id=1, source_target_pairs={{8,0},{10,2},{12,4},{14,6},{16,8},{18,10},{20,12},{22,14},{24,16},... | collective-permute-start | bytes 98312 | tf_op jit(solution)/shard_map/ppermute | solution.py:10
  96.7 17.1 %collective-permute-start.9 = (bf16[16,4,256]{2,0,1:T(8,128)(2,1)S(1)}, bf16[16,4,256]{2,0,1:T(8,128)(2,1)S(1)}, u32[]{:S(2)}, u32[]{:S(2)}) collective-permute-start(bf16[16,4,256]{2,0,1:T(8,128)(2,1)S(1)} %copy.114), channel_id=1, source_target_pairs={{6,0},{8,2},{10,4},{12,6},{14,8},{16,10},{18,12},{20,14},{22,16},{... | collective-permute-start | bytes 98312 | tf_op jit(solution)/shard_map/ppermute | solution.py:10
  98.6 23.0 %collective-permute-start.10 = (bf16[16,4,256]{2,0,1:T(8,128)(2,1)S(1)}, bf16[16,4,256]{2,0,1:T(8,128)(2,1)S(1)}, u32[]{:S(2)}, u32[]{:S(2)}) collective-permute-start(bf16[16,4,256]{2,0,1:T(8,128)(2,1)S(1)} %copy.115), channel_id=1, source_target_pairs={{4,0},{6,2},{8,4},{10,6},{12,8},{14,10},{16,12},{18,14},{20,16},{2... | collective-permute-start | bytes 98312 | tf_op jit(solution)/shard_map/ppermute | solution.py:10
  100.5 26.4 %collective-permute-start.11 = (bf16[16,4,256]{2,0,1:T(8,128)(2,1)S(1)}, bf16[16,4,256]{2,0,1:T(8,128)(2,1)S(1)}, u32[]{:S(2)}, u32[]{:S(2)}) collective-permute-start(bf16[16,4,256]{2,0,1:T(8,128)(2,1)S(1)} %copy.116), channel_id=1, source_target_pairs={{2,0},{4,2},{6,4},{8,6},{10,8},{12,10},{14,12},{16,14},{18,16},{20... | collective-permute-start | bytes 98312 | tf_op jit(solution)/shard_map/ppermute | solution.py:10
  102.5 25.1 %collective-permute-start.12 = (bf16[16,4,256]{2,0,1:T(8,128)(2,1)S(1)}, bf16[16,4,256]{2,0,1:T(8,128)(2,1)S(1)}, u32[]{:S(2)}, u32[]{:S(2)}) collective-permute-start(bf16[16,4,256]{2,0,1:T(8,128)(2,1)S(1)} %copy.117), channel_id=1, source_target_pairs={{0,2},{2,4},{4,6},{6,8},{8,10},{10,12},{12,14},{14,16},{16,18},{18... | collective-permute-start | bytes 98312 | tf_op jit(solution)/shard_map/ppermute | solution.py:10
  107.7 20.5 %collective-permute-start.13 = (bf16[16,4,256]{2,0,1:T(8,128)(2,1)S(1)}, bf16[16,4,256]{2,0,1:T(8,128)(2,1)S(1)}, u32[]{:S(2)}, u32[]{:S(2)}) collective-permute-start(bf16[16,4,256]{2,0,1:T(8,128)(2,1)S(1)} %copy.118), channel_id=1, source_target_pairs={{0,4},{2,6},{4,8},{6,10},{8,12},{10,14},{12,16},{14,18},{16,20},{1... | collective-permute-start | bytes 98312 | tf_op jit(solution)/shard_map/ppermute | solution.py:10
  113.7 15.1 %collective-permute-start.14 = (bf16[16,4,256]{2,0,1:T(8,128)(2,1)S(1)}, bf16[16,4,256]{2,0,1:T(8,128)(2,1)S(1)}, u32[]{:S(2)}, u32[]{:S(2)}) collective-permute-start(bf16[16,4,256]{2,0,1:T(8,128)(2,1)S(1)} %copy.119), channel_id=1, source_target_pairs={{0,6},{2,8},{4,10},{6,12},{8,14},{10,16},{12,18},{14,20},{16,22},{... | collective-permute-start | bytes 98312 | tf_op jit(solution)/shard_map/ppermute | solution.py:10
  121.6 7.8 collective-permute-start.15
  131.7 1114.2 %copy-start.6 = (bf16[256,256]{1,0:T(8,128)(2,1)S(1)}, bf16[256,256]{1,0:T(8,128)(2,1)}, u32[]{:S(2)}) copy-start(bf16[256,256]{1,0:T(8,128)(2,1)} %param.22) | copy-start | bytes 393220
  229.4 15.2 %copy-start.3 = (f32[32,189,4,256]{3,2,1,0:T(4,128)S(1)}, f32[32,189,4,256]{3,2,1,0:T(4,128)}, u32[]{:S(2)}) copy-start(f32[32,189,4,256]{3,2,1,0:T(4,128)} %select_convert_fusion.2) | copy-start | bytes 74317824 | tf_op jit(solution)/shard_map/while
  (11 other events, 136.0 us)
where the time goes:
time: 1260 us; the launch traced here: 1250 us
  local copies, waits for them, and re-layouts  825 us (65%)
  other arithmetic  354 us (28%)
  starting transfers between devices  57.7 us (5%)
    gather x18, local copies, waits for them, and re-layouts, one_block(): picked = jnp.take(flat_table, block_pairs[:, 0].reshape(-1), axis=0)  449 us
    gather x18, local copies, waits for them, and re-layouts, one_block(): factor = jnp.take(translation, block_pairs[:, 1].reshape(-1), axis=0)  269 us
    convert_element_type x9, other arithmetic, one_block(): picked.reshape(block_pairs.shape[0], list_len, width_r, width_k)  156 us
    reduce_sum x9, other arithmetic, one_block(): real_part = jnp.sum(factor_re * wave_re - factor_im * wave_im, axis=1)  97.9 us
    select_n x18, other arithmetic, one_block(): factor = jnp.take(translation, block_pairs[:, 1].reshape(-1), axis=0)  63.6 us
    ppermute x16, starting transfers between devices, from_behind(): lax.ppermute(value, axis, [(source, source + steps) for source in range(i...  54.1 us
    mul x9, local copies, waits for them, and re-layouts, one_block(): real_part = jnp.sum(factor_re * wave_re - factor_im * wave_im, axis=1)  51.8 us
    another operation x1, other arithmetic  32.3 us
  transfers between devices with their start and end apart: 17, of which 1 were waited for; matrix products, arithmetic and copies ran while one was open for 2% of the time, Pallas kernels for 0%

commit v1 on v0

v1 whole, which is shorter than its diff:
```python
import functools
import math

import jax
import jax.numpy as jnp
from jax import lax
from jax.experimental import pallas as pl
from jax.experimental.pallas import tpu as pltpu
from jax.sharding import PartitionSpec as P

F32 = jnp.float32
BF16 = jnp.bfloat16
CHUNK = 63
GROUP = 9
SIN_POLY = (4.44286790342698, -7.307443431653506, 3.594788153158899, -0.7843741906863176)
COS_POLY = (
    1.4142134967586113,
    -6.978850998632011,
    5.7394613208713325,
    -1.883563790130787,
    0.31069962133630835,
)

VMEM = pl.BlockSpec(memory_space=pltpu.VMEM)
SMEM = pl.BlockSpec(memory_space=pltpu.SMEM)


def swap_cores(value):
    return lax.ppermute(value, "rhs", [(0, 1), (1, 0)])


def horner(coefficients, x):
    total = coefficients[-1] * x + coefficients[-2]
    for coefficient in coefficients[-3::-1]:
        total = total * x + coefficient
    return total


def tree(values):
    values = list(values)
    while len(values) > 1:
        paired = [values[i] + values[i + 1] for i in range(0, len(values) - 1, 2)]
        values = paired + values[2 * len(paired) :]
    return values[0]


def sin_cos_turns(turns):
    r = turns - jnp.round(turns)
    r2 = r * r
    s = r * horner(SIN_POLY, r2)
    c = horner(COS_POLY, r2)
    return s * c, 1.0 - s * s


def upward_kernel(
    core_ref, counts_ref, octants_ref, freq_ref, pos_ref, own_ref, recv_ref, shift_ref, wave_mat_ref,
    out_ref, freq_scr, mult_scr, child_scr,
):
    core = core_ref[0]
    leaves, slots = pos_ref.shape[0], pos_ref.shape[2]
    nodes = freq_ref.shape[1]
    for d in range(3):
        row = freq_ref[d : d + 1, :] * (1.0 / (2.0 * math.pi))
        freq_scr[d] = jnp.broadcast_to(row, (slots, nodes)).T
    lane = lax.broadcasted_iota(jnp.int32, (2 * own_ref.shape[1], slots), 1)

    def one_leaf(b, carry):
        lo = jnp.where(core == 0, own_ref[b].astype(F32), recv_ref[b].astype(F32))
        hi = jnp.where(core == 0, recv_ref[b].astype(F32), own_ref[b].astype(F32))
        charge = jnp.concatenate([lo, hi], axis=0)
        charge = jnp.where(lane < counts_ref[b], charge, 0.0).astype(BF16)
        xs = [jnp.broadcast_to(pos_ref[b, d : d + 1, :], (nodes, slots)) for d in range(3)]
        turns = freq_scr[0] * xs[0] + freq_scr[1] * xs[1] + freq_scr[2] * xs[2]
        sin, cos = sin_cos_turns(turns)
        basis = jnp.concatenate([cos.astype(BF16), sin.astype(BF16)], axis=0)
        multipole = lax.dot_general(
            charge, basis, (((1,), (1,)), ((), ())), preferred_element_type=F32
        ).astype(BF16)
        mult_scr[b] = multipole
        child_scr[octants_ref[b], b // 8] = multipole
        return carry

    lax.fori_loop(0, leaves, one_leaf, 0)
    parents = leaves // 8
    rhs, width = mult_scr.shape[1:]
    wave_mat = wave_mat_ref[...]
    multipoles = mult_scr[...].reshape(leaves * rhs, width)
    waves = jnp.dot(multipoles, wave_mat, preferred_element_type=F32).astype(BF16)
    out_ref[:leaves] = waves.reshape(leaves, rhs, width)
    summed = None
    for octant in range(8):
        part = jnp.dot(
            child_scr[octant].reshape(parents * rhs, width),
            shift_ref[octant],
            preferred_element_type=F32,
        )
        summed = part if summed is None else summed + part
    parent_waves = jnp.dot(summed.astype(BF16), wave_mat, preferred_element_type=F32)
    out_ref[leaves:] = parent_waves.astype(BF16).reshape(parents, rhs, width)


def pack_kernel(leaf_ids_ref, parent_ids_ref, own_ref, recv_ref, *refs):
    outs, scr = refs[:-1], refs[-1]
    held = own_ref.shape[0]
    scr[:held] = own_ref[...]
    scr[held:] = recv_ref[...]
    cap_l, cap_p = leaf_ids_ref.shape[1], parent_ids_ref.shape[1]
    for j, out in enumerate(outs):
        for k in range(cap_l):
            out[k] = scr[leaf_ids_ref[j, k]]
        for k in range(cap_p):
            out[cap_l + k] = scr[parent_ids_ref[j, k]]


def interact_kernel(dims, info_ref, source_ref, class_ref, *refs):
    leaves, parents, slots, cap_l, cap_p, list_len, stride = dims
    own_ref, recv_ref = refs[:2]
    near_own = refs[2 : 2 + slots]
    near_recv = refs[2 + slots : 2 + 2 * slots]
    trans_ref, keep_ref, send_ref, table, factor = refs[2 + 2 * slots :]
    core = info_ref[0]
    other = 1 - core
    half = keep_ref.shape[2] // 2
    rows = 16

    def put(source, at, count, base, valid=None):
        def body(k, carry):
            value = source[at + k].astype(F32)
            if valid is not None:
                value = jnp.where(valid > 0, value, 0.0)
            row = pl.multiple_of((base + k) * rows, rows)
            table[pl.ds(row, 8), :] = value[:, :half]
            table[pl.ds(pl.multiple_of(row + 8, 8), 8), :] = value[:, half:]
            return carry

        lax.fori_loop(0, count, body, 0, unroll=8)

    for values, which in ((own_ref, core), (recv_ref, other)):
        put(values, 0, leaves, which * leaves)
        put(values, leaves, parents, 2 * leaves + which * parents)
    base = 2 * (leaves + parents)
    for j in range(slots):
        for values, which in ((near_own[j], core), (near_recv[j], other)):
            valid = info_ref[1 + j]
            put(values, 0, cap_l, base + (2 * j + which) * cap_l, valid)
            put(values, cap_l, cap_p, base + 2 * slots * cap_l + (2 * j + which) * cap_p, valid)

    def put_factors(first, values):
        for k in range(values.shape[0]):
            row = pl.multiple_of((first + k) * rows, rows)
            factor[pl.ds(row, 8), :] = jnp.broadcast_to(values[k : k + 1, :half], (8, half))
            factor[pl.ds(pl.multiple_of(row + 8, 8), 8), :] = jnp.broadcast_to(
                values[k : k + 1, half:], (8, half)
            )

    def factor_block(g, carry):
        first = pl.multiple_of(g * 8, 8)
        put_factors(first, trans_ref[pl.ds(first, 8), :])
        return carry

    classes_full = trans_ref.shape[0] // 8 * 8
    lax.fori_loop(0, classes_full // 8, factor_block, 0)
    if classes_full < trans_ref.shape[0]:
        put_factors(classes_full, trans_ref[classes_full:, :])

    def accumulate(first, count, total):
        total_re, total_im = total
        reals, imags = [], []
        for k in range(count):
            if k % GROUP == 0:
                span = min(GROUP, count - k)
                sources = source_ref.at[pl.ds(first + k, span)]
                classes = class_ref.at[pl.ds(first + k, span)]
            s = pl.multiple_of(sources[k % GROUP], 8)
            o = pl.multiple_of(classes[k % GROUP], 8)
            wave = table.at[pl.ds(s, rows)]
            shift = factor.at[pl.ds(o, rows)]
            wave_re, wave_im, shift_re, shift_im = wave[:8], wave[8:], shift[:8], shift[8:]
            reals.append(shift_re * wave_re - shift_im * wave_im)
            imags.append(shift_re * wave_im + shift_im * wave_re)
            if len(reals) == 3 or k == count - 1:
                total_re, total_im = total_re + tree(reals), total_im + tree(imags)
                reals, imags = [], []
        return total_re, total_im

    def one_target(b, carry):
        zero = jnp.zeros((8, half), F32)
        start = b * stride
        total = lax.fori_loop(
            0,
            list_len // CHUNK,
            lambda c, t: accumulate(start + c * CHUNK, CHUNK, t),
            (zero, zero),
        )
        if list_len % CHUNK:
            total = accumulate(start + list_len - list_len % CHUNK, list_len % CHUNK, total)
        incoming = jnp.concatenate(total, axis=1)
        lower, upper = incoming[:4], incoming[4:]
        keep_ref[b] = jnp.where(core == 0, lower, upper).astype(BF16)
        send_ref[b] = jnp.where(core == 0, upper, lower).astype(BF16)
        return carry

    lax.fori_loop(0, keep_ref.shape[0], one_target, 0)


def local_kernel(leaves, core_ref, keep_ref, recv_ref, mat_ref, leaf_ref, parent_ref):
    core = core_ref[0]
    parents = keep_ref.shape[0] - leaves
    rhs, width = keep_ref.shape[1:]
    for values, which in ((keep_ref, core), (recv_ref, 1 - core)):
        flat = values[...].reshape((leaves + parents) * rhs, width)
        local = jnp.dot(flat, mat_ref[...], preferred_element_type=F32)
        local = local.reshape(leaves + parents, rhs, width)
        leaf_ref[pl.ds(which * leaves, leaves)] = local[:leaves]
        parent_ref[pl.ds(which * parents, parents)] = local[leaves:]


def shards(
    positions, point_counts, charges, frequencies, octants, child_shift, to_wave, to_local,
    translation, send_leaf, send_parent, leaf_pairs, parent_pairs,
):
    core = lax.axis_index("rhs")
    other = 1 - core
    device = lax.axis_index("space")
    count = lax.axis_size("space")
    leaves = positions.shape[0] // 2
    parents = leaves // 8
    rhs = charges.shape[1]
    width = to_wave.shape[0]
    slots = send_leaf.shape[1]
    near = slots // 2
    held = leaves + parents
    core_arr = core.reshape(1)

    def half_of(value, which):
        size = value.shape[0] // 2
        return lax.dynamic_slice_in_dim(value, which * size, size, 0)

    arrived_charges = swap_cores(half_of(charges, other))
    waves = pl.pallas_call(
        upward_kernel,
        out_shape=jax.ShapeDtypeStruct((held, 2 * rhs, width), BF16),
        in_specs=[SMEM] * 3 + [VMEM] * 6,
        out_specs=VMEM,
        scratch_shapes=[
            pltpu.VMEM((3, width // 2, positions.shape[2]), F32),
            pltpu.VMEM((leaves, 2 * rhs, width), BF16),
            pltpu.VMEM((8, parents, 2 * rhs, width), BF16),
        ],
        name="upward",
    )(
        core_arr,
        half_of(point_counts, core),
        half_of(octants, core),
        frequencies,
        half_of(positions, core),
        half_of(charges, core),
        arrived_charges,
        child_shift,
        to_wave,
    )
    arrived_waves = swap_cores(waves)

    cap_l, cap_p = send_leaf.shape[2] // 2, send_parent.shape[2] // 2
    leaf_ids = lax.dynamic_slice_in_dim(send_leaf[0], core * cap_l, cap_l, 1)
    parent_ids = lax.dynamic_slice_in_dim(send_parent[0], core * cap_p, cap_p, 1)
    leaf_rows = jnp.where(leaf_ids // leaves == core, 0, held) + leaf_ids % leaves
    parent_rows = jnp.where(parent_ids // parents == core, 0, held) + leaves + parent_ids % parents
    sent = pl.pallas_call(
        pack_kernel,
        out_shape=[jax.ShapeDtypeStruct((cap_l + cap_p, 2 * rhs, width), BF16)] * slots,
        in_specs=[SMEM] * 2 + [VMEM] * 2,
        out_specs=[VMEM] * slots,
        scratch_shapes=[pltpu.VMEM((2 * held, 2 * rhs, width), BF16)],
        name="pack",
    )(leaf_rows, parent_rows, waves, arrived_waves)
    offsets = [j - near if j < near else j - near + 1 for j in range(slots)]
    near_own = [
        lax.ppermute(part, "space", [(e, (e + o) % count) for e in range(count)])
        for part, o in zip(sent, offsets)
    ]
    near_recv = [swap_cores(part) for part in near_own]

    list_len = leaf_pairs.shape[2]
    stride = -(-list_len // 64) * 64
    targets = jnp.concatenate([half_of(leaf_pairs, core), half_of(parent_pairs, core)], axis=0)
    targets = jnp.pad(targets * 16, ((0, 0), (0, 0), (0, stride - list_len)))
    source_rows = targets[:, 0].reshape(-1)
    class_rows = targets[:, 1].reshape(-1)
    senders = device - jnp.array(offsets, jnp.int32)
    valid = ((senders >= 0) & (senders < count)).astype(jnp.int32)
    info = jnp.concatenate([core_arr, valid])
    dims = (leaves, parents, slots, cap_l, cap_p, list_len, stride)
    table_rows = 2 * held + 2 * slots * (cap_l + cap_p)
    keep, send = pl.pallas_call(
        functools.partial(interact_kernel, dims),
        out_shape=[jax.ShapeDtypeStruct((held, rhs, width), BF16)] * 2,
        in_specs=[SMEM] * 3 + [VMEM] * (3 + 2 * slots),
        out_specs=[VMEM] * 2,
        scratch_shapes=[
            pltpu.VMEM((table_rows * 16, width // 2), F32),
            pltpu.VMEM((translation.shape[0] * 16, width // 2), F32),
        ],
        name="interact",
    )(info, source_rows, class_rows, waves, arrived_waves, *near_own, *near_recv, translation)
    arrived = swap_cores(send)
    return tuple(
        pl.pallas_call(
            functools.partial(local_kernel, leaves),
            out_shape=[
                jax.ShapeDtypeStruct((2 * leaves, rhs, width), F32),
                jax.ShapeDtypeStruct((2 * parents, rhs, width), F32),
            ],
            in_specs=[SMEM] + [VMEM] * 3,
            out_specs=[VMEM] * 2,
            name="local",
        )(core_arr, keep, arrived, to_local)
    )


def solution(mesh):
    in_specs = (
        P("space", None, None), P("space"), P("space", "rhs", None), P(), P("space"), P(), P(), P(),
        P(), P("space", None, None), P("space", None, None), P("space", None, None),
        P("space", None, None),
    )
    out_specs = (P("space", "rhs", None), P("space", "rhs", None))
    return jax.shard_map(shards, mesh=mesh, in_specs=in_specs, out_specs=out_specs, check_vma=False)
```

time: 1260 us -> 115 us (0.09)
  local copies, waits for them, and re-layouts: 825 us -> 10.7 us
  other arithmetic: 354 us -> 2.11 us
  Pallas kernels: 0 us -> 75 us
  starting transfers between devices: 57.7 us -> 15.9 us
    gather x38 -> x0, local copies, waits for them, and re-layouts: 721 us -> none  [the longest x18 449 us: one_block(): picked = jnp.take(flat_table, block_pairs[:, 0].reshape(-1), axis=0)]
    convert_element_type x9 -> x1, other arithmetic: 156 us -> 0.01 us  [shards(): valid = ((senders >= 0) & (senders < count)).astype(jnp.int32)]
    reduce_sum x10 -> x0, other arithmetic: 100 us -> none  [the longest x9 97.9 us: one_block(): real_part = jnp.sum(factor_re * wave_re - factor_im * wave_im, axis=1)]
    pallas_call x0 -> x4, Pallas kernels: none -> 75 us  [the longest x1 43.6 us: shards(): pl.pallas_call(functools.partial(interact_kernel, dims), out_shape=[jax.S...]
    select_n x29 -> x0, other arithmetic: 63.9 us -> none  [the longest x18 63.6 us: one_block(): factor = jnp.take(translation, block_pairs[:, 1].reshape(-1), axis=0)]
    mul x11 -> x0, local copies, waits for them, and re-layouts: 53.5 us -> none  [the longest x9 51.8 us: one_block(): real_part = jnp.sum(factor_re * wave_re - factor_im * wave_im, axis=1)]
    ppermute x16 -> x19, starting transfers between devices: 54.1 us -> 15.9 us  [the longest x8 13.2 us: shards(): lax.ppermute(part, 'space', [(e, (e + o) % count) for e in range(count)])]
    another operation x1 -> x0, other arithmetic: 32.3 us -> none
  transfers between devices with their start and end apart: 17 -> 19, of which waited for: 1 -> 7; matrix products, arithmetic and copies ran while one was open for 2% -> 6% of each run, Pallas kernels for 0% -> 0%
where the time goes in v1:
time: 115 us
  Pallas kernels  75 us (65%)
  starting transfers between devices  15.9 us (14%)
  local copies, waits for them, and re-layouts  10.7 us (9%)
  waiting for transfers between devices  10 us (9%)
  other arithmetic  2.11 us (2%)
    pallas_call x1, Pallas kernels, shards(): pl.pallas_call(functools.partial(interact_kernel, dims), out_shape=[jax.S...  43.6 us
    pallas_call x1, Pallas kernels, shards(): pl.pallas_call(upward_kernel, out_shape=jax.ShapeDtypeStruct((held, 2 * r...  26.7 us
    ppermute x8, starting transfers between devices, shards(): lax.ppermute(part, 'space', [(e, (e + o) % count) for e in range(count)])  13.2 us
    ppermute x8, waiting for transfers between devices, shards(): lax.ppermute(part, 'space', [(e, (e + o) % count) for e in range(count)])  8.46 us
    unnamed x59, local copies, waits for them, and re-layouts  5.41 us
    dynamic_slice x7, local copies, waits for them, and re-layouts, half_of(): return lax.dynamic_slice_in_dim(value, which * size, size, 0)  3.25 us
    ppermute x11, starting transfers between devices, swap_cores(): return lax.ppermute(value, 'rhs', [(0, 1), (1, 0)])  2.73 us
    pallas_call x1, Pallas kernels, shards(): pl.pallas_call(functools.partial(local_kernel, leaves), out_shape=[jax.Sh...  2.42 us
  transfers between devices with their start and end apart: 19, of which 7 were waited for; matrix products, arithmetic and copies ran while one was open for 6% of the time, Pallas kernels for 0%

profile of v1, /device:TPU:0, one launch (start us, length us, event | category | flops | bytes accessed | tf_op | source)
XLA Modules:
  0.0 114.6 jit_solution(15815579898371424363)
XLA Ops:
  0.7 1.8 %constant_dynamic-slice_fusion = (bf16[128,4,128]{2,1,0:T(4,128)(2,1)S(1)}, bf16[128,4,128]{2,1,0:T(4,128)(2,1)}) fusion(bf16[256,4,128]{2,1,0:T(4,128)(2,1)} %param.16, s32[]{:T(128)S(6)} %select_n.52, s32[]{:T(128)S(6)} %select_n.50), kind=kLoop, calls=%fused_computation.28 | loop fusion | bytes 524296 | tf_op jit(solution)/shard_map/dynamic_slice | solution.py:237
  4.4 0.8 copy.22.pos_ref
  5.8 26.7 %upward.1.own_ref.refs_0_ = bf16[144,8,256]{2,1,0:T(8,128)(2,1)} custom-call(s32[1]{0:T(128)} %bitcast.core_ref, s32[128]{0:T(128)} %dynamic_slice.33.counts_ref, s32[128]{0:T(128)} %dynamic_slice.34.octants_ref, f32[3,128]{1,0:T(4,128)} %freq_ref.1, f32[128,3,128]{2,1,0:T(4,128)} %copy.22.pos_ref, bf16[128,4,128]{2,1,0:T(4,128)(2,1)} %get-tuple-element.25.own_ref, ...), custom_call_target="tpu_custom_call" | custom-call | tf_op jit(solution)/shard_map/upward/pallas_call | solution.py:240
  33.0 0.7 copy-done.22
  33.7 0.7 fusion.1.leaf_ids_ref
  34.4 0.7 fusion.3.parent_ids_ref
  35.0 0.8 copy-done.1
  35.9 2.3 %pack.1 = (bf16[32,8,256]{2,1,0:T(8,128)(2,1)}, bf16[32,8,256]{2,1,0:T(8,128)(2,1)}, bf16[32,8,256]{2,1,0:T(8,128)(2,1)}, bf16[32,8,256]{2,1,0:T(8,128)(2,1)}, b...) custom-call(s32[8,24]{1,0:T(8,128)} %fusion.1.leaf_ids_ref, ...), custom_call_target="tpu_custom_call" | custom-call | tf_op jit(solution)/shard_map/pack/pallas_call | solution.py:269
  38.2 4.8 %collective-permute-start.2 = (bf16[32,8,256]{2,1,0:T(8,128)(2,1)}, bf16[32,8,256]{2,1,0:T(8,128)(2,1)S(1)}, u32[]{:S(2)}, u32[]{:S(2)}) collective-permute-start(bf16[32,8,256]{2,1,0:T(8,128)(2,1)} %get-tuple-element.12), channel_id=1, source_target_pairs={{0,24},{2,26},{4,28},{6,30},{8,0},{10,2},{12,4},{14,6},{16,8},{18,... | collective-permute-start | bytes 393224 | tf_op jit(solution)/shard_map/ppermute | solution.py:279
  43.0 1.4 %collective-permute-start.3 = (bf16[32,8,256]{2,1,0:T(8,128)(2,1)}, bf16[32,8,256]{2,1,0:T(8,128)(2,1)S(1)}, u32[]{:S(2)}, u32[]{:S(2)}) collective-permute-start(bf16[32,8,256]{2,1,0:T(8,128)(2,1)} %get-tuple-element.13), channel_id=1, source_target_pairs={{0,26},{2,28},{4,30},{6,0},{8,2},{10,4},{12,6},{14,8},{16,10},{18,... | collective-permute-start | bytes 393224 | tf_op jit(solution)/shard_map/ppermute | solution.py:279
  44.3 1.4 %collective-permute-start.4 = (bf16[32,8,256]{2,1,0:T(8,128)(2,1)}, bf16[32,8,256]{2,1,0:T(8,128)(2,1)S(1)}, u32[]{:S(2)}, u32[]{:S(2)}) collective-permute-start(bf16[32,8,256]{2,1,0:T(8,128)(2,1)} %get-tuple-element.14), channel_id=1, source_target_pairs={{0,28},{2,30},{4,0},{6,2},{8,4},{10,6},{12,8},{14,10},{16,12},{18,... | collective-permute-start | bytes 393224 | tf_op jit(solution)/shard_map/ppermute | solution.py:279
  45.7 1.4 %collective-permute-start.5 = (bf16[32,8,256]{2,1,0:T(8,128)(2,1)}, bf16[32,8,256]{2,1,0:T(8,128)(2,1)S(1)}, u32[]{:S(2)}, u32[]{:S(2)}) collective-permute-start(bf16[32,8,256]{2,1,0:T(8,128)(2,1)} %get-tuple-element.15), channel_id=1, source_target_pairs={{0,30},{2,0},{4,2},{6,4},{8,6},{10,8},{12,10},{14,12},{16,14},{18,... | collective-permute-start | bytes 393224 | tf_op jit(solution)/shard_map/ppermute | solution.py:279
  47.8 0.9 collective-permute-start.7
  48.8 1.7 %collective-permute-done.3.refs_3_ = bf16[32,8,256]{2,1,0:T(8,128)(2,1)S(1)} collective-permute-done((bf16[32,8,256]{2,1,0:T(8,128)(2,1)}, bf16[32,8,256]{2,1,0:T(8,128)(2,1)S(1)}, u32[]{:S(2)}, u32[]{:S(2)}) %collective-permute-start.3) | collective-permute-done | bytes 131104 | tf_op jit(solution)/shard_map/ppermute | solution.py:279
  50.5 2.2 %collective-permute-start.8 = (bf16[32,8,256]{2,1,0:T(8,128)(2,1)S(1)}, bf16[32,8,256]{2,1,0:T(8,128)(2,1)S(1)}, u32[]{:S(2)}, u32[]{:S(2)}) collective-permute-start(bf16[32,8,256]{2,1,0:T(8,128)(2,1)S(1)} %copy-done.25), channel_id=1, source_target_pairs={{0,6},{2,8},{4,10},{6,12},{8,14},{10,16},{12,18},{14,20},{16,22},{... | collective-permute-start | bytes 393224 | tf_op jit(solution)/shard_map/ppermute | solution.py:279
  53.7 2.8 %collective-permute-done.5.refs_5_ = bf16[32,8,256]{2,1,0:T(8,128)(2,1)S(1)} collective-permute-done((bf16[32,8,256]{2,1,0:T(8,128)(2,1)}, bf16[32,8,256]{2,1,0:T(8,128)(2,1)S(1)}, u32[]{:S(2)}, u32[]{:S(2)}) %collective-permute-start.5) | collective-permute-done | bytes 131104 | tf_op jit(solution)/shard_map/ppermute | solution.py:279
  56.6 1.4 %collective-permute-done.6.refs_6_ = bf16[32,8,256]{2,1,0:T(8,128)(2,1)S(1)} collective-permute-done((bf16[32,8,256]{2,1,0:T(8,128)(2,1)}, bf16[32,8,256]{2,1,0:T(8,128)(2,1)S(1)}, u32[]{:S(2)}, u32[]{:S(2)}) %collective-permute-start.6) | collective-permute-done | bytes 131104 | tf_op jit(solution)/shard_map/ppermute | solution.py:279
  59.2 1.7 %collective-permute-done.9.refs_9_ = bf16[32,8,256]{2,1,0:T(8,128)(2,1)S(1)} collective-permute-done((bf16[32,8,256]{2,1,0:T(8,128)(2,1)S(1)}, bf16[32,8,256]{2,1,0:T(8,128)(2,1)S(1)}, u32[]{:S(2)}, u32[]{:S(2)}) %collective-permute-start.9) | collective-permute-done | bytes 131104 | tf_op jit(solution)/shard_map/ppermute | solution.py:279
  62.5 0.7 reshape_squeeze.7.class_ref
  63.3 0.8 reshape_squeeze.6.source_ref
  66.2 43.6 %interact.1 = (bf16[144,4,256]{2,1,0:T(4,128)(2,1)}, bf16[144,4,256]{2,1,0:T(4,128)(2,1)}) custom-call(s32[9]{0:T(128)} %pad_add_fusion.info_ref, s32[27648]{0:T(1024)} %reshape_squeeze.6.source_ref, s32[27648]{0:T(1024)} %reshape_squeeze.7.class_ref, bf16[144,8,256]{2,1,0:T(8,128)(2,1)} %upward.1.own_ref.refs_0_, bf16[144,8,256]{2,1,0:T(8,128)(2,1)} %copy-done.1, ...), custom_call_target="tpu_custom_call" | custom-call | tf_op jit(solution)/shard_map/interact/pallas_call | solution.py:295
  110.0 1.5 %collective-permute-done.18.recv_ref = bf16[144,4,256]{2,1,0:T(4,128)(2,1)S(1)} collective-permute-done((bf16[144,4,256]{2,1,0:T(4,128)(2,1)}, bf16[144,4,256]{2,1,0:T(4,128)(2,1)S(1)}, u32[]{:S(2)}, u32[]{:S(2)}) %collective-permute-start.18) | collective-permute-done | bytes 294944 | tf_op jit(solution)/shard_map/ppermute | solution.py:29
  111.5 0.7 copy-done.2
  112.2 2.4 %local.1 = (f32[256,4,256]{2,1,0:T(4,128)}, f32[32,4,256]{2,1,0:T(4,128)}) custom-call(s32[1]{0:T(128)} %bitcast.core_ref, bf16[144,4,256]{2,1,0:T(4,128)(2,1)} %get-tuple-element.20.keep_ref, bf16[144,4,256]{2,1,0:T(4,128)(2,1)} %copy-done.2, bf16[256,256]{1,0:T(8,128)(2,1)} %mat_ref.1), custom_call_target="tpu_custom_call" | custom-call | tf_op jit(solution)/shard_map/local/pallas_call | solution.py:308
  (94 shorter events, 9.9 us)
Async XLA Ops:
  2.4 2.8 %collective-permute-start = (bf16[128,4,128]{2,1,0:T(4,128)(2,1)S(1)}, bf16[128,4,128]{2,1,0:T(4,128)(2,1)S(1)}, u32[]{:S(2)}, u32[]{:S(2)}) collective-permute-start(bf16[128,4,128]{2,1,0:T(4,128)(2,1)S(1)} %get-tuple-element.24), channel_id=1, source_target_pairs={{0,1},{1,0},{2,3},{3,2},{4,5},{5,4},{6,7},{7,6},{8,9},{9,8},{10,11... | collective-permute-start | bytes 393224 | tf_op jit(solution)/shard_map/ppermute | solution.py:29
  32.5 2.5 %collective-permute-start.1 = (bf16[144,8,256]{2,1,0:T(8,128)(2,1)}, bf16[144,8,256]{2,1,0:T(8,128)(2,1)S(1)}, u32[]{:S(2)}, u32[]{:S(2)}) collective-permute-start(bf16[144,8,256]{2,1,0:T(8,128)(2,1)} %upward.1.own_ref.refs_0_), channel_id=1, source_target_pairs={{0,1},{1,0},{2,3},{3,2},{4,5},{5,4},{6,7},{7,6},{8,9},{9,8},{10,11... | collective-permute-start | bytes 1769480 | tf_op jit(solution)/shard_map/ppermute | solution.py:29
  35.0 13.6 %copy-start.20 = (s32[256,2,189]{0,1,2:T(2,128)S(1)}, s32[256,2,189]{0,1,2:T(2,128)}, u32[]{:S(2)}) copy-start(s32[256,2,189]{0,1,2:T(2,128)} %param.25) | copy-start | bytes 1161220
  38.2 9.6 %collective-permute-start.2 = (bf16[32,8,256]{2,1,0:T(8,128)(2,1)}, bf16[32,8,256]{2,1,0:T(8,128)(2,1)S(1)}, u32[]{:S(2)}, u32[]{:S(2)}) collective-permute-start(bf16[32,8,256]{2,1,0:T(8,128)(2,1)} %get-tuple-element.12), channel_id=1, source_target_pairs={{0,24},{2,26},{4,28},{6,30},{8,0},{10,2},{12,4},{14,6},{16,8},{18,... | collective-permute-start | bytes 393224 | tf_op jit(solution)/shard_map/ppermute | solution.py:279
  43.0 7.5 %collective-permute-start.3 = (bf16[32,8,256]{2,1,0:T(8,128)(2,1)}, bf16[32,8,256]{2,1,0:T(8,128)(2,1)S(1)}, u32[]{:S(2)}, u32[]{:S(2)}) collective-permute-start(bf16[32,8,256]{2,1,0:T(8,128)(2,1)} %get-tuple-element.13), channel_id=1, source_target_pairs={{0,26},{2,28},{4,30},{6,0},{8,2},{10,4},{12,6},{14,8},{16,10},{18,... | collective-permute-start | bytes 393224 | tf_op jit(solution)/shard_map/ppermute | solution.py:279
  44.3 8.8 %collective-permute-start.4 = (bf16[32,8,256]{2,1,0:T(8,128)(2,1)}, bf16[32,8,256]{2,1,0:T(8,128)(2,1)S(1)}, u32[]{:S(2)}, u32[]{:S(2)}) collective-permute-start(bf16[32,8,256]{2,1,0:T(8,128)(2,1)} %get-tuple-element.14), channel_id=1, source_target_pairs={{0,28},{2,30},{4,0},{6,2},{8,4},{10,6},{12,8},{14,10},{16,12},{18,... | collective-permute-start | bytes 393224 | tf_op jit(solution)/shard_map/ppermute | solution.py:279
  45.7 10.8 %collective-permute-start.5 = (bf16[32,8,256]{2,1,0:T(8,128)(2,1)}, bf16[32,8,256]{2,1,0:T(8,128)(2,1)S(1)}, u32[]{:S(2)}, u32[]{:S(2)}) collective-permute-start(bf16[32,8,256]{2,1,0:T(8,128)(2,1)} %get-tuple-element.15), channel_id=1, source_target_pairs={{0,30},{2,0},{4,2},{6,4},{8,6},{10,8},{12,10},{14,12},{16,14},{18,... | collective-permute-start | bytes 393224 | tf_op jit(solution)/shard_map/ppermute | solution.py:279
  47.2 10.8 %collective-permute-start.6 = (bf16[32,8,256]{2,1,0:T(8,128)(2,1)}, bf16[32,8,256]{2,1,0:T(8,128)(2,1)S(1)}, u32[]{:S(2)}, u32[]{:S(2)}) collective-permute-start(bf16[32,8,256]{2,1,0:T(8,128)(2,1)} %get-tuple-element.16), channel_id=1, source_target_pairs={{0,2},{2,4},{4,6},{6,8},{8,10},{10,12},{12,14},{14,16},{16,18},{18... | collective-permute-start | bytes 393224 | tf_op jit(solution)/shard_map/ppermute | solution.py:279
  47.8 8.8 %copy-start.3 = (bf16[32,8,256]{2,1,0:T(8,128)(2,1)}, bf16[32,8,256]{2,1,0:T(8,128)(2,1)S(1)}, u32[]{:S(2)}) copy-start(bf16[32,8,256]{2,1,0:T(8,128)(2,1)S(1)} %collective-permute-done.2.refs_2_) | copy-start | bytes 393220
  47.8 10.2 %collective-permute-start.7 = (bf16[32,8,256]{2,1,0:T(8,128)(2,1)}, bf16[32,8,256]{2,1,0:T(8,128)(2,1)S(1)}, u32[]{:S(2)}, u32[]{:S(2)}) collective-permute-start(bf16[32,8,256]{2,1,0:T(8,128)(2,1)} %get-tuple-element.17), channel_id=1, source_target_pairs={{0,4},{2,6},{4,8},{6,10},{8,12},{10,14},{12,16},{14,18},{16,20},{1... | collective-permute-start | bytes 393224 | tf_op jit(solution)/shard_map/ppermute | solution.py:279
  48.7 9.8 %copy-start.21 = (s32[32,2,189]{2,1,0:T(2,128)S(1)}, s32[32,2,189]{2,1,0:T(2,128)}, u32[]{:S(2)}) copy-start(s32[32,2,189]{2,1,0:T(2,128)} %param.26) | copy-start | bytes 145156
  50.5 8.2 %copy-start.4 = (bf16[32,8,256]{2,1,0:T(8,128)(2,1)}, bf16[32,8,256]{2,1,0:T(8,128)(2,1)S(1)}, u32[]{:S(2)}) copy-start(bf16[32,8,256]{2,1,0:T(8,128)(2,1)S(1)} %collective-permute-done.3.refs_3_) | copy-start | bytes 393220
  50.5 8.8 %collective-permute-start.8 = (bf16[32,8,256]{2,1,0:T(8,128)(2,1)S(1)}, bf16[32,8,256]{2,1,0:T(8,128)(2,1)S(1)}, u32[]{:S(2)}, u32[]{:S(2)}) collective-permute-start(bf16[32,8,256]{2,1,0:T(8,128)(2,1)S(1)} %copy-done.25), channel_id=1, source_target_pairs={{0,6},{2,8},{4,10},{6,12},{8,14},{10,16},{12,18},{14,20},{16,22},{... | collective-permute-start | bytes 393224 | tf_op jit(solution)/shard_map/ppermute | solution.py:279
  53.2 5.5 %copy-start.5 = (bf16[32,8,256]{2,1,0:T(8,128)(2,1)}, bf16[32,8,256]{2,1,0:T(8,128)(2,1)S(1)}, u32[]{:S(2)}) copy-start(bf16[32,8,256]{2,1,0:T(8,128)(2,1)S(1)} %collective-permute-done.4.refs_4_) | copy-start | bytes 393220
  53.2 7.7 %collective-permute-start.9 = (bf16[32,8,256]{2,1,0:T(8,128)(2,1)S(1)}, bf16[32,8,256]{2,1,0:T(8,128)(2,1)S(1)}, u32[]{:S(2)}, u32[]{:S(2)}) collective-permute-start(bf16[32,8,256]{2,1,0:T(8,128)(2,1)S(1)} %copy-done.24), channel_id=1, source_target_pairs={{0,8},{2,10},{4,12},{6,14},{8,16},{10,18},{12,20},{14,22},{16,24},... | collective-permute-start | bytes 393224 | tf_op jit(solution)/shard_map/ppermute | solution.py:279
  56.6 4.3 %collective-permute-start.10 = (bf16[32,8,256]{2,1,0:T(8,128)(2,1)S(1)}, bf16[32,8,256]{2,1,0:T(8,128)(2,1)S(1)}, u32[]{:S(2)}, u32[]{:S(2)}) collective-permute-start(bf16[32,8,256]{2,1,0:T(8,128)(2,1)S(1)} %collective-permute-done.2.refs_2_), channel_id=1, source_target_pairs={{0,1},{1,0},{2,3},{3,2},{4,5},{5,4},{6,7},{7,6},{8,9},{9,8},{10,11... | collective-permute-start | bytes 393224 | tf_op jit(solution)/shard_map/ppermute | solution.py:29
  58.0 3.5 %collective-permute-start.11 = (bf16[32,8,256]{2,1,0:T(8,128)(2,1)S(1)}, bf16[32,8,256]{2,1,0:T(8,128)(2,1)S(1)}, u32[]{:S(2)}, u32[]{:S(2)}) collective-permute-start(bf16[32,8,256]{2,1,0:T(8,128)(2,1)S(1)} %collective-permute-done.3.refs_3_), channel_id=1, source_target_pairs={{0,1},{1,0},{2,3},{3,2},{4,5},{5,4},{6,7},{7,6},{8,9},{9,8},{10,11... | collective-permute-start | bytes 393224 | tf_op jit(solution)/shard_map/ppermute | solution.py:29
  58.0 3.6 %collective-permute-start.12 = (bf16[32,8,256]{2,1,0:T(8,128)(2,1)S(1)}, bf16[32,8,256]{2,1,0:T(8,128)(2,1)S(1)}, u32[]{:S(2)}, u32[]{:S(2)}) collective-permute-start(bf16[32,8,256]{2,1,0:T(8,128)(2,1)S(1)} %collective-permute-done.4.refs_4_), channel_id=1, source_target_pairs={{0,1},{1,0},{2,3},{3,2},{4,5},{5,4},{6,7},{7,6},{8,9},{9,8},{10,11... | collective-permute-start | bytes 393224 | tf_op jit(solution)/shard_map/ppermute | solution.py:29
  59.2 5.5 %collective-permute-start.13 = (bf16[32,8,256]{2,1,0:T(8,128)(2,1)S(1)}, bf16[32,8,256]{2,1,0:T(8,128)(2,1)S(1)}, u32[]{:S(2)}, u32[]{:S(2)}) collective-permute-start(bf16[32,8,256]{2,1,0:T(8,128)(2,1)S(1)} %collective-permute-done.5.refs_5_), channel_id=1, source_target_pairs={{0,1},{1,0},{2,3},{3,2},{4,5},{5,4},{6,7},{7,6},{8,9},{9,8},{10,11... | collective-permute-start | bytes 393224 | tf_op jit(solution)/shard_map/ppermute | solution.py:29
  60.9 3.8 %collective-permute-start.14 = (bf16[32,8,256]{2,1,0:T(8,128)(2,1)S(1)}, bf16[32,8,256]{2,1,0:T(8,128)(2,1)S(1)}, u32[]{:S(2)}, u32[]{:S(2)}) collective-permute-start(bf16[32,8,256]{2,1,0:T(8,128)(2,1)S(1)} %collective-permute-done.6.refs_6_), channel_id=1, source_target_pairs={{0,1},{1,0},{2,3},{3,2},{4,5},{5,4},{6,7},{7,6},{8,9},{9,8},{10,11... | collective-permute-start | bytes 393224 | tf_op jit(solution)/shard_map/ppermute | solution.py:29
  60.9 3.8 %collective-permute-start.15 = (bf16[32,8,256]{2,1,0:T(8,128)(2,1)S(1)}, bf16[32,8,256]{2,1,0:T(8,128)(2,1)S(1)}, u32[]{:S(2)}, u32[]{:S(2)}) collective-permute-start(bf16[32,8,256]{2,1,0:T(8,128)(2,1)S(1)} %collective-permute-done.7.refs_7_), channel_id=1, source_target_pairs={{0,1},{1,0},{2,3},{3,2},{4,5},{5,4},{6,7},{7,6},{8,9},{9,8},{10,11... | collective-permute-start | bytes 393224 | tf_op jit(solution)/shard_map/ppermute | solution.py:29
  61.5 3.2 %collective-permute-start.16 = (bf16[32,8,256]{2,1,0:T(8,128)(2,1)S(1)}, bf16[32,8,256]{2,1,0:T(8,128)(2,1)S(1)}, u32[]{:S(2)}, u32[]{:S(2)}) collective-permute-start(bf16[32,8,256]{2,1,0:T(8,128)(2,1)S(1)} %collective-permute-done.8.refs_8_), channel_id=1, source_target_pairs={{0,1},{1,0},{2,3},{3,2},{4,5},{5,4},{6,7},{7,6},{8,9},{9,8},{10,11... | collective-permute-start | bytes 393224 | tf_op jit(solution)/shard_map/ppermute | solution.py:29
  61.6 3.2 %collective-permute-start.17 = (bf16[32,8,256]{2,1,0:T(8,128)(2,1)S(1)}, bf16[32,8,256]{2,1,0:T(8,128)(2,1)S(1)}, u32[]{:S(2)}, u32[]{:S(2)}) collective-permute-start(bf16[32,8,256]{2,1,0:T(8,128)(2,1)S(1)} %collective-permute-done.9.refs_9_), channel_id=1, source_target_pairs={{0,1},{1,0},{2,3},{3,2},{4,5},{5,4},{6,7},{7,6},{8,9},{9,8},{10,11... | collective-permute-start | bytes 393224 | tf_op jit(solution)/shard_map/ppermute | solution.py:29
  109.7 1.8 %collective-permute-start.18 = (bf16[144,4,256]{2,1,0:T(4,128)(2,1)}, bf16[144,4,256]{2,1,0:T(4,128)(2,1)S(1)}, u32[]{:S(2)}, u32[]{:S(2)}) collective-permute-start(bf16[144,4,256]{2,1,0:T(4,128)(2,1)} %get-tuple-element.21), channel_id=1, source_target_pairs={{0,1},{1,0},{2,3},{3,2},{4,5},{5,4},{6,7},{7,6},{8,9},{9,8},{10,11... | collective-permute-start | bytes 884744 | tf_op jit(solution)/shard_map/ppermute | solution.py:29
  (24 other events, 36.5 us)

commit v2 on v1

v2 whole, which is shorter than its diff:
```python
import functools
import math

import jax
import jax.numpy as jnp
from jax import lax
from jax.experimental import pallas as pl
from jax.experimental.pallas import tpu as pltpu
from jax.sharding import PartitionSpec as P

F32 = jnp.float32
BF16 = jnp.bfloat16
CHUNKS = 3
GROUP = 9
LEAF_UNROLL = 8
SIN_POLY = (4.44286790342698, -7.307443431653506, 3.594788153158899, -0.7843741906863176)
COS_POLY = (
    1.4142134967586113,
    -6.978850998632011,
    5.7394613208713325,
    -1.883563790130787,
    0.31069962133630835,
)

VMEM = pl.BlockSpec(memory_space=pltpu.VMEM)
SMEM = pl.BlockSpec(memory_space=pltpu.SMEM)


def swap_cores(value):
    return lax.ppermute(value, "rhs", [(0, 1), (1, 0)])


def horner(coefficients, x):
    total = coefficients[-1] * x + coefficients[-2]
    for coefficient in coefficients[-3::-1]:
        total = total * x + coefficient
    return total


def tree(values):
    values = list(values)
    while len(values) > 1:
        paired = [values[i] + values[i + 1] for i in range(0, len(values) - 1, 2)]
        values = paired + values[2 * len(paired) :]
    return values[0]


def sin_cos_turns(turns):
    r = turns - jnp.round(turns)
    r2 = r * r
    s = r * horner(SIN_POLY, r2)
    c = horner(COS_POLY, r2)
    return s * c, 1.0 - s * s


def upward_kernel(
    counts_ref, octants_ref, freq_ref, pos_ref, own_ref, recv_ref, shift_ref, wave_mat_ref,
    out_ref, freq_scr, mult_scr, child_scr,
):
    core = lax.axis_index("rhs")
    leaves, rhs_half, slots = recv_ref.shape
    nodes = freq_ref.shape[1]
    base = core * leaves
    for d in range(3):
        row = freq_ref[d : d + 1, :] * (1.0 / (2.0 * math.pi))
        freq_scr[d] = jnp.broadcast_to(row, (slots, nodes)).T
    lane = lax.broadcasted_iota(jnp.int32, (2 * rhs_half, slots), 1)

    def one_leaf(b):
        own, recv = own_ref[base + b].astype(F32), recv_ref[b].astype(F32)
        lower = jnp.where(core == 0, own, recv)
        upper = jnp.where(core == 0, recv, own)
        charge = jnp.concatenate([lower, upper], axis=0)
        charge = jnp.where(lane < counts_ref[base + b], charge, 0.0).astype(BF16)
        xs = [jnp.broadcast_to(pos_ref[d, pl.ds(base + b, 1), :], (nodes, slots)) for d in range(3)]
        turns = freq_scr[0] * xs[0] + freq_scr[1] * xs[1] + freq_scr[2] * xs[2]
        sin, cos = sin_cos_turns(turns)
        basis = jnp.concatenate([cos.astype(BF16), sin.astype(BF16)], axis=0)
        multipole = lax.dot_general(
            charge, basis, (((1,), (1,)), ((), ())), preferred_element_type=F32
        ).astype(BF16)
        mult_scr[b] = multipole
        child_scr[octants_ref[base + b], b // 8] = multipole

    def step(g, carry):
        for k in range(LEAF_UNROLL):
            one_leaf(g * LEAF_UNROLL + k)
        return carry

    lax.fori_loop(0, leaves // LEAF_UNROLL, step, 0)
    parents = leaves // 8
    rhs, width = mult_scr.shape[1:]
    wave_mat = wave_mat_ref[...]
    multipoles = mult_scr[...].reshape(leaves * rhs, width)
    waves = jnp.dot(multipoles, wave_mat, preferred_element_type=F32).astype(BF16)
    out_ref[:leaves] = waves.reshape(leaves, rhs, width)
    summed = None
    for octant in range(8):
        part = jnp.dot(
            child_scr[octant].reshape(parents * rhs, width),
            shift_ref[octant],
            preferred_element_type=F32,
        )
        summed = part if summed is None else summed + part
    parent_waves = jnp.dot(summed.astype(BF16), wave_mat, preferred_element_type=F32)
    out_ref[leaves:] = parent_waves.astype(BF16).reshape(parents, rhs, width)


def plan_kernel(local_rows, chunk, leaf_ref, parent_ref, source_out, class_out, chunks_out):
    core = lax.axis_index("rhs")
    list_len = leaf_ref.shape[0]
    targets = source_out.shape[0] // 2
    parents = parent_ref.shape[0] // 2
    leaves = targets - parents
    depth = -(-list_len // 8) * 8

    def packed(source, shift):
        return source + shift * (1 << 10)

    lanes = pl.ds(pl.multiple_of(core * leaves, leaves), leaves)
    leaf_words = packed(leaf_ref[:, 0, lanes], leaf_ref[:, 1, lanes])
    rows = pl.ds(core * parents, parents)
    parent_words = packed(parent_ref[rows, 0, :], parent_ref[rows, 1, :])
    parent_words = jnp.concatenate(
        [parent_words, jnp.zeros((parents, 256 - list_len), jnp.int32)], axis=1
    )
    parent_words = jnp.concatenate(
        [parent_words, jnp.zeros((128 - parents, 256), jnp.int32)], axis=0
    ).T[:depth]
    leaf_words = jnp.concatenate(
        [leaf_words, jnp.zeros((depth - list_len, leaves), jnp.int32)], axis=0
    )
    words = jnp.concatenate([leaf_words, parent_words], axis=1)
    row = lax.broadcasted_iota(jnp.int32, words.shape, 0)
    local = ((words & 1023) < local_rows) & (row < list_len)
    below = lax.broadcasted_iota(jnp.int32, (depth, depth), 0) >= lax.broadcasted_iota(
        jnp.int32, (depth, depth), 1
    )
    running = jnp.dot(
        jnp.where(below, 1.0, 0.0).astype(BF16),
        jnp.where(local, 1.0, 0.0).astype(BF16),
        preferred_element_type=F32,
    ).astype(jnp.int32)
    total = running[depth - 1 :]
    front = jnp.where(local, words + (row + 1 - running) * (1 << 20), 0)
    back = jnp.where(local, 0, words + (total - running) * (1 << 20))
    for k in range(8):
        bit = 1 << (20 + k)
        step = 1 << k
        moved = pltpu.roll(front, depth - step, 0)
        front = jnp.where((moved & bit) != 0, moved, jnp.where((front & bit) != 0, 0, front))
        moved = pltpu.roll(back, step, 0)
        back = jnp.where((moved & bit) != 0, moved, jnp.where((back & bit) != 0, 0, back))
    words = front + back
    for out, values in (
        (source_out, (words & 1023) * 16),
        (class_out, (lax.shift_right_logical(words, 10) & 1023) * 16),
    ):
        out[:targets] = values[:128].T[:targets]
        out[targets:] = pltpu.roll(values, depth - 2 * chunk, 0)[:128].T[:targets]
    full = [(total >= n * chunk).astype(jnp.int32) for n in range(1, list_len // chunk + 1)]
    chunks_out[...] = tree(full)


def pack_kernel(leaf_ids_ref, parent_ids_ref, own_ref, recv_ref, *refs):
    core = lax.axis_index("rhs")
    rows_ref, outs = refs[0], refs[1:]
    cap_l, cap_p = leaf_ids_ref.shape[1] // 2, parent_ids_ref.shape[1] // 2
    parents = rows_ref.shape[0] // 18
    leaves = 8 * parents
    for values, which in ((own_ref, core), (recv_ref, 1 - core)):
        rows_ref[pl.ds(which * leaves, leaves)] = values[:leaves]
        rows_ref[pl.ds(2 * leaves + which * parents, parents)] = values[leaves:]
    for j, out in enumerate(outs):
        for k in range(cap_l):
            out[k] = rows_ref[leaf_ids_ref[j, core * cap_l + k]]
        for k in range(cap_p):
            out[cap_l + k] = rows_ref[2 * leaves + parent_ids_ref[j, core * cap_p + k]]


def put_rows(table, source, at, count, base, valid=None):
    half = table.shape[1]

    def body(k, carry):
        value = source[at + k].astype(F32)
        if valid is not None:
            value = jnp.where(valid, value, 0.0)
        row = pl.multiple_of((base + k) * 16, 16)
        table[pl.ds(row, 8), :] = value[:, :half]
        table[pl.ds(pl.multiple_of(row + 8, 8), 8), :] = value[:, half:]
        return carry

    lax.fori_loop(0, count, body, 0, unroll=8)


def put_all_factors(factor, trans_ref):
    half = factor.shape[1]

    def put_factors(first, values):
        for k in range(values.shape[0]):
            row = pl.multiple_of((first + k) * 16, 16)
            factor[pl.ds(row, 8), :] = jnp.broadcast_to(values[k : k + 1, :half], (8, half))
            factor[pl.ds(pl.multiple_of(row + 8, 8), 8), :] = jnp.broadcast_to(
                values[k : k + 1, half:], (8, half)
            )

    def factor_block(g, carry):
        first = pl.multiple_of(g * 8, 8)
        put_factors(first, trans_ref[pl.ds(first, 8), :])
        return carry

    full = trans_ref.shape[0] // 8 * 8
    lax.fori_loop(0, full // 8, factor_block, 0)
    if full < trans_ref.shape[0]:
        put_factors(full, trans_ref[full:, :])


def pair_sums(source_ref, class_ref, table, factor, chunk, targets):
    def accumulate(b, c, total):
        total_re, total_im = total
        first = b * 128 + jnp.where(c == 2, targets * 128, c * chunk)
        reals, imags = [], []
        for k in range(chunk):
            if k % GROUP == 0:
                span = min(GROUP, chunk - k)
                sources = source_ref.at[pl.ds(first + k, span)]
                classes = class_ref.at[pl.ds(first + k, span)]
            s = pl.multiple_of(sources[k % GROUP], 8)
            o = pl.multiple_of(classes[k % GROUP], 8)
            wave, shift = table.at[pl.ds(s, 16)], factor.at[pl.ds(o, 16)]
            wave_re, wave_im, shift_re, shift_im = wave[:8], wave[8:], shift[:8], shift[8:]
            reals.append(shift_re * wave_re - shift_im * wave_im)
            imags.append(shift_re * wave_im + shift_im * wave_re)
            if len(reals) == 3 or k == chunk - 1:
                total_re, total_im = total_re + tree(reals), total_im + tree(imags)
                reals, imags = [], []
        return total_re, total_im

    return accumulate


def near_kernel(chunk, chunks_ref, source_ref, class_ref, rows_ref, trans_ref, acc_ref, table, factor):
    put_rows(table, rows_ref, 0, rows_ref.shape[0], 0)
    put_all_factors(factor, trans_ref)
    targets = acc_ref.shape[0]
    accumulate = pair_sums(source_ref, class_ref, table, factor, chunk, targets)

    def one_target(b, carry):
        zero = jnp.zeros((8, table.shape[1]), F32)
        total = lax.fori_loop(
            0, chunks_ref[0, b], lambda c, t: accumulate(b, c, t), (zero, zero)
        )
        acc_ref[b, :8] = total[0]
        acc_ref[b, 8:] = total[1]
        return carry

    lax.fori_loop(0, targets, one_target, 0)


def rest_kernel(dims, chunks_ref, source_ref, class_ref, rows_ref, *refs):
    slots, cap_l, cap_p, chunk, chunk_count, count = dims
    near_own, near_recv = refs[:slots], refs[slots : 2 * slots]
    trans_ref, acc_ref, keep_ref, send_ref, table, factor = refs[2 * slots :]
    core = lax.axis_index("rhs")
    device = lax.axis_index("space")
    put_rows(table, rows_ref, 0, rows_ref.shape[0], 0)
    base = rows_ref.shape[0]
    for j in range(slots):
        sender = device - (j - slots // 2 if j < slots // 2 else j - slots // 2 + 1)
        valid = (sender >= 0) & (sender < count)
        for values, which in ((near_own[j], core), (near_recv[j], 1 - core)):
            put_rows(table, values, 0, cap_l, base + (2 * j + which) * cap_l, valid)
            parent_base = base + 2 * slots * cap_l + (2 * j + which) * cap_p
            put_rows(table, values, cap_l, cap_p, parent_base, valid)
    put_all_factors(factor, trans_ref)
    targets = acc_ref.shape[0]
    accumulate = pair_sums(source_ref, class_ref, table, factor, chunk, targets)

    def one_target(b, carry):
        total = lax.fori_loop(
            chunks_ref[0, b],
            chunk_count,
            lambda c, t: accumulate(b, c, t),
            (acc_ref[b, :8], acc_ref[b, 8:]),
        )
        incoming = jnp.concatenate(total, axis=1)
        lower, upper = incoming[:4], incoming[4:]
        keep_ref[b] = jnp.where(core == 0, lower, upper).astype(BF16)
        send_ref[b] = jnp.where(core == 0, upper, lower).astype(BF16)
        return carry

    lax.fori_loop(0, targets, one_target, 0)


def local_kernel(leaves, keep_ref, recv_ref, mat_ref, leaf_ref, parent_ref):
    core = lax.axis_index("rhs")
    parents = keep_ref.shape[0] - leaves
    rhs, width = keep_ref.shape[1:]
    for values, which in ((keep_ref, core), (recv_ref, 1 - core)):
        flat = values[...].reshape((leaves + parents) * rhs, width)
        local = jnp.dot(flat, mat_ref[...], preferred_element_type=F32)
        local = local.reshape(leaves + parents, rhs, width)
        leaf_ref[pl.ds(which * leaves, leaves)] = local[:leaves]
        parent_ref[pl.ds(which * parents, parents)] = local[leaves:]


def shards(
    positions, point_counts, charges, frequencies, octants, child_shift, to_wave, to_local,
    translation, send_leaf, send_parent, leaf_pairs, parent_pairs,
):
    other = 1 - lax.axis_index("rhs")
    count = lax.axis_size("space")
    leaves = positions.shape[0] // 2
    parents = leaves // 8
    rhs = charges.shape[1]
    width = to_wave.shape[0]
    slots = send_leaf.shape[1]
    near = slots // 2
    held = leaves + parents
    list_len = leaf_pairs.shape[2]
    chunk = list_len // CHUNKS
    cap_l, cap_p = send_leaf.shape[2] // 2, send_parent.shape[2] // 2
    table_rows = 2 * held + 2 * slots * (cap_l + cap_p)

    arrived_charges = swap_cores(lax.dynamic_slice_in_dim(charges, other * leaves, leaves, 0))
    index_shape = jax.ShapeDtypeStruct((2 * held, 128), jnp.int32)
    source_rows, class_rows, chunks = pl.pallas_call(
        functools.partial(plan_kernel, 2 * held, chunk),
        out_shape=[index_shape, index_shape, jax.ShapeDtypeStruct((1, 256), jnp.int32)],
        in_specs=[VMEM] * 2,
        out_specs=[VMEM] * 3,
        name="plan",
    )(jnp.transpose(leaf_pairs, (2, 1, 0)), parent_pairs)
    arrived_charges, source_rows, class_rows, chunks = lax.optimization_barrier(
        (arrived_charges, source_rows, class_rows, chunks)
    )
    source_rows, class_rows = source_rows.reshape(-1), class_rows.reshape(-1)
    waves = pl.pallas_call(
        upward_kernel,
        out_shape=jax.ShapeDtypeStruct((held, 2 * rhs, width), BF16),
        in_specs=[SMEM] * 2 + [VMEM] * 6,
        out_specs=VMEM,
        scratch_shapes=[
            pltpu.VMEM((3, width // 2, positions.shape[2]), F32),
            pltpu.VMEM((leaves, 2 * rhs, width), BF16),
            pltpu.VMEM((8, parents, 2 * rhs, width), BF16),
        ],
        name="upward",
    )(
        point_counts, octants, frequencies, jnp.transpose(positions, (1, 0, 2)), charges,
        arrived_charges, child_shift, to_wave,
    )
    arrived_waves = swap_cores(waves)
    rows, *sent = pl.pallas_call(
        pack_kernel,
        out_shape=[jax.ShapeDtypeStruct((2 * held, 2 * rhs, width), BF16)]
        + [jax.ShapeDtypeStruct((cap_l + cap_p, 2 * rhs, width), BF16)] * slots,
        in_specs=[SMEM] * 2 + [VMEM] * 2,
        out_specs=[VMEM] * (1 + slots),
        name="pack",
    )(send_leaf[0], send_parent[0], waves, arrived_waves)
    offsets = [j - near if j < near else j - near + 1 for j in range(slots)]
    near_own = [
        lax.ppermute(part, "space", [(e, (e + o) % count) for e in range(count)])
        for part, o in zip(sent, offsets)
    ]
    factor_scr = pltpu.VMEM((translation.shape[0] * 16, width // 2), F32)
    acc_shape = jax.ShapeDtypeStruct((held, 16, width // 2), F32)
    acc = pl.pallas_call(
        functools.partial(near_kernel, chunk),
        out_shape=acc_shape,
        in_specs=[SMEM] * 3 + [VMEM] * 2,
        out_specs=VMEM,
        scratch_shapes=[pltpu.VMEM((2 * held * 16, width // 2), F32), factor_scr],
        cost_estimate=pl.CostEstimate(flops=25_000_000_000, bytes_accessed=80_000_000, transcendentals=0),
        name="near",
    )(chunks, source_rows, class_rows, rows, translation)
    near_recv = [swap_cores(part) for part in near_own]
    keep, send = pl.pallas_call(
        functools.partial(rest_kernel, (slots, cap_l, cap_p, chunk, CHUNKS, count)),
        out_shape=[jax.ShapeDtypeStruct((held, rhs, width), BF16)] * 2,
        in_specs=[SMEM] * 3 + [VMEM] * (3 + 2 * slots),
        out_specs=[VMEM] * 2,
        scratch_shapes=[pltpu.VMEM((table_rows * 16, width // 2), F32), factor_scr],
        name="rest",
    )(chunks, source_rows, class_rows, rows, *near_own, *near_recv, translation, acc)
    arrived = swap_cores(send)
    return tuple(
        pl.pallas_call(
            functools.partial(local_kernel, leaves),
            out_shape=[
                jax.ShapeDtypeStruct((2 * leaves, rhs, width), F32),
                jax.ShapeDtypeStruct((2 * parents, rhs, width), F32),
            ],
            in_specs=[VMEM] * 3,
            out_specs=[VMEM] * 2,
            name="local",
        )(keep, arrived, to_local)
    )


def solution(mesh):
    in_specs = (
        P("space", None, None), P("space"), P("space", "rhs", None), P(), P("space"), P(), P(), P(),
        P(), P("space", None, None), P("space", None, None), P("space", None, None),
        P("space", None, None),
    )
    out_specs = (P("space", "rhs", None), P("space", "rhs", None))
    return jax.shard_map(shards, mesh=mesh, in_specs=in_specs, out_specs=out_specs, check_vma=False)
```

time: 115 us -> 110 us (0.957)
  local copies, waits for them, and re-layouts: 10.7 us -> 4.57 us
  waiting for transfers between devices: 10 us -> 14 us
  other arithmetic: 2.11 us -> 0 us
  starting transfers between devices: 15.9 us -> 14.5 us
    pallas_call x2 -> x4, Pallas kernels: 45.9 us -> 60.9 us  [the longest x1 33.1 us: shards(): pl.pallas_call(functools.partial(near_kernel, chunk), out_shape=acc_shape...]
    pallas_call x1, Pallas kernels: 26.7 us -> 12.5 us  [shards(): pl.pallas_call(upward_kernel, out_shape=jax.ShapeDtypeStruct((held, 2 * r...]
    ppermute x11, waiting for transfers between devices: 1.53 us -> 3.89 us  [swap_cores(): return lax.ppermute(value, 'rhs', [(0, 1), (1, 0)])]
    dynamic_slice x7 -> x1, local copies, waits for them, and re-layouts: 3.25 us -> 0.95 us  [shards(): lax.dynamic_slice_in_dim(charges, other * leaves, leaves, 0)]
    unnamed x59 -> x38, local copies, waits for them, and re-layouts: 5.41 us -> 3.61 us
    ppermute x8, waiting for transfers between devices: 8.46 us -> 10.1 us  [shards(): lax.ppermute(part, 'space', [(e, (e + o) % count) for e in range(count)])]
    another operation x2 -> x0, local copies, waits for them, and re-layouts: 1.51 us -> none  [the longest x1 0.76 us: shards(): source_rows = targets[:, 0].reshape(-1)]
    add x2 -> x0, other arithmetic: 1.35 us -> none  [the longest x1 0.68 us: shards(): jnp.where(leaf_ids // leaves == core, 0, held) + leaf_ids % leaves]
  transfers between devices with their start and end apart: 19 -> 19, of which waited for: 7 -> 9; matrix products, arithmetic and copies ran while one was open for 6% -> 0% of each run, Pallas kernels for 0% -> 33%
where the time goes in v2:
time: 110 us
  Pallas kernels  75.7 us (69%)
  starting transfers between devices  14.5 us (13%)
  waiting for transfers between devices  14 us (13%)
  local copies, waits for them, and re-layouts  4.57 us (4%)
    pallas_call x1, Pallas kernels, shards(): pl.pallas_call(functools.partial(near_kernel, chunk), out_shape=acc_shape...  33.1 us
    pallas_call x1, Pallas kernels, shards(): pl.pallas_call(functools.partial(rest_kernel, (slots, cap_l, cap_p, chunk...  21.6 us
    pallas_call x1, Pallas kernels, shards(): pl.pallas_call(upward_kernel, out_shape=jax.ShapeDtypeStruct((held, 2 * r...  12.5 us
    ppermute x8, starting transfers between devices, shards(): lax.ppermute(part, 'space', [(e, (e + o) % count) for e in range(count)])  12.4 us
    ppermute x8, waiting for transfers between devices, shards(): lax.ppermute(part, 'space', [(e, (e + o) % count) for e in range(count)])  10.1 us
    ppermute x11, waiting for transfers between devices, swap_cores(): return lax.ppermute(value, 'rhs', [(0, 1), (1, 0)])  3.89 us
    unnamed x38, local copies, waits for them, and re-layouts  3.61 us
    pallas_call x1, Pallas kernels, shards(): pl.pallas_call(functools.partial(plan_kernel, 2 * held, chunk), out_shape...  3.18 us
  transfers between devices with their start and end apart: 19, of which 9 were waited for; matrix products, arithmetic and copies ran while one was open for 0% of the time, Pallas kernels for 33%

profile of v2, /device:TPU:0, one launch (start us, length us, event | category | flops | bytes accessed | tf_op | source)
XLA Modules:
  0.0 109.6 jit_solution(10182540925894772900)
XLA Ops:
  0.6 1.0 constant_dynamic-slice_fusion
  2.1 3.2 %plan.1 = (s32[288,128]{1,0:T(8,128)}, s32[288,128]{1,0:T(8,128)}, s32[1,256]{1,0:T(1,128)}) custom-call(s32[189,2,256]{2,1,0:T(2,128)} %bitcast.7, s32[32,2,189]{2,1,0:T(2,128)} %parent_ref.1), custom_call_target="tpu_custom_call" | custom-call | tf_op jit(solution)/shard_map/plan/pallas_call | solution.py:327
  5.3 0.7 copy-done.18
  5.9 12.5 %upward.1.own_ref = bf16[144,8,256]{2,1,0:T(8,128)(2,1)} custom-call(s32[256]{0:T(256)} %counts_ref.1, s32[256]{0:T(256)} %octants_ref.1, f32[3,128]{1,0:T(4,128)} %freq_ref.1, f32[3,256,128]{2,1,0:T(8,128)} %bitcast.6, bf16[256,4,128]{2,1,0:T(4,128)(2,1)} %own_ref.1, bf16[128,4,128]{2,1,0:T(4,128)(2,1)} %copy-done.18, bf16[8,256,256]{2,1,0:T(8,128)(2,1)} %shift_ref.1, ...), custom_call_target="tpu_custom_call" | custom-call | tf_op jit(solution)/shard_map/upward/pallas_call | solution.py:338
  18.5 2.2 %collective-permute-done.1.recv_ref = bf16[144,8,256]{2,1,0:T(8,128)(2,1)S(1)} collective-permute-done((bf16[144,8,256]{2,1,0:T(8,128)(2,1)}, bf16[144,8,256]{2,1,0:T(8,128)(2,1)S(1)}, u32[]{:S(2)}, u32[]{:S(2)}) %collective-permute-start.1) | collective-permute-done | bytes 589856 | tf_op jit(solution)/shard_map/ppermute | solution.py:30
  20.6 0.8 copy-done
  21.5 3.0 %pack.1 = (bf16[288,8,256]{2,1,0:T(8,128)(2,1)}, bf16[32,8,256]{2,1,0:T(8,128)(2,1)}, bf16[32,8,256]{2,1,0:T(8,128)(2,1)}, bf16[32,8,256]{2,1,0:T(8,128)(2,1)}, ...) custom-call(s32[8,48]{1,0:T(8,128)} %bitcast.12, ...), custom_call_target="tpu_custom_call" | custom-call | tf_op jit(solution)/shard_map/pack/pallas_call | solution.py:354
  24.5 4.7 %collective-permute-start.2 = (bf16[32,8,256]{2,1,0:T(8,128)(2,1)}, bf16[32,8,256]{2,1,0:T(8,128)(2,1)S(1)}, u32[]{:S(2)}, u32[]{:S(2)}) collective-permute-start(bf16[32,8,256]{2,1,0:T(8,128)(2,1)} %get-tuple-element.28), channel_id=1, source_target_pairs={{0,24},{2,26},{4,28},{6,30},{8,0},{10,2},{12,4},{14,6},{16,8},{18,... | collective-permute-start | bytes 393224 | tf_op jit(solution)/shard_map/ppermute | solution.py:364
  29.2 1.4 %collective-permute-start.3 = (bf16[32,8,256]{2,1,0:T(8,128)(2,1)}, bf16[32,8,256]{2,1,0:T(8,128)(2,1)S(1)}, u32[]{:S(2)}, u32[]{:S(2)}) collective-permute-start(bf16[32,8,256]{2,1,0:T(8,128)(2,1)} %get-tuple-element.29), channel_id=1, source_target_pairs={{0,26},{2,28},{4,30},{6,0},{8,2},{10,4},{12,6},{14,8},{16,10},{18,... | collective-permute-start | bytes 393224 | tf_op jit(solution)/shard_map/ppermute | solution.py:364
  30.6 1.4 %collective-permute-start.4 = (bf16[32,8,256]{2,1,0:T(8,128)(2,1)}, bf16[32,8,256]{2,1,0:T(8,128)(2,1)S(1)}, u32[]{:S(2)}, u32[]{:S(2)}) collective-permute-start(bf16[32,8,256]{2,1,0:T(8,128)(2,1)} %get-tuple-element.30), channel_id=1, source_target_pairs={{0,28},{2,30},{4,0},{6,2},{8,4},{10,6},{12,8},{14,10},{16,12},{18,... | collective-permute-start | bytes 393224 | tf_op jit(solution)/shard_map/ppermute | solution.py:364
  32.0 1.4 %collective-permute-start.5 = (bf16[32,8,256]{2,1,0:T(8,128)(2,1)}, bf16[32,8,256]{2,1,0:T(8,128)(2,1)S(1)}, u32[]{:S(2)}, u32[]{:S(2)}) collective-permute-start(bf16[32,8,256]{2,1,0:T(8,128)(2,1)} %get-tuple-element.31), channel_id=1, source_target_pairs={{0,30},{2,0},{4,2},{6,4},{8,6},{10,8},{12,10},{14,12},{16,14},{18,... | collective-permute-start | bytes 393224 | tf_op jit(solution)/shard_map/ppermute | solution.py:364
  34.0 0.9 collective-permute-start.7
  34.9 1.8 %collective-permute-done.3.refs_1_ = bf16[32,8,256]{2,1,0:T(8,128)(2,1)S(1)} collective-permute-done((bf16[32,8,256]{2,1,0:T(8,128)(2,1)}, bf16[32,8,256]{2,1,0:T(8,128)(2,1)S(1)}, u32[]{:S(2)}, u32[]{:S(2)}) %collective-permute-start.3) | collective-permute-done | bytes 131104 | tf_op jit(solution)/shard_map/ppermute | solution.py:364
  36.7 1.6 %collective-permute-start.8 = (bf16[32,8,256]{2,1,0:T(8,128)(2,1)}, bf16[32,8,256]{2,1,0:T(8,128)(2,1)S(1)}, u32[]{:S(2)}, u32[]{:S(2)}) collective-permute-start(bf16[32,8,256]{2,1,0:T(8,128)(2,1)} %get-tuple-element.34), channel_id=1, source_target_pairs={{0,6},{2,8},{4,10},{6,12},{8,14},{10,16},{12,18},{14,20},{16,22},{... | collective-permute-start | bytes 393224 | tf_op jit(solution)/shard_map/ppermute | solution.py:364
  38.3 1.1 collective-permute-done.4.refs_2_
  39.8 3.1 %collective-permute-done.5.refs_3_ = bf16[32,8,256]{2,1,0:T(8,128)(2,1)S(1)} collective-permute-done((bf16[32,8,256]{2,1,0:T(8,128)(2,1)}, bf16[32,8,256]{2,1,0:T(8,128)(2,1)S(1)}, u32[]{:S(2)}, u32[]{:S(2)}) %collective-permute-start.5) | collective-permute-done | bytes 131104 | tf_op jit(solution)/shard_map/ppermute | solution.py:364
  42.8 1.4 %collective-permute-done.6.refs_4_ = bf16[32,8,256]{2,1,0:T(8,128)(2,1)S(1)} collective-permute-done((bf16[32,8,256]{2,1,0:T(8,128)(2,1)}, bf16[32,8,256]{2,1,0:T(8,128)(2,1)S(1)}, u32[]{:S(2)}, u32[]{:S(2)}) %collective-permute-start.6) | collective-permute-done | bytes 131104 | tf_op jit(solution)/shard_map/ppermute | solution.py:364
  44.7 0.9 collective-permute-done.8.refs_6_
  45.7 1.7 %collective-permute-done.9.refs_7_ = bf16[32,8,256]{2,1,0:T(8,128)(2,1)S(1)} collective-permute-done((bf16[32,8,256]{2,1,0:T(8,128)(2,1)}, bf16[32,8,256]{2,1,0:T(8,128)(2,1)S(1)}, u32[]{:S(2)}, u32[]{:S(2)}) %collective-permute-start.9) | collective-permute-done | bytes 131104 | tf_op jit(solution)/shard_map/ppermute | solution.py:364
  48.4 33.1 %near.1.refs_17_ = f32[144,16,128]{2,1,0:T(8,128)} custom-call(s32[1,256]{1,0:T(1,128)} %get-tuple-element.23.chunks_ref, s32[36864]{0:T(1024)} %bitcast.8, s32[36864]{0:T(1024)} %bitcast.10, bf16[288,8,256]{2,1,0:T(8,128)(2,1)} %get-tuple-element.27.rows_ref, f32[316,256]{1,0:T(8,128)} %refs_16_.1), custom_call_target="tpu_custom_call" | custom-call | flops 24999999488 | bytes 80000000 | tf_op jit(solution)/shard_map/near/pallas_call | solution.py:369
  83.1 21.6 %rest.1 = (bf16[144,4,256]{2,1,0:T(4,128)(2,1)}, bf16[144,4,256]{2,1,0:T(4,128)(2,1)}) custom-call(s32[1,256]{1,0:T(1,128)} %get-tuple-element.23.chunks_ref, s32[36864]{0:T(1024)} %bitcast.9, s32[36864]{0:T(1024)} %bitcast.11, bf16[288,8,256]{2,1,0:T(8,128)(2,1)} %get-tuple-element.27.rows_ref, bf16[32,8,256]{2,1,0:T(8,128)(2,1)} %copy-done.2, ...), custom_call_target="tpu_custom_call" | custom-call | tf_op jit(solution)/shard_map/rest/pallas_call | solution.py:379
  104.8 1.7 %collective-permute-done.18.recv_ref = bf16[144,4,256]{2,1,0:T(4,128)(2,1)S(1)} collective-permute-done((bf16[144,4,256]{2,1,0:T(4,128)(2,1)}, bf16[144,4,256]{2,1,0:T(4,128)(2,1)S(1)}, u32[]{:S(2)}, u32[]{:S(2)}) %collective-permute-start.18) | collective-permute-done | bytes 294944 | tf_op jit(solution)/shard_map/ppermute | solution.py:30
  106.5 0.7 copy-done.1
  107.2 2.4 %local.1 = (f32[256,4,256]{2,1,0:T(4,128)}, f32[32,4,256]{2,1,0:T(4,128)}) custom-call(bf16[144,4,256]{2,1,0:T(4,128)(2,1)} %get-tuple-element.36.keep_ref, bf16[144,4,256]{2,1,0:T(4,128)(2,1)} %copy-done.1, bf16[256,256]{1,0:T(8,128)(2,1)} %mat_ref.1), custom_call_target="tpu_custom_call" | custom-call | tf_op jit(solution)/shard_map/local/pallas_call | solution.py:389
  (59 shorter events, 4.6 us)
Async XLA Ops:
  1.6 3.7 %collective-permute-start = (bf16[128,4,128]{2,1,0:T(4,128)(2,1)S(1)}, bf16[128,4,128]{2,1,0:T(4,128)(2,1)S(1)}, u32[]{:S(2)}, u32[]{:S(2)}) collective-permute-start(bf16[128,4,128]{2,1,0:T(4,128)(2,1)S(1)} %constant_dynamic-slice_fusion), channel_id=1, source_target_pairs={{0,1},{1,0},{2,3},{3,2},{4,5},{5,4},{6,7},{7,6},{8,9},{9,8},{10,11... | collective-permute-start | bytes 393224 | tf_op jit(solution)/shard_map/ppermute | solution.py:30
  18.4 2.2 %collective-permute-start.1 = (bf16[144,8,256]{2,1,0:T(8,128)(2,1)}, bf16[144,8,256]{2,1,0:T(8,128)(2,1)S(1)}, u32[]{:S(2)}, u32[]{:S(2)}) collective-permute-start(bf16[144,8,256]{2,1,0:T(8,128)(2,1)} %upward.1.own_ref), channel_id=1, source_target_pairs={{0,1},{1,0},{2,3},{3,2},{4,5},{5,4},{6,7},{7,6},{8,9},{9,8},{10,11... | collective-permute-start | bytes 1769480 | tf_op jit(solution)/shard_map/ppermute | solution.py:30
  24.5 9.6 %collective-permute-start.2 = (bf16[32,8,256]{2,1,0:T(8,128)(2,1)}, bf16[32,8,256]{2,1,0:T(8,128)(2,1)S(1)}, u32[]{:S(2)}, u32[]{:S(2)}) collective-permute-start(bf16[32,8,256]{2,1,0:T(8,128)(2,1)} %get-tuple-element.28), channel_id=1, source_target_pairs={{0,24},{2,26},{4,28},{6,30},{8,0},{10,2},{12,4},{14,6},{16,8},{18,... | collective-permute-start | bytes 393224 | tf_op jit(solution)/shard_map/ppermute | solution.py:364
  29.2 7.5 %collective-permute-start.3 = (bf16[32,8,256]{2,1,0:T(8,128)(2,1)}, bf16[32,8,256]{2,1,0:T(8,128)(2,1)S(1)}, u32[]{:S(2)}, u32[]{:S(2)}) collective-permute-start(bf16[32,8,256]{2,1,0:T(8,128)(2,1)} %get-tuple-element.29), channel_id=1, source_target_pairs={{0,26},{2,28},{4,30},{6,0},{8,2},{10,4},{12,6},{14,8},{16,10},{18,... | collective-permute-start | bytes 393224 | tf_op jit(solution)/shard_map/ppermute | solution.py:364
  30.6 8.8 %collective-permute-start.4 = (bf16[32,8,256]{2,1,0:T(8,128)(2,1)}, bf16[32,8,256]{2,1,0:T(8,128)(2,1)S(1)}, u32[]{:S(2)}, u32[]{:S(2)}) collective-permute-start(bf16[32,8,256]{2,1,0:T(8,128)(2,1)} %get-tuple-element.30), channel_id=1, source_target_pairs={{0,28},{2,30},{4,0},{6,2},{8,4},{10,6},{12,8},{14,10},{16,12},{18,... | collective-permute-start | bytes 393224 | tf_op jit(solution)/shard_map/ppermute | solution.py:364
  32.0 10.8 %collective-permute-start.5 = (bf16[32,8,256]{2,1,0:T(8,128)(2,1)}, bf16[32,8,256]{2,1,0:T(8,128)(2,1)S(1)}, u32[]{:S(2)}, u32[]{:S(2)}) collective-permute-start(bf16[32,8,256]{2,1,0:T(8,128)(2,1)} %get-tuple-element.31), channel_id=1, source_target_pairs={{0,30},{2,0},{4,2},{6,4},{8,6},{10,8},{12,10},{14,12},{16,14},{18,... | collective-permute-start | bytes 393224 | tf_op jit(solution)/shard_map/ppermute | solution.py:364
  33.4 10.8 %collective-permute-start.6 = (bf16[32,8,256]{2,1,0:T(8,128)(2,1)}, bf16[32,8,256]{2,1,0:T(8,128)(2,1)S(1)}, u32[]{:S(2)}, u32[]{:S(2)}) collective-permute-start(bf16[32,8,256]{2,1,0:T(8,128)(2,1)} %get-tuple-element.32), channel_id=1, source_target_pairs={{0,2},{2,4},{4,6},{6,8},{8,10},{10,12},{12,14},{14,16},{16,18},{18... | collective-permute-start | bytes 393224 | tf_op jit(solution)/shard_map/ppermute | solution.py:364
  34.0 47.5 %copy-start.2 = (bf16[32,8,256]{2,1,0:T(8,128)(2,1)}, bf16[32,8,256]{2,1,0:T(8,128)(2,1)S(1)}, u32[]{:S(2)}) copy-start(bf16[32,8,256]{2,1,0:T(8,128)(2,1)S(1)} %collective-permute-done.2.refs_0_) | copy-start | bytes 393220
  34.0 10.3 %collective-permute-start.7 = (bf16[32,8,256]{2,1,0:T(8,128)(2,1)}, bf16[32,8,256]{2,1,0:T(8,128)(2,1)S(1)}, u32[]{:S(2)}, u32[]{:S(2)}) collective-permute-start(bf16[32,8,256]{2,1,0:T(8,128)(2,1)} %get-tuple-element.33), channel_id=1, source_target_pairs={{0,4},{2,6},{4,8},{6,10},{8,12},{10,14},{12,16},{14,18},{16,20},{1... | collective-permute-start | bytes 393224 | tf_op jit(solution)/shard_map/ppermute | solution.py:364
  36.7 44.8 %copy-start.3 = (bf16[32,8,256]{2,1,0:T(8,128)(2,1)}, bf16[32,8,256]{2,1,0:T(8,128)(2,1)S(1)}, u32[]{:S(2)}) copy-start(bf16[32,8,256]{2,1,0:T(8,128)(2,1)S(1)} %collective-permute-done.3.refs_1_) | copy-start | bytes 393220
  36.7 9.0 %collective-permute-start.8 = (bf16[32,8,256]{2,1,0:T(8,128)(2,1)}, bf16[32,8,256]{2,1,0:T(8,128)(2,1)S(1)}, u32[]{:S(2)}, u32[]{:S(2)}) collective-permute-start(bf16[32,8,256]{2,1,0:T(8,128)(2,1)} %get-tuple-element.34), channel_id=1, source_target_pairs={{0,6},{2,8},{4,10},{6,12},{8,14},{10,16},{12,18},{14,20},{16,22},{... | collective-permute-start | bytes 393224 | tf_op jit(solution)/shard_map/ppermute | solution.py:364
  39.4 42.1 %copy-start.4 = (bf16[32,8,256]{2,1,0:T(8,128)(2,1)}, bf16[32,8,256]{2,1,0:T(8,128)(2,1)S(1)}, u32[]{:S(2)}) copy-start(bf16[32,8,256]{2,1,0:T(8,128)(2,1)S(1)} %collective-permute-done.4.refs_2_) | copy-start | bytes 393220
  39.4 8.0 %collective-permute-start.9 = (bf16[32,8,256]{2,1,0:T(8,128)(2,1)}, bf16[32,8,256]{2,1,0:T(8,128)(2,1)S(1)}, u32[]{:S(2)}, u32[]{:S(2)}) collective-permute-start(bf16[32,8,256]{2,1,0:T(8,128)(2,1)} %get-tuple-element.35), channel_id=1, source_target_pairs={{0,8},{2,10},{4,12},{6,14},{8,16},{10,18},{12,20},{14,22},{16,24},... | collective-permute-start | bytes 393224 | tf_op jit(solution)/shard_map/ppermute | solution.py:364
  42.8 38.7 %copy-start.5 = (bf16[32,8,256]{2,1,0:T(8,128)(2,1)}, bf16[32,8,256]{2,1,0:T(8,128)(2,1)S(1)}, u32[]{:S(2)}) copy-start(bf16[32,8,256]{2,1,0:T(8,128)(2,1)S(1)} %collective-permute-done.5.refs_3_) | copy-start | bytes 393220
  42.8 4.6 %collective-permute-start.10 = (bf16[32,8,256]{2,1,0:T(8,128)(2,1)S(1)}, bf16[32,8,256]{2,1,0:T(8,128)(2,1)S(1)}, u32[]{:S(2)}, u32[]{:S(2)}) collective-permute-start(bf16[32,8,256]{2,1,0:T(8,128)(2,1)S(1)} %collective-permute-done.2.refs_0_), channel_id=1, source_target_pairs={{0,1},{1,0},{2,3},{3,2},{4,5},{5,4},{6,7},{7,6},{8,9},{9,8},{10,11... | collective-permute-start | bytes 393224 | tf_op jit(solution)/shard_map/ppermute | solution.py:30
  44.2 37.3 %copy-start.6 = (bf16[32,8,256]{2,1,0:T(8,128)(2,1)}, bf16[32,8,256]{2,1,0:T(8,128)(2,1)S(1)}, u32[]{:S(2)}) copy-start(bf16[32,8,256]{2,1,0:T(8,128)(2,1)S(1)} %collective-permute-done.6.refs_4_) | copy-start | bytes 393220
  44.2 3.7 %collective-permute-start.11 = (bf16[32,8,256]{2,1,0:T(8,128)(2,1)S(1)}, bf16[32,8,256]{2,1,0:T(8,128)(2,1)S(1)}, u32[]{:S(2)}, u32[]{:S(2)}) collective-permute-start(bf16[32,8,256]{2,1,0:T(8,128)(2,1)S(1)} %collective-permute-done.3.refs_1_), channel_id=1, source_target_pairs={{0,1},{1,0},{2,3},{3,2},{4,5},{5,4},{6,7},{7,6},{8,9},{9,8},{10,11... | collective-permute-start | bytes 393224 | tf_op jit(solution)/shard_map/ppermute | solution.py:30
  44.3 3.7 %collective-permute-start.12 = (bf16[32,8,256]{2,1,0:T(8,128)(2,1)S(1)}, bf16[32,8,256]{2,1,0:T(8,128)(2,1)S(1)}, u32[]{:S(2)}, u32[]{:S(2)}) collective-permute-start(bf16[32,8,256]{2,1,0:T(8,128)(2,1)S(1)} %collective-permute-done.4.refs_2_), channel_id=1, source_target_pairs={{0,1},{1,0},{2,3},{3,2},{4,5},{5,4},{6,7},{7,6},{8,9},{9,8},{10,11... | collective-permute-start | bytes 393224 | tf_op jit(solution)/shard_map/ppermute | solution.py:30
  45.7 35.9 %collective-permute-start.13 = (bf16[32,8,256]{2,1,0:T(8,128)(2,1)S(1)}, bf16[32,8,256]{2,1,0:T(8,128)(2,1)S(1)}, u32[]{:S(2)}, u32[]{:S(2)}) collective-permute-start(bf16[32,8,256]{2,1,0:T(8,128)(2,1)S(1)} %collective-permute-done.5.refs_3_), channel_id=1, source_target_pairs={{0,1},{1,0},{2,3},{3,2},{4,5},{5,4},{6,7},{7,6},{8,9},{9,8},{10,11... | collective-permute-start | bytes 393224 | tf_op jit(solution)/shard_map/ppermute | solution.py:30
  47.4 34.3 %collective-permute-start.14 = (bf16[32,8,256]{2,1,0:T(8,128)(2,1)S(1)}, bf16[32,8,256]{2,1,0:T(8,128)(2,1)S(1)}, u32[]{:S(2)}, u32[]{:S(2)}) collective-permute-start(bf16[32,8,256]{2,1,0:T(8,128)(2,1)S(1)} %collective-permute-done.6.refs_4_), channel_id=1, source_target_pairs={{0,1},{1,0},{2,3},{3,2},{4,5},{5,4},{6,7},{7,6},{8,9},{9,8},{10,11... | collective-permute-start | bytes 393224 | tf_op jit(solution)/shard_map/ppermute | solution.py:30
  47.4 34.3 %collective-permute-start.15 = (bf16[32,8,256]{2,1,0:T(8,128)(2,1)S(1)}, bf16[32,8,256]{2,1,0:T(8,128)(2,1)S(1)}, u32[]{:S(2)}, u32[]{:S(2)}) collective-permute-start(bf16[32,8,256]{2,1,0:T(8,128)(2,1)S(1)} %collective-permute-done.7.refs_5_), channel_id=1, source_target_pairs={{0,1},{1,0},{2,3},{3,2},{4,5},{5,4},{6,7},{7,6},{8,9},{9,8},{10,11... | collective-permute-start | bytes 393224 | tf_op jit(solution)/shard_map/ppermute | solution.py:30
  47.9 33.8 %collective-permute-start.16 = (bf16[32,8,256]{2,1,0:T(8,128)(2,1)S(1)}, bf16[32,8,256]{2,1,0:T(8,128)(2,1)S(1)}, u32[]{:S(2)}, u32[]{:S(2)}) collective-permute-start(bf16[32,8,256]{2,1,0:T(8,128)(2,1)S(1)} %collective-permute-done.8.refs_6_), channel_id=1, source_target_pairs={{0,1},{1,0},{2,3},{3,2},{4,5},{5,4},{6,7},{7,6},{8,9},{9,8},{10,11... | collective-permute-start | bytes 393224 | tf_op jit(solution)/shard_map/ppermute | solution.py:30
  48.0 33.7 %collective-permute-start.17 = (bf16[32,8,256]{2,1,0:T(8,128)(2,1)S(1)}, bf16[32,8,256]{2,1,0:T(8,128)(2,1)S(1)}, u32[]{:S(2)}, u32[]{:S(2)}) collective-permute-start(bf16[32,8,256]{2,1,0:T(8,128)(2,1)S(1)} %collective-permute-done.9.refs_7_), channel_id=1, source_target_pairs={{0,1},{1,0},{2,3},{3,2},{4,5},{5,4},{6,7},{7,6},{8,9},{9,8},{10,11... | collective-permute-start | bytes 393224 | tf_op jit(solution)/shard_map/ppermute | solution.py:30
  104.7 1.8 %collective-permute-start.18 = (bf16[144,4,256]{2,1,0:T(4,128)(2,1)}, bf16[144,4,256]{2,1,0:T(4,128)(2,1)S(1)}, u32[]{:S(2)}, u32[]{:S(2)}) collective-permute-start(bf16[144,4,256]{2,1,0:T(4,128)(2,1)} %get-tuple-element.37), channel_id=1, source_target_pairs={{0,1},{1,0},{2,3},{3,2},{4,5},{5,4},{6,7},{7,6},{8,9},{9,8},{10,11... | collective-permute-start | bytes 884744 | tf_op jit(solution)/shard_map/ppermute | solution.py:30
  (14 other events, 214.5 us)

commit v3 on v2

--- a/solution.py
+++ b/solution.py
@@ -13,6 +13,7 @@
 CHUNKS = 3
 GROUP = 9
 LEAF_UNROLL = 8
+TARGET_GROUP = 16
 SIN_POLY = (4.44286790342698, -7.307443431653506, 3.594788153158899, -0.7843741906863176)
 COS_POLY = (
     1.4142134967586113,
@@ -24,6 +25,7 @@
 
 VMEM = pl.BlockSpec(memory_space=pltpu.VMEM)
 SMEM = pl.BlockSpec(memory_space=pltpu.SMEM)
+ANY = pl.BlockSpec(memory_space=pl.ANY)
 
 
 def swap_cores(value):
@@ -165,17 +167,18 @@
 def pack_kernel(leaf_ids_ref, parent_ids_ref, own_ref, recv_ref, *refs):
     core = lax.axis_index("rhs")
     rows_ref, outs = refs[0], refs[1:]
-    cap_l, cap_p = leaf_ids_ref.shape[1] // 2, parent_ids_ref.shape[1] // 2
+    cap_l, cap_p = leaf_ids_ref.shape[1], parent_ids_ref.shape[1]
     parents = rows_ref.shape[0] // 18
     leaves = 8 * parents
     for values, which in ((own_ref, core), (recv_ref, 1 - core)):
         rows_ref[pl.ds(which * leaves, leaves)] = values[:leaves]
         rows_ref[pl.ds(2 * leaves + which * parents, parents)] = values[leaves:]
     for j, out in enumerate(outs):
+        slot = core * len(outs) + j
         for k in range(cap_l):
-            out[k] = rows_ref[leaf_ids_ref[j, core * cap_l + k]]
+            out[k] = rows_ref[leaf_ids_ref[slot, k]]
         for k in range(cap_p):
-            out[cap_l + k] = rows_ref[2 * leaves + parent_ids_ref[j, core * cap_p + k]]
+            out[cap_l + k] = rows_ref[2 * leaves + parent_ids_ref[slot, k]]
 
 
 def put_rows(table, source, at, count, base, valid=None):
@@ -239,46 +242,84 @@
     return accumulate
 
 
-def near_kernel(chunk, chunks_ref, source_ref, class_ref, rows_ref, trans_ref, acc_ref, table, factor):
+def index_copies(hbm_refs, smem_refs, sems, group, parts):
+    words = TARGET_GROUP * 128
+    part_words = hbm_refs[0].shape[0] // 2
+    copies = []
+    for hbm, smem in zip(hbm_refs, smem_refs):
+        for part in range(parts):
+            span = pl.ds(pl.multiple_of(part * part_words + group * words, 1024), words)
+            sem = sems.at[group, len(copies)]
+            copies.append(pltpu.make_async_copy(hbm.at[span], smem.at[span], sem))
+    return copies
+
+
+def over_targets(hbm_refs, smem_refs, sems, parts, targets, one_target):
+    def one_group(g, carry):
+        for copy in index_copies(hbm_refs, smem_refs, sems, g, parts):
+            copy.wait()
+        return lax.fori_loop(
+            0, TARGET_GROUP, lambda t, c: one_target(g * TARGET_GROUP + t, c), carry
+        )
+
+    lax.fori_loop(0, targets // TARGET_GROUP, one_group, 0)
+
+
+def start_indices(hbm_refs, smem_refs, sems, parts, targets):
+    for group in range(targets // TARGET_GROUP):
+        for copy in index_copies(hbm_refs, smem_refs, sems, group, parts):
+            copy.start()
+
+
+def near_kernel(
+    chunk, chunks_ref, source_ref, class_ref, rows_ref, trans_ref, acc_ref,
+    table, factor, source_scr, class_scr, sems,
+):
+    targets = acc_ref.shape[0]
+    index = ((source_ref, class_ref), (source_scr, class_scr), sems)
+    start_indices(*index, 1, targets)
     put_rows(table, rows_ref, 0, rows_ref.shape[0], 0)
     put_all_factors(factor, trans_ref)
-    targets = acc_ref.shape[0]
-    accumulate = pair_sums(source_ref, class_ref, table, factor, chunk, targets)
+    accumulate = pair_sums(source_scr, class_scr, table, factor, chunk, targets)
 
     def one_target(b, carry):
         zero = jnp.zeros((8, table.shape[1]), F32)
         total = lax.fori_loop(
-            0, chunks_ref[0, b], lambda c, t: accumulate(b, c, t), (zero, zero)
+            0, jnp.minimum(chunks_ref[0, b], 2), lambda c, t: accumulate(b, c, t), (zero, zero)
         )
         acc_ref[b, :8] = total[0]
         acc_ref[b, 8:] = total[1]
         return carry
 
-    lax.fori_loop(0, targets, one_target, 0)
+    over_targets(*index, 1, targets, one_target)
 
 
 def rest_kernel(dims, chunks_ref, source_ref, class_ref, rows_ref, *refs):
     slots, cap_l, cap_p, chunk, chunk_count, count = dims
-    near_own, near_recv = refs[:slots], refs[slots : 2 * slots]
-    trans_ref, acc_ref, keep_ref, send_ref, table, factor = refs[2 * slots :]
+    near = slots // 2
+    near_own, near_recv = refs[:near], refs[near:slots]
+    trans_ref, acc_ref, keep_ref, send_ref = refs[slots : slots + 4]
+    table, factor, source_scr, class_scr, sems = refs[slots + 4 :]
     core = lax.axis_index("rhs")
     device = lax.axis_index("space")
+    targets = acc_ref.shape[0]
+    index = ((source_ref, class_ref), (source_scr, class_scr), sems)
+    start_indices(*index, 2, targets)
     put_rows(table, rows_ref, 0, rows_ref.shape[0], 0)
     base = rows_ref.shape[0]
-    for j in range(slots):
-        sender = device - (j - slots // 2 if j < slots // 2 else j - slots // 2 + 1)
-        valid = (sender >= 0) & (sender < count)
-        for values, which in ((near_own[j], core), (near_recv[j], 1 - core)):
-            put_rows(table, values, 0, cap_l, base + (2 * j + which) * cap_l, valid)
-            parent_base = base + 2 * slots * cap_l + (2 * j + which) * cap_p
-            put_rows(table, values, cap_l, cap_p, parent_base, valid)
+    for k in range(near):
+        for values, which in ((near_own[k], core), (near_recv[k], 1 - core)):
+            slot = which * near + k
+            sender = device - jnp.where(which == 0, k - near, k + 1)
+            valid = (sender >= 0) & (sender < count)
+            put_rows(table, values, 0, cap_l, base + slot * cap_l, valid)
+            put_rows(table, values, cap_l, cap_p, base + slots * cap_l + slot * cap_p, valid)
     put_all_factors(factor, trans_ref)
-    targets = acc_ref.shape[0]
-    accumulate = pair_sums(source_ref, class_ref, table, factor, chunk, targets)
+    accumulate = pair_sums(source_scr, class_scr, table, factor, chunk, targets)
 
     def one_target(b, carry):
         total = lax.fori_loop(
-            chunks_ref[0, b],
+            jnp.minimum(chunks_ref[0, b], 2),
             chunk_count,
             lambda c, t: accumulate(b, c, t),
             (acc_ref[b, :8], acc_ref[b, 8:]),
@@ -289,7 +330,7 @@
         send_ref[b] = jnp.where(core == 0, upper, lower).astype(BF16)
         return carry
 
-    lax.fori_loop(0, targets, one_target, 0)
+    over_targets(*index, 2, targets, one_target)
 
 
 def local_kernel(leaves, keep_ref, recv_ref, mat_ref, leaf_ref, parent_ref):
@@ -319,8 +360,8 @@
     held = leaves + parents
     list_len = leaf_pairs.shape[2]
     chunk = list_len // CHUNKS
-    cap_l, cap_p = send_leaf.shape[2] // 2, send_parent.shape[2] // 2
-    table_rows = 2 * held + 2 * slots * (cap_l + cap_p)
+    cap_l, cap_p = send_leaf.shape[2], send_parent.shape[2]
+    table_rows = 2 * held + slots * (cap_l + cap_p)
 
     arrived_charges = swap_cores(lax.dynamic_slice_in_dim(charges, other * leaves, leaves, 0))
     index_shape = jax.ShapeDtypeStruct((2 * held, 128), jnp.int32)
@@ -329,6 +370,7 @@
         out_shape=[index_shape, index_shape, jax.ShapeDtypeStruct((1, 256), jnp.int32)],
         in_specs=[VMEM] * 2,
         out_specs=[VMEM] * 3,
+        compiler_params=pltpu.CompilerParams(vmem_limit_bytes=12 << 20),
         name="plan",
     )(jnp.transpose(leaf_pairs, (2, 1, 0)), parent_pairs)
     arrived_charges, source_rows, class_rows, chunks = lax.optimization_barrier(
@@ -345,6 +387,7 @@
             pltpu.VMEM((leaves, 2 * rhs, width), BF16),
             pltpu.VMEM((8, parents, 2 * rhs, width), BF16),
         ],
+        compiler_params=pltpu.CompilerParams(vmem_limit_bytes=12 << 20),
         name="upward",
     )(
         point_counts, octants, frequencies, jnp.transpose(positions, (1, 0, 2)), charges,
@@ -354,34 +397,46 @@
     rows, *sent = pl.pallas_call(
         pack_kernel,
         out_shape=[jax.ShapeDtypeStruct((2 * held, 2 * rhs, width), BF16)]
-        + [jax.ShapeDtypeStruct((cap_l + cap_p, 2 * rhs, width), BF16)] * slots,
+        + [jax.ShapeDtypeStruct((cap_l + cap_p, 2 * rhs, width), BF16)] * near,
         in_specs=[SMEM] * 2 + [VMEM] * 2,
-        out_specs=[VMEM] * (1 + slots),
+        out_specs=[VMEM] * (1 + near),
+        compiler_params=pltpu.CompilerParams(vmem_limit_bytes=12 << 20),
         name="pack",
     )(send_leaf[0], send_parent[0], waves, arrived_waves)
-    offsets = [j - near if j < near else j - near + 1 for j in range(slots)]
+    def slot_permutation(k):
+        pairs = []
+        for core, offset in ((0, k - near), (1, k + 1)):
+            pairs += [(2 * e + core, 2 * ((e + offset) % count) + core) for e in range(count)]
+        return pairs
+
     near_own = [
-        lax.ppermute(part, "space", [(e, (e + o) % count) for e in range(count)])
-        for part, o in zip(sent, offsets)
+        lax.ppermute(part, ("space", "rhs"), slot_permutation(k)) for k, part in enumerate(sent)
     ]
-    factor_scr = pltpu.VMEM((translation.shape[0] * 16, width // 2), F32)
-    acc_shape = jax.ShapeDtypeStruct((held, 16, width // 2), F32)
+    index_scratch = [
+        pltpu.VMEM((translation.shape[0] * 16, width // 2), F32),
+        pltpu.SMEM((4 * held * 64,), jnp.int32),
+        pltpu.SMEM((4 * held * 64,), jnp.int32),
+        pltpu.SemaphoreType.DMA((held // TARGET_GROUP, 4)),
+    ]
     acc = pl.pallas_call(
         functools.partial(near_kernel, chunk),
-        out_shape=acc_shape,
-        in_specs=[SMEM] * 3 + [VMEM] * 2,
+        out_shape=jax.ShapeDtypeStruct((held, 16, width // 2), F32),
+        in_specs=[SMEM] + [ANY] * 2 + [VMEM] * 2,
         out_specs=VMEM,
-        scratch_shapes=[pltpu.VMEM((2 * held * 16, width // 2), F32), factor_scr],
+        scratch_shapes=[pltpu.VMEM((2 * held * 16, width // 2), F32)] + index_scratch,
         cost_estimate=pl.CostEstimate(flops=25_000_000_000, bytes_accessed=80_000_000, transcendentals=0),
+        compiler_params=pltpu.CompilerParams(vmem_limit_bytes=16 << 20),
         name="near",
     )(chunks, source_rows, class_rows, rows, translation)
+    *near_own, acc = lax.optimization_barrier((*near_own, acc))
     near_recv = [swap_cores(part) for part in near_own]
     keep, send = pl.pallas_call(
         functools.partial(rest_kernel, (slots, cap_l, cap_p, chunk, CHUNKS, count)),
         out_shape=[jax.ShapeDtypeStruct((held, rhs, width), BF16)] * 2,
-        in_specs=[SMEM] * 3 + [VMEM] * (3 + 2 * slots),
+        in_specs=[SMEM] + [ANY] * 2 + [VMEM] * (3 + slots),
         out_specs=[VMEM] * 2,
-        scratch_shapes=[pltpu.VMEM((table_rows * 16, width // 2), F32), factor_scr],
+        scratch_shapes=[pltpu.VMEM((table_rows * 16, width // 2), F32)] + index_scratch,
+        compiler_params=pltpu.CompilerParams(vmem_limit_bytes=24 << 20),
         name="rest",
     )(chunks, source_rows, class_rows, rows, *near_own, *near_recv, translation, acc)
     arrived = swap_cores(send)
@@ -394,7 +449,8 @@
             ],
             in_specs=[VMEM] * 3,
             out_specs=[VMEM] * 2,
-            name="local",
+            compiler_params=pltpu.CompilerParams(vmem_limit_bytes=12 << 20),
+        name="local",
         )(keep, arrived, to_local)
     )
 

time: 110 us -> 84.9 us (0.77)
  Pallas kernels: 75.7 us -> 58.9 us
  waiting for transfers between devices: 14 us -> 4.95 us
  local copies, waits for them, and re-layouts: 4.57 us -> 8.91 us
  starting transfers between devices: 14.5 us -> 11 us
    ppermute x8 -> x4, waiting for transfers between devices: 10.1 us -> 0.01 us  [shards(): lax.ppermute(part, ('space', 'rhs'), slot_permutation(k))]
    pallas_call x1, Pallas kernels: 33.1 us -> 27.9 us  [shards(): pl.pallas_call(functools.partial(near_kernel, chunk), out_shape=jax.Shape...]
    pallas_call x1, Pallas kernels: 21.6 us -> 16.5 us  [shards(): pl.pallas_call(functools.partial(rest_kernel, (slots, cap_l, cap_p, chunk...]
    unnamed x38 -> x26, local copies, waits for them, and re-layouts: 3.61 us -> 7.96 us
    ppermute x8 -> x4, starting transfers between devices: 12.4 us -> 9 us  [shards(): lax.ppermute(part, ('space', 'rhs'), slot_permutation(k))]
    pallas_call x1, Pallas kernels: 2.97 us -> 0.98 us  [shards(): pl.pallas_call(pack_kernel, out_shape=[jax.ShapeDtypeStruct((2 * held, 2...]
    pallas_call x1, Pallas kernels: 12.5 us -> 10.7 us  [shards(): pl.pallas_call(upward_kernel, out_shape=jax.ShapeDtypeStruct((held, 2 * r...]
    pallas_call x1, Pallas kernels: 3.18 us -> 1.49 us  [shards(): pl.pallas_call(functools.partial(plan_kernel, 2 * held, chunk), out_shape...]
  transfers between devices with their start and end apart: 19 -> 11, of which waited for: 9 -> 6; matrix products, arithmetic and copies ran while one was open for 0% -> 0% of each run, Pallas kernels for 33% -> 35%
where the time goes in v3:
time: 84.9 us; the launch traced here: 84.5 us
  Pallas kernels  58.9 us (69%)
  starting transfers between devices  11 us (13%)
  local copies, waits for them, and re-layouts  8.91 us (10%)
  waiting for transfers between devices  4.95 us (6%)
    pallas_call x1, Pallas kernels, shards(): pl.pallas_call(functools.partial(near_kernel, chunk), out_shape=jax.Shape...  27.9 us
    pallas_call x1, Pallas kernels, shards(): pl.pallas_call(functools.partial(rest_kernel, (slots, cap_l, cap_p, chunk...  16.5 us
    pallas_call x1, Pallas kernels, shards(): pl.pallas_call(upward_kernel, out_shape=jax.ShapeDtypeStruct((held, 2 * r...  10.7 us
    ppermute x4, starting transfers between devices, shards(): lax.ppermute(part, ('space', 'rhs'), slot_permutation(k))  9 us
    unnamed x26, local copies, waits for them, and re-layouts  7.96 us
    ppermute x7, waiting for transfers between devices, swap_cores(): return lax.ppermute(value, 'rhs', [(0, 1), (1, 0)])  4.94 us
    ppermute x7, starting transfers between devices, swap_cores(): return lax.ppermute(value, 'rhs', [(0, 1), (1, 0)])  2.01 us
  transfers between devices with their start and end apart: 11, of which 6 were waited for; matrix products, arithmetic and copies ran while one was open for 0% of the time, Pallas kernels for 35%

profile of v3, /device:TPU:0, one launch (start us, length us, event | category | flops | bytes accessed | tf_op | source)
XLA Modules:
  0.0 84.5 jit_solution(382854027003269519)
XLA Ops:
  0.6 1.0 %constant_dynamic-slice_fusion = bf16[128,4,128]{2,1,0:T(4,128)(2,1)S(1)} fusion(bf16[256,4,128]{2,1,0:T(4,128)(2,1)} %own_ref.1, s32[]{:T(128)S(6)} %select_n.3), kind=kLoop, calls=%fused_computation | loop fusion | bytes 262148 | tf_op jit(solution)/shard_map/dynamic_slice | solution.py:366
  1.6 0.5 collective-permute-start
  2.1 1.0 %copy-done.3 = s32[256,2,189]{0,1,2:T(2,128)S(1)} copy-done((s32[256,2,189]{0,1,2:T(2,128)S(1)}, s32[256,2,189]{0,1,2:T(2,128)}, u32[]{:S(2)}) %copy-start.3) | copy-done | bytes 387096
  3.1 0.8 copy-done.7
  3.9 1.5 %plan.1 = (s32[288,128]{1,0:T(8,128)S(1)}, s32[288,128]{1,0:T(8,128)S(1)}, s32[1,256]{1,0:T(1,128)S(1)}) custom-call(s32[189,2,256]{2,1,0:T(2,128)S(1)} %bitcast.7, s32[32,2,189]{2,1,0:T(2,128)S(1)} %copy-done.7), custom_call_target="tpu_custom_call" | custom-call | tf_op jit(solution)/shard_map/plan/pallas_call | solution.py:368
  5.5 1.2 %copy-done = bf16[8,256,256]{2,1,0:T(8,128)(2,1)S(1)} copy-done((bf16[8,256,256]{2,1,0:T(8,128)(2,1)S(1)}, bf16[8,256,256]{2,1,0:T(8,128)(2,1)}, u32[]{:S(2)}) %copy-start) | copy-done | bytes 1048600
  6.7 0.9 %copy-done.1 = bf16[256,4,128]{2,1,0:T(4,128)(2,1)S(1)} copy-done((bf16[256,4,128]{2,1,0:T(4,128)(2,1)S(1)}, bf16[256,4,128]{2,1,0:T(4,128)(2,1)}, u32[]{:S(2)}) %copy-start.1) | copy-done | bytes 262168
  7.6 1.0 %copy-done.2 = f32[256,3,128]{2,0,1:T(8,128)S(1)} copy-done((f32[256,3,128]{2,0,1:T(8,128)S(1)}, f32[256,3,128]{2,0,1:T(8,128)}, u32[]{:S(2)}) %copy-start.2) | copy-done | bytes 393240
  8.6 0.9 %copy-done.5 = bf16[256,256]{1,0:T(8,128)(2,1)S(1)} copy-done((bf16[256,256]{1,0:T(8,128)(2,1)S(1)}, bf16[256,256]{1,0:T(8,128)(2,1)}, u32[]{:S(2)}) %copy-start.5) | copy-done | bytes 131096
  9.5 0.7 copy-done.10
  10.2 0.7 copy-done.11
  10.9 0.7 copy-done.12
  11.6 10.7 %upward.1.own_ref = bf16[144,8,256]{2,1,0:T(8,128)(2,1)S(1)} custom-call(s32[256]{0:T(256)S(1)} %copy-done.11, s32[256]{0:T(256)S(1)} %copy-done.12, f32[3,128]{1,0:T(4,128)S(1)} %copy-done.10, f32[3,256,128]{2,1,0:T(8,128)S(1)} %bitcast.6, bf16[256,4,128]{2,1,0:T(4,128)(2,1)S(1)} %copy-done.1, bf16[128,4,128]{2,1,0:T(4,128)(2,1)S(1)} %collective-permute-done.recv_ref, ...), custom_call_target="tpu_custom_call" | custom-call | tf_op jit(solution)/shard_map/upward/pallas_call | solution.py:380
  22.4 1.9 %collective-permute-done.1.recv_ref = bf16[144,8,256]{2,1,0:T(8,128)(2,1)S(1)} collective-permute-done((bf16[144,8,256]{2,1,0:T(8,128)(2,1)S(1)}, bf16[144,8,256]{2,1,0:T(8,128)(2,1)S(1)}, u32[]{:S(2)}, u32[]{:S(2)}) %collective-permute-start.1) | collective-permute-done | bytes 589856 | tf_op jit(solution)/shard_map/ppermute | solution.py:32
  24.4 1.0 %pack.1 = (bf16[288,8,256]{2,1,0:T(8,128)(2,1)S(1)}, bf16[64,8,256]{2,1,0:T(8,128)(2,1)S(1)}, bf16[64,8,256]{2,1,0:T(8,128)(2,1)S(1)}, bf16[64,8,256]{2,1,0:T(8,128)(2,1)S(1)}, bf16[64,8,256]{2,1,0:T(8,128)(2,1)S(1)}) custom-call(s32[8,48]{1,0:T(8,128)S(1)} %bitcast.12, s32[8,16]{1,0:T(8,128)S(1)} %bitcast.13, bf16[144,8,256]{2,1,0:T(8,128)(2,1)S(1)} %upward.1.own_ref, ...), custom_call_target="tpu_custom_call" | custom-call | tf_op jit(solution)/shard_map/pack/pallas_call | solution.py:397
  25.4 4.8 %collective-permute-start.2 = (bf16[64,8,256]{2,1,0:T(8,128)(2,1)S(1)}, bf16[64,8,256]{2,1,0:T(8,128)(2,1)S(1)}, u32[]{:S(2)}, u32[]{:S(2)}) collective-permute-start(bf16[64,8,256]{2,1,0:T(8,128)(2,1)S(1)} %get-tuple-element.29), channel_id=1, source_target_pairs={{0,24},{2,26},{4,28},{6,30},{8,0},{10,2},{12,4},{14,6},{16,8},{18,... | collective-permute-start | bytes 786440 | tf_op jit(solution)/shard_map/ppermute | solution.py:413
  30.1 1.4 %collective-permute-start.3 = (bf16[64,8,256]{2,1,0:T(8,128)(2,1)S(1)}, bf16[64,8,256]{2,1,0:T(8,128)(2,1)S(1)}, u32[]{:S(2)}, u32[]{:S(2)}) collective-permute-start(bf16[64,8,256]{2,1,0:T(8,128)(2,1)S(1)} %get-tuple-element.30), channel_id=1, source_target_pairs={{0,26},{2,28},{4,30},{6,0},{8,2},{10,4},{12,6},{14,8},{16,10},{18,... | collective-permute-start | bytes 786440 | tf_op jit(solution)/shard_map/ppermute | solution.py:413
  31.5 1.4 %collective-permute-start.4 = (bf16[64,8,256]{2,1,0:T(8,128)(2,1)S(1)}, bf16[64,8,256]{2,1,0:T(8,128)(2,1)S(1)}, u32[]{:S(2)}, u32[]{:S(2)}) collective-permute-start(bf16[64,8,256]{2,1,0:T(8,128)(2,1)S(1)} %get-tuple-element.31), channel_id=1, source_target_pairs={{0,28},{2,30},{4,0},{6,2},{8,4},{10,6},{12,8},{14,10},{16,12},{18,... | collective-permute-start | bytes 786440 | tf_op jit(solution)/shard_map/ppermute | solution.py:413
  32.9 1.4 %collective-permute-start.5 = (bf16[64,8,256]{2,1,0:T(8,128)(2,1)S(1)}, bf16[64,8,256]{2,1,0:T(8,128)(2,1)S(1)}, u32[]{:S(2)}, u32[]{:S(2)}) collective-permute-start(bf16[64,8,256]{2,1,0:T(8,128)(2,1)S(1)} %get-tuple-element.32), channel_id=1, source_target_pairs={{0,30},{2,0},{4,2},{6,4},{8,6},{10,8},{12,10},{14,12},{16,14},{18,... | collective-permute-start | bytes 786440 | tf_op jit(solution)/shard_map/ppermute | solution.py:413
  34.4 27.9 %near.1.refs_9_ = f32[144,16,128]{2,1,0:T(8,128)S(1)} custom-call(s32[1,256]{1,0:T(1,128)S(1)} %get-tuple-element.24.chunks_ref, s32[36864]{0:T(1024)S(1)} %bitcast.8, s32[36864]{0:T(1024)S(1)} %bitcast.10, bf16[288,8,256]{2,1,0:T(8,128)(2,1)S(1)} %get-tuple-element.28.rows_ref, f32[316,256]{1,0:T(8,128)S(1)} %copy-done.4), custom_call_target="tpu_custom_call" | custom-call | flops 24999999488 | bytes 80000000 | tf_op jit(solution)/shard_map/near/pallas_call | solution.py:421
  63.4 0.5 collective-permute-done.6.refs_4_
  65.0 16.5 %rest.1 = (bf16[144,4,256]{2,1,0:T(4,128)(2,1)S(1)}, bf16[144,4,256]{2,1,0:T(4,128)(2,1)S(1)}) custom-call(s32[1,256]{1,0:T(1,128)S(1)} %get-tuple-element.24.chunks_ref, s32[36864]{0:T(1024)S(1)} %bitcast.9, s32[36864]{0:T(1024)S(1)} %bitcast.11, bf16[288,8,256]{2,1,0:T(8,128)(2,1)S(1)} %get-tuple-element.28.rows_ref, ...), custom_call_target="tpu_custom_call" | custom-call | tf_op jit(solution)/shard_map/rest/pallas_call | solution.py:433
  81.8 1.4 %collective-permute-done.10.recv_ref = bf16[144,4,256]{2,1,0:T(4,128)(2,1)S(1)} collective-permute-done((bf16[144,4,256]{2,1,0:T(4,128)(2,1)S(1)}, bf16[144,4,256]{2,1,0:T(4,128)(2,1)S(1)}, u32[]{:S(2)}, u32[]{:S(2)}) %collective-permute-start.10) | collective-permute-done | bytes 294944 | tf_op jit(solution)/shard_map/ppermute | solution.py:32
  83.2 1.3 %local.1 = (f32[256,4,256]{2,1,0:T(4,128)}, f32[32,4,256]{2,1,0:T(4,128)}) custom-call(bf16[144,4,256]{2,1,0:T(4,128)(2,1)S(1)} %get-tuple-element.38.keep_ref, bf16[144,4,256]{2,1,0:T(4,128)(2,1)S(1)} %collective-permute-done.10.recv_ref, bf16[256,256]{1,0:T(8,128)(2,1)S(1)} %copy-done.6), custom_call_target="tpu_custom_call" | custom-call | tf_op jit(solution)/shard_map/local/pallas_call | solution.py:444
  (31 shorter events, 2.7 us)
Async XLA Ops:
  1.6 3.9 %collective-permute-start = (bf16[128,4,128]{2,1,0:T(4,128)(2,1)S(1)}, bf16[128,4,128]{2,1,0:T(4,128)(2,1)S(1)}, u32[]{:S(2)}, u32[]{:S(2)}) collective-permute-start(bf16[128,4,128]{2,1,0:T(4,128)(2,1)S(1)} %constant_dynamic-slice_fusion), channel_id=1, source_target_pairs={{0,1},{1,0},{2,3},{3,2},{4,5},{5,4},{6,7},{7,6},{8,9},{9,8},{10,11... | collective-permute-start | bytes 393224 | tf_op jit(solution)/shard_map/ppermute | solution.py:32
  2.1 1.0 %copy-start.3 = (s32[256,2,189]{0,1,2:T(2,128)S(1)}, s32[256,2,189]{0,1,2:T(2,128)}, u32[]{:S(2)}) copy-start(s32[256,2,189]{0,1,2:T(2,128)} %param.24) | copy-start | bytes 1161220
  3.1 0.8 copy-start.7
  5.4 1.2 %copy-start = (bf16[8,256,256]{2,1,0:T(8,128)(2,1)S(1)}, bf16[8,256,256]{2,1,0:T(8,128)(2,1)}, u32[]{:S(2)}) copy-start(bf16[8,256,256]{2,1,0:T(8,128)(2,1)} %shift_ref.1) | copy-start | bytes 3145732
  6.7 0.9 %copy-start.1 = (bf16[256,4,128]{2,1,0:T(4,128)(2,1)S(1)}, bf16[256,4,128]{2,1,0:T(4,128)(2,1)}, u32[]{:S(2)}) copy-start(bf16[256,4,128]{2,1,0:T(4,128)(2,1)} %own_ref.1) | copy-start | bytes 786436
  7.6 1.0 %copy-start.2 = (f32[256,3,128]{2,0,1:T(8,128)S(1)}, f32[256,3,128]{2,0,1:T(8,128)}, u32[]{:S(2)}) copy-start(f32[256,3,128]{2,0,1:T(8,128)} %param.13) | copy-start | bytes 1179652
  8.6 0.9 %copy-start.5 = (bf16[256,256]{1,0:T(8,128)(2,1)S(1)}, bf16[256,256]{1,0:T(8,128)(2,1)}, u32[]{:S(2)}) copy-start(bf16[256,256]{1,0:T(8,128)(2,1)} %wave_mat_ref.1) | copy-start | bytes 393220
  9.5 0.7 copy-start.10
  10.2 0.7 copy-start.11
  10.9 0.7 copy-start.12
  11.6 12.8 %copy-start.8 = (s32[1,8,48]{2,1,0:T(8,128)S(1)}, s32[1,8,48]{2,1,0:T(8,128)}, u32[]{:S(2)}) copy-start(s32[1,8,48]{2,1,0:T(8,128)} %param.22) | copy-start | bytes 4612
  11.6 12.8 %copy-start.9 = (s32[1,8,16]{2,1,0:T(8,128)S(1)}, s32[1,8,16]{2,1,0:T(8,128)}, u32[]{:S(2)}) copy-start(s32[1,8,16]{2,1,0:T(8,128)} %param.23) | copy-start | bytes 1540
  22.3 12.1 %copy-start.4 = (f32[316,256]{1,0:T(8,128)S(1)}, f32[316,256]{1,0:T(8,128)}, u32[]{:S(2)}) copy-start(f32[316,256]{1,0:T(8,128)} %refs_8_.1) | copy-start | bytes 970756
  22.3 2.1 %collective-permute-start.1 = (bf16[144,8,256]{2,1,0:T(8,128)(2,1)S(1)}, bf16[144,8,256]{2,1,0:T(8,128)(2,1)S(1)}, u32[]{:S(2)}, u32[]{:S(2)}) collective-permute-start(bf16[144,8,256]{2,1,0:T(8,128)(2,1)S(1)} %upward.1.own_ref), channel_id=1, source_target_pairs={{0,1},{1,0},{2,3},{3,2},{4,5},{5,4},{6,7},{7,6},{8,9},{9,8},{10,11... | collective-permute-start | bytes 1769480 | tf_op jit(solution)/shard_map/ppermute | solution.py:32
  25.4 36.9 %collective-permute-start.2 = (bf16[64,8,256]{2,1,0:T(8,128)(2,1)S(1)}, bf16[64,8,256]{2,1,0:T(8,128)(2,1)S(1)}, u32[]{:S(2)}, u32[]{:S(2)}) collective-permute-start(bf16[64,8,256]{2,1,0:T(8,128)(2,1)S(1)} %get-tuple-element.29), channel_id=1, source_target_pairs={{0,24},{2,26},{4,28},{6,30},{8,0},{10,2},{12,4},{14,6},{16,8},{18,... | collective-permute-start | bytes 786440 | tf_op jit(solution)/shard_map/ppermute | solution.py:413
  30.1 32.1 %collective-permute-start.3 = (bf16[64,8,256]{2,1,0:T(8,128)(2,1)S(1)}, bf16[64,8,256]{2,1,0:T(8,128)(2,1)S(1)}, u32[]{:S(2)}, u32[]{:S(2)}) collective-permute-start(bf16[64,8,256]{2,1,0:T(8,128)(2,1)S(1)} %get-tuple-element.30), channel_id=1, source_target_pairs={{0,26},{2,28},{4,30},{6,0},{8,2},{10,4},{12,6},{14,8},{16,10},{18,... | collective-permute-start | bytes 786440 | tf_op jit(solution)/shard_map/ppermute | solution.py:413
  31.5 30.8 %collective-permute-start.4 = (bf16[64,8,256]{2,1,0:T(8,128)(2,1)S(1)}, bf16[64,8,256]{2,1,0:T(8,128)(2,1)S(1)}, u32[]{:S(2)}, u32[]{:S(2)}) collective-permute-start(bf16[64,8,256]{2,1,0:T(8,128)(2,1)S(1)} %get-tuple-element.31), channel_id=1, source_target_pairs={{0,28},{2,30},{4,0},{6,2},{8,4},{10,6},{12,8},{14,10},{16,12},{18,... | collective-permute-start | bytes 786440 | tf_op jit(solution)/shard_map/ppermute | solution.py:413
  32.9 29.4 %collective-permute-start.5 = (bf16[64,8,256]{2,1,0:T(8,128)(2,1)S(1)}, bf16[64,8,256]{2,1,0:T(8,128)(2,1)S(1)}, u32[]{:S(2)}, u32[]{:S(2)}) collective-permute-start(bf16[64,8,256]{2,1,0:T(8,128)(2,1)S(1)} %get-tuple-element.32), channel_id=1, source_target_pairs={{0,30},{2,0},{4,2},{6,4},{8,6},{10,8},{12,10},{14,12},{16,14},{18,... | collective-permute-start | bytes 786440 | tf_op jit(solution)/shard_map/ppermute | solution.py:413
  62.3 21.0 %copy-start.6 = (bf16[256,256]{1,0:T(8,128)(2,1)S(1)}, bf16[256,256]{1,0:T(8,128)(2,1)}, u32[]{:S(2)}) copy-start(bf16[256,256]{1,0:T(8,128)(2,1)} %mat_ref.1) | copy-start | bytes 393220
  62.3 1.6 %collective-permute-start.6 = (bf16[64,8,256]{2,1,0:T(8,128)(2,1)S(1)}, bf16[64,8,256]{2,1,0:T(8,128)(2,1)S(1)}, u32[]{:S(2)}, u32[]{:S(2)}) collective-permute-start(bf16[64,8,256]{2,1,0:T(8,128)(2,1)S(1)} %collective-permute-done.2.refs_0_), channel_id=1, source_target_pairs={{0,1},{1,0},{2,3},{3,2},{4,5},{5,4},{6,7},{7,6},{8,9},{9,8},{10,11... | collective-permute-start | bytes 786440 | tf_op jit(solution)/shard_map/ppermute | solution.py:32
  62.4 1.9 %collective-permute-start.7 = (bf16[64,8,256]{2,1,0:T(8,128)(2,1)S(1)}, bf16[64,8,256]{2,1,0:T(8,128)(2,1)S(1)}, u32[]{:S(2)}, u32[]{:S(2)}) collective-permute-start(bf16[64,8,256]{2,1,0:T(8,128)(2,1)S(1)} %collective-permute-done.3.refs_1_), channel_id=1, source_target_pairs={{0,1},{1,0},{2,3},{3,2},{4,5},{5,4},{6,7},{7,6},{8,9},{9,8},{10,11... | collective-permute-start | bytes 786440 | tf_op jit(solution)/shard_map/ppermute | solution.py:32
  62.9 1.8 %collective-permute-start.8 = (bf16[64,8,256]{2,1,0:T(8,128)(2,1)S(1)}, bf16[64,8,256]{2,1,0:T(8,128)(2,1)S(1)}, u32[]{:S(2)}, u32[]{:S(2)}) collective-permute-start(bf16[64,8,256]{2,1,0:T(8,128)(2,1)S(1)} %collective-permute-done.4.refs_2_), channel_id=1, source_target_pairs={{0,1},{1,0},{2,3},{3,2},{4,5},{5,4},{6,7},{7,6},{8,9},{9,8},{10,11... | collective-permute-start | bytes 786440 | tf_op jit(solution)/shard_map/ppermute | solution.py:32
  63.0 2.1 %collective-permute-start.9 = (bf16[64,8,256]{2,1,0:T(8,128)(2,1)S(1)}, bf16[64,8,256]{2,1,0:T(8,128)(2,1)S(1)}, u32[]{:S(2)}, u32[]{:S(2)}) collective-permute-start(bf16[64,8,256]{2,1,0:T(8,128)(2,1)S(1)} %collective-permute-done.5.refs_3_), channel_id=1, source_target_pairs={{0,1},{1,0},{2,3},{3,2},{4,5},{5,4},{6,7},{7,6},{8,9},{9,8},{10,11... | collective-permute-start | bytes 786440 | tf_op jit(solution)/shard_map/ppermute | solution.py:32
  81.6 1.6 %collective-permute-start.10 = (bf16[144,4,256]{2,1,0:T(4,128)(2,1)S(1)}, bf16[144,4,256]{2,1,0:T(4,128)(2,1)S(1)}, u32[]{:S(2)}, u32[]{:S(2)}) collective-permute-start(bf16[144,4,256]{2,1,0:T(4,128)(2,1)S(1)} %get-tuple-element.39), channel_id=1, source_target_pairs={{0,1},{1,0},{2,3},{3,2},{4,5},{5,4},{6,7},{7,6},{8,9},{9,8},{10,11... | collective-permute-start | bytes 884744 | tf_op jit(solution)/shard_map/ppermute | solution.py:32

commit v4 on v3

--- a/solution.py
+++ b/solution.py
@@ -14,6 +14,7 @@
 GROUP = 9
 LEAF_UNROLL = 8
 TARGET_GROUP = 16
+FIRST_TARGETS = 112
 SIN_POLY = (4.44286790342698, -7.307443431653506, 3.594788153158899, -0.7843741906863176)
 COS_POLY = (
     1.4142134967586113,
@@ -26,6 +27,11 @@
 VMEM = pl.BlockSpec(memory_space=pltpu.VMEM)
 SMEM = pl.BlockSpec(memory_space=pltpu.SMEM)
 ANY = pl.BlockSpec(memory_space=pl.ANY)
+HBM = pl.BlockSpec(memory_space=pltpu.HBM)
+
+
+def in_hbm(*values):
+    return [pltpu.with_memory_space_constraint(value, pltpu.HBM) for value in values]
 
 
 def swap_cores(value):
@@ -56,25 +62,41 @@
 
 
 def upward_kernel(
-    counts_ref, octants_ref, freq_ref, pos_ref, own_ref, recv_ref, shift_ref, wave_mat_ref,
+    counts_hbm, octants_hbm, freq_hbm, pos_hbm, own_hbm, shift_hbm, wave_mat_hbm, recv_ref,
     out_ref, freq_scr, mult_scr, child_scr,
+    counts_ref, octants_ref, freq_ref, pos_ref, own_ref, shift_ref, wave_mat_ref, sems,
 ):
     core = lax.axis_index("rhs")
-    leaves, rhs_half, slots = recv_ref.shape
+    leaves, rhs_half, slots = own_ref.shape
     nodes = freq_ref.shape[1]
     base = core * leaves
+    half = pl.ds(pl.multiple_of(base, leaves), leaves)
+    moves = (
+        (counts_hbm, counts_ref),
+        (octants_hbm, octants_ref),
+        (freq_hbm, freq_ref),
+        (pos_hbm.at[:, half, :], pos_ref),
+        (own_hbm.at[half], own_ref),
+        (wave_mat_hbm, wave_mat_ref),
+        (shift_hbm, shift_ref),
+    )
+    copies = [pltpu.make_async_copy(a, b, sems.at[i]) for i, (a, b) in enumerate(moves)]
+    for copy in copies:
+        copy.start()
+    for copy in copies[:5]:
+        copy.wait()
     for d in range(3):
         row = freq_ref[d : d + 1, :] * (1.0 / (2.0 * math.pi))
         freq_scr[d] = jnp.broadcast_to(row, (slots, nodes)).T
     lane = lax.broadcasted_iota(jnp.int32, (2 * rhs_half, slots), 1)
 
     def one_leaf(b):
-        own, recv = own_ref[base + b].astype(F32), recv_ref[b].astype(F32)
+        own, recv = own_ref[b].astype(F32), recv_ref[base + b].astype(F32)
         lower = jnp.where(core == 0, own, recv)
         upper = jnp.where(core == 0, recv, own)
         charge = jnp.concatenate([lower, upper], axis=0)
         charge = jnp.where(lane < counts_ref[base + b], charge, 0.0).astype(BF16)
-        xs = [jnp.broadcast_to(pos_ref[d, pl.ds(base + b, 1), :], (nodes, slots)) for d in range(3)]
+        xs = [jnp.broadcast_to(pos_ref[d, pl.ds(b, 1), :], (nodes, slots)) for d in range(3)]
         turns = freq_scr[0] * xs[0] + freq_scr[1] * xs[1] + freq_scr[2] * xs[2]
         sin, cos = sin_cos_turns(turns)
         basis = jnp.concatenate([cos.astype(BF16), sin.astype(BF16)], axis=0)
@@ -90,6 +112,8 @@
         return carry
 
     lax.fori_loop(0, leaves // LEAF_UNROLL, step, 0)
+    for copy in copies[5:]:
+        copy.wait()
     parents = leaves // 8
     rhs, width = mult_scr.shape[1:]
     wave_mat = wave_mat_ref[...]
@@ -108,21 +132,33 @@
     out_ref[leaves:] = parent_waves.astype(BF16).reshape(parents, rhs, width)
 
 
-def plan_kernel(local_rows, chunk, leaf_ref, parent_ref, source_out, class_out, chunks_out):
+def plan_kernel(
+    local_rows, chunk, leaf_hbm, parent_hbm, send_leaf_hbm, send_parent_hbm, trans_hbm,
+    index_out, chunks_out, send_leaf_out, send_parent_out, trans_out, leaf_ref, parent_ref, sems,
+):
     core = lax.axis_index("rhs")
-    list_len = leaf_ref.shape[0]
-    targets = source_out.shape[0] // 2
-    parents = parent_ref.shape[0] // 2
-    leaves = targets - parents
+    list_len, _, leaves = leaf_ref.shape
+    parents = parent_ref.shape[0]
+    targets = leaves + parents
+    lanes = pl.ds(pl.multiple_of(core * leaves, leaves), leaves)
+    copies = [
+        pltpu.make_async_copy(leaf_hbm.at[:, :, lanes], leaf_ref, sems.at[0]),
+        pltpu.make_async_copy(parent_hbm.at[pl.ds(core * parents, parents)], parent_ref, sems.at[1]),
+        pltpu.make_async_copy(send_leaf_hbm, send_leaf_out, sems.at[2]),
+        pltpu.make_async_copy(send_parent_hbm, send_parent_out, sems.at[3]),
+        pltpu.make_async_copy(trans_hbm, trans_out, sems.at[4]),
+    ]
+    for copy in copies:
+        copy.start()
+    for copy in copies[:2]:
+        copy.wait()
     depth = -(-list_len // 8) * 8
 
     def packed(source, shift):
         return source + shift * (1 << 10)
 
-    lanes = pl.ds(pl.multiple_of(core * leaves, leaves), leaves)
-    leaf_words = packed(leaf_ref[:, 0, lanes], leaf_ref[:, 1, lanes])
-    rows = pl.ds(core * parents, parents)
-    parent_words = packed(parent_ref[rows, 0, :], parent_ref[rows, 1, :])
+    leaf_words = packed(leaf_ref[:, 0, :], leaf_ref[:, 1, :])
+    parent_words = packed(parent_ref[:, 0, :], parent_ref[:, 1, :])
     parent_words = jnp.concatenate(
         [parent_words, jnp.zeros((parents, 256 - list_len), jnp.int32)], axis=1
     )
@@ -154,14 +190,16 @@
         moved = pltpu.roll(back, step, 0)
         back = jnp.where((moved & bit) != 0, moved, jnp.where((back & bit) != 0, 0, back))
     words = front + back
-    for out, values in (
-        (source_out, (words & 1023) * 16),
-        (class_out, (lax.shift_right_logical(words, 10) & 1023) * 16),
-    ):
-        out[:targets] = values[:128].T[:targets]
-        out[targets:] = pltpu.roll(values, depth - 2 * chunk, 0)[:128].T[:targets]
+    sources = (words & 1023) * 16
+    classes = (lax.shift_right_logical(words, 10) & 1023) * 16
+    for h, values in enumerate((sources, classes)):
+        index_out[pl.ds(h, targets, stride=4), :] = values[:128].T[:targets]
+        tail = pltpu.roll(values, depth - 2 * chunk, 0)[:128].T[:targets]
+        index_out[pl.ds(2 + h, targets, stride=4), :] = tail
     full = [(total >= n * chunk).astype(jnp.int32) for n in range(1, list_len // chunk + 1)]
     chunks_out[...] = tree(full)
+    for copy in copies[2:]:
+        copy.wait()
 
 
 def pack_kernel(leaf_ids_ref, parent_ids_ref, own_ref, recv_ref, *refs):
@@ -218,16 +256,16 @@
         put_factors(full, trans_ref[full:, :])
 
 
-def pair_sums(source_ref, class_ref, table, factor, chunk, targets):
+def pair_sums(index_ref, table, factor, chunk):
     def accumulate(b, c, total):
         total_re, total_im = total
-        first = b * 128 + jnp.where(c == 2, targets * 128, c * chunk)
+        first = b * 512 + jnp.where(c == 2, 256, c * chunk)
         reals, imags = [], []
         for k in range(chunk):
             if k % GROUP == 0:
                 span = min(GROUP, chunk - k)
-                sources = source_ref.at[pl.ds(first + k, span)]
-                classes = class_ref.at[pl.ds(first + k, span)]
+                sources = index_ref.at[pl.ds(first + k, span)]
+                classes = index_ref.at[pl.ds(first + 128 + k, span)]
             s = pl.multiple_of(sources[k % GROUP], 8)
             o = pl.multiple_of(classes[k % GROUP], 8)
             wave, shift = table.at[pl.ds(s, 16)], factor.at[pl.ds(o, 16)]
@@ -242,71 +280,75 @@
     return accumulate
 
 
-def index_copies(hbm_refs, smem_refs, sems, group, parts):
-    words = TARGET_GROUP * 128
-    part_words = hbm_refs[0].shape[0] // 2
-    copies = []
-    for hbm, smem in zip(hbm_refs, smem_refs):
-        for part in range(parts):
-            span = pl.ds(pl.multiple_of(part * part_words + group * words, 1024), words)
-            sem = sems.at[group, len(copies)]
-            copies.append(pltpu.make_async_copy(hbm.at[span], smem.at[span], sem))
-    return copies
-
-
-def over_targets(hbm_refs, smem_refs, sems, parts, targets, one_target):
+def index_copy(index_hbm, index_scr, sems, group):
+    words = TARGET_GROUP * 512
+    span = pl.ds(pl.multiple_of(group * words, 1024), words)
+    return pltpu.make_async_copy(index_hbm.at[span], index_scr.at[span], sems.at[group])
+
+
+def over_targets(index, first, last, one_target):
     def one_group(g, carry):
-        for copy in index_copies(hbm_refs, smem_refs, sems, g, parts):
-            copy.wait()
+        @pl.when(g + 2 < last // TARGET_GROUP)
+        def _():
+            index_copy(*index, g + 2).start()
+
+        index_copy(*index, g).wait()
         return lax.fori_loop(
             0, TARGET_GROUP, lambda t, c: one_target(g * TARGET_GROUP + t, c), carry
         )
 
-    lax.fori_loop(0, targets // TARGET_GROUP, one_group, 0)
-
-
-def start_indices(hbm_refs, smem_refs, sems, parts, targets):
-    for group in range(targets // TARGET_GROUP):
-        for copy in index_copies(hbm_refs, smem_refs, sems, group, parts):
-            copy.start()
-
-
-def near_kernel(
-    chunk, chunks_ref, source_ref, class_ref, rows_ref, trans_ref, acc_ref,
-    table, factor, source_scr, class_scr, sems,
-):
-    targets = acc_ref.shape[0]
-    index = ((source_ref, class_ref), (source_scr, class_scr), sems)
-    start_indices(*index, 1, targets)
-    put_rows(table, rows_ref, 0, rows_ref.shape[0], 0)
-    put_all_factors(factor, trans_ref)
-    accumulate = pair_sums(source_scr, class_scr, table, factor, chunk, targets)
+    lax.fori_loop(first // TARGET_GROUP, last // TARGET_GROUP, one_group, 0)
+
+
+def start_indices(index, first, last):
+    for group in range(first // TARGET_GROUP, min(first // TARGET_GROUP + 2, last // TARGET_GROUP)):
+        index_copy(*index, group).start()
+
+
+def near_targets(index, first, last, chunks_ref, table, factor, chunk, acc_ref):
+    accumulate = pair_sums(index[1], table, factor, chunk)
 
     def one_target(b, carry):
         zero = jnp.zeros((8, table.shape[1]), F32)
         total = lax.fori_loop(
             0, jnp.minimum(chunks_ref[0, b], 2), lambda c, t: accumulate(b, c, t), (zero, zero)
         )
-        acc_ref[b, :8] = total[0]
-        acc_ref[b, 8:] = total[1]
+        acc_ref[b - first, :8] = total[0]
+        acc_ref[b - first, 8:] = total[1]
         return carry
 
-    over_targets(*index, 1, targets, one_target)
-
-
-def rest_kernel(dims, chunks_ref, source_ref, class_ref, rows_ref, *refs):
-    slots, cap_l, cap_p, chunk, chunk_count, count = dims
+    over_targets(index, first, last, one_target)
+
+
+def near_kernel(
+    chunk, last, chunks_ref, index_hbm, rows_ref, trans_ref, table, factor, acc_ref, index_scr, sems
+):
+    index = (index_hbm, index_scr, sems)
+    start_indices(index, 0, last)
+    put_rows(table, rows_ref, 0, rows_ref.shape[0], 0)
+    put_all_factors(factor, trans_ref)
+    near_targets(index, 0, last, chunks_ref, table, factor, chunk, acc_ref)
+
+
+def more_kernel(
+    chunk, first, last, chunks_ref, index_hbm, table, factor, acc_ref, index_scr, sems
+):
+    index = (index_hbm, index_scr, sems)
+    start_indices(index, first, last)
+    near_targets(index, first, last, chunks_ref, table, factor, chunk, acc_ref)
+
+
+def rest_kernel(dims, chunks_ref, index_hbm, table_in, factor, *refs):
+    slots, cap_l, cap_p, base, chunk, chunk_count, count = dims
     near = slots // 2
     near_own, near_recv = refs[:near], refs[near:slots]
-    trans_ref, acc_ref, keep_ref, send_ref = refs[slots : slots + 4]
-    table, factor, source_scr, class_scr, sems = refs[slots + 4 :]
+    acc_refs = refs[slots : slots + 2]
+    keep_ref, send_ref, table, index_scr, sems = refs[slots + 2 :]
     core = lax.axis_index("rhs")
     device = lax.axis_index("space")
-    targets = acc_ref.shape[0]
-    index = ((source_ref, class_ref), (source_scr, class_scr), sems)
-    start_indices(*index, 2, targets)
-    put_rows(table, rows_ref, 0, rows_ref.shape[0], 0)
-    base = rows_ref.shape[0]
+    targets = keep_ref.shape[0]
+    index = (index_hbm, index_scr, sems)
+    start_indices(index, 0, targets)
     for k in range(near):
         for values, which in ((near_own[k], core), (near_recv[k], 1 - core)):
             slot = which * near + k
@@ -314,23 +356,28 @@
             valid = (sender >= 0) & (sender < count)
             put_rows(table, values, 0, cap_l, base + slot * cap_l, valid)
             put_rows(table, values, cap_l, cap_p, base + slots * cap_l + slot * cap_p, valid)
-    put_all_factors(factor, trans_ref)
-    accumulate = pair_sums(source_scr, class_scr, table, factor, chunk, targets)
-
-    def one_target(b, carry):
-        total = lax.fori_loop(
-            jnp.minimum(chunks_ref[0, b], 2),
-            chunk_count,
-            lambda c, t: accumulate(b, c, t),
-            (acc_ref[b, :8], acc_ref[b, 8:]),
-        )
-        incoming = jnp.concatenate(total, axis=1)
-        lower, upper = incoming[:4], incoming[4:]
-        keep_ref[b] = jnp.where(core == 0, lower, upper).astype(BF16)
-        send_ref[b] = jnp.where(core == 0, upper, lower).astype(BF16)
-        return carry
-
-    over_targets(*index, 2, targets, one_target)
+    accumulate = pair_sums(index_scr, table, factor, chunk)
+    first = 0
+    for acc_ref in acc_refs:
+
+        def one_target(b, carry, acc_ref=acc_ref, first=first):
+            total = lax.fori_loop(
+                jnp.minimum(chunks_ref[0, b], 2),
+                chunk_count,
+                lambda c, t: accumulate(b, c, t),
+                (acc_ref[b - first, :8], acc_ref[b - first, 8:]),
+            )
+            incoming = jnp.concatenate(total, axis=1)
+            lower, upper = incoming[:4], incoming[4:]
+            keep_ref[b] = jnp.where(core == 0, lower, upper).astype(BF16)
+            send_ref[b] = jnp.where(core == 0, upper, lower).astype(BF16)
+            return carry
+
+        last = first + acc_ref.shape[0]
+        if first:
+            start_indices(index, first, last)
+        over_targets(index, first, last, one_target)
+        first = last
 
 
 def local_kernel(leaves, keep_ref, recv_ref, mat_ref, leaf_ref, parent_ref):
@@ -363,35 +410,61 @@
     cap_l, cap_p = send_leaf.shape[2], send_parent.shape[2]
     table_rows = 2 * held + slots * (cap_l + cap_p)
 
-    arrived_charges = swap_cores(lax.dynamic_slice_in_dim(charges, other * leaves, leaves, 0))
-    index_shape = jax.ShapeDtypeStruct((2 * held, 128), jnp.int32)
-    source_rows, class_rows, chunks = pl.pallas_call(
+    arrived_charges = swap_cores(charges)
+    indices, chunks, leaf_ids, parent_ids, factors = pl.pallas_call(
         functools.partial(plan_kernel, 2 * held, chunk),
-        out_shape=[index_shape, index_shape, jax.ShapeDtypeStruct((1, 256), jnp.int32)],
-        in_specs=[VMEM] * 2,
-        out_specs=[VMEM] * 3,
+        out_shape=[
+            jax.ShapeDtypeStruct((4 * held, 128), jnp.int32),
+            jax.ShapeDtypeStruct((1, 256), jnp.int32),
+            jax.ShapeDtypeStruct(send_leaf.shape[1:], jnp.int32),
+            jax.ShapeDtypeStruct(send_parent.shape[1:], jnp.int32),
+            jax.ShapeDtypeStruct(translation.shape, F32),
+        ],
+        in_specs=[HBM] * 5,
+        out_specs=[VMEM] * 5,
+        scratch_shapes=[
+            pltpu.VMEM((list_len, 2, leaves), jnp.int32),
+            pltpu.VMEM((parents, 2, list_len), jnp.int32),
+            pltpu.SemaphoreType.DMA((5,)),
+        ],
         compiler_params=pltpu.CompilerParams(vmem_limit_bytes=12 << 20),
         name="plan",
-    )(jnp.transpose(leaf_pairs, (2, 1, 0)), parent_pairs)
-    arrived_charges, source_rows, class_rows, chunks = lax.optimization_barrier(
-        (arrived_charges, source_rows, class_rows, chunks)
-    )
-    source_rows, class_rows = source_rows.reshape(-1), class_rows.reshape(-1)
+    )(
+        *in_hbm(
+            jnp.transpose(leaf_pairs, (2, 1, 0)), parent_pairs, send_leaf[0], send_parent[0],
+            translation,
+        )
+    )
+    arrived_charges, indices, chunks, leaf_ids, parent_ids, factors = lax.optimization_barrier(
+        (arrived_charges, indices, chunks, leaf_ids, parent_ids, factors)
+    )
+    indices = indices.reshape(-1)
     waves = pl.pallas_call(
         upward_kernel,
         out_shape=jax.ShapeDtypeStruct((held, 2 * rhs, width), BF16),
-        in_specs=[SMEM] * 2 + [VMEM] * 6,
+        in_specs=[HBM] * 7 + [VMEM],
         out_specs=VMEM,
         scratch_shapes=[
             pltpu.VMEM((3, width // 2, positions.shape[2]), F32),
             pltpu.VMEM((leaves, 2 * rhs, width), BF16),
             pltpu.VMEM((8, parents, 2 * rhs, width), BF16),
+            pltpu.SMEM(point_counts.shape, jnp.int32),
+            pltpu.SMEM(octants.shape, jnp.int32),
+            pltpu.VMEM(frequencies.shape, F32),
+            pltpu.VMEM((3, leaves, positions.shape[2]), F32),
+            pltpu.VMEM((leaves,) + charges.shape[1:], BF16),
+            pltpu.VMEM(child_shift.shape, BF16),
+            pltpu.VMEM(to_wave.shape, BF16),
+            pltpu.SemaphoreType.DMA((7,)),
         ],
         compiler_params=pltpu.CompilerParams(vmem_limit_bytes=12 << 20),
         name="upward",
     )(
-        point_counts, octants, frequencies, jnp.transpose(positions, (1, 0, 2)), charges,
-        arrived_charges, child_shift, to_wave,
+        *in_hbm(
+            point_counts, octants, frequencies, jnp.transpose(positions, (1, 0, 2)), charges,
+            child_shift, to_wave,
+        ),
+        arrived_charges,
     )
     arrived_waves = swap_cores(waves)
     rows, *sent = pl.pallas_call(
@@ -402,7 +475,7 @@
         out_specs=[VMEM] * (1 + near),
         compiler_params=pltpu.CompilerParams(vmem_limit_bytes=12 << 20),
         name="pack",
-    )(send_leaf[0], send_parent[0], waves, arrived_waves)
+    )(leaf_ids, parent_ids, waves, arrived_waves)
     def slot_permutation(k):
         pairs = []
         for core, offset in ((0, k - near), (1, k + 1)):
@@ -413,32 +486,54 @@
         lax.ppermute(part, ("space", "rhs"), slot_permutation(k)) for k, part in enumerate(sent)
     ]
     index_scratch = [
-        pltpu.VMEM((translation.shape[0] * 16, width // 2), F32),
-        pltpu.SMEM((4 * held * 64,), jnp.int32),
-        pltpu.SMEM((4 * held * 64,), jnp.int32),
-        pltpu.SemaphoreType.DMA((held // TARGET_GROUP, 4)),
+        pltpu.SMEM((held * 512,), jnp.int32),
+        pltpu.SemaphoreType.DMA((held // TARGET_GROUP,)),
     ]
-    acc = pl.pallas_call(
-        functools.partial(near_kernel, chunk),
-        out_shape=jax.ShapeDtypeStruct((held, 16, width // 2), F32),
-        in_specs=[SMEM] + [ANY] * 2 + [VMEM] * 2,
+    table_shape = jax.ShapeDtypeStruct((table_rows * 16, width // 2), F32)
+    factor_shape = jax.ShapeDtypeStruct((translation.shape[0] * 16, width // 2), F32)
+
+    def acc_shape(targets):
+        return jax.ShapeDtypeStruct((targets, 16, width // 2), F32)
+
+    def cost(targets):
+        return pl.CostEstimate(
+            flops=targets * 170_000_000, bytes_accessed=targets * 500_000, transcendentals=0
+        )
+
+    table, factor, acc_first = pl.pallas_call(
+        functools.partial(near_kernel, chunk, FIRST_TARGETS),
+        out_shape=[table_shape, factor_shape, acc_shape(FIRST_TARGETS)],
+        in_specs=[SMEM, ANY, VMEM, VMEM],
+        out_specs=[VMEM] * 3,
+        scratch_shapes=index_scratch,
+        cost_estimate=cost(FIRST_TARGETS),
+        compiler_params=pltpu.CompilerParams(vmem_limit_bytes=20 << 20),
+        name="near",
+    )(chunks, indices, rows, factors)
+    *near_own, acc_first = lax.optimization_barrier((*near_own, acc_first))
+    near_recv = [swap_cores(part) for part in near_own]
+    acc_last = pl.pallas_call(
+        functools.partial(more_kernel, chunk, FIRST_TARGETS, held),
+        out_shape=acc_shape(held - FIRST_TARGETS),
+        in_specs=[SMEM, ANY, VMEM, VMEM],
         out_specs=VMEM,
-        scratch_shapes=[pltpu.VMEM((2 * held * 16, width // 2), F32)] + index_scratch,
-        cost_estimate=pl.CostEstimate(flops=25_000_000_000, bytes_accessed=80_000_000, transcendentals=0),
-        compiler_params=pltpu.CompilerParams(vmem_limit_bytes=16 << 20),
-        name="near",
-    )(chunks, source_rows, class_rows, rows, translation)
-    *near_own, acc = lax.optimization_barrier((*near_own, acc))
-    near_recv = [swap_cores(part) for part in near_own]
-    keep, send = pl.pallas_call(
-        functools.partial(rest_kernel, (slots, cap_l, cap_p, chunk, CHUNKS, count)),
-        out_shape=[jax.ShapeDtypeStruct((held, rhs, width), BF16)] * 2,
-        in_specs=[SMEM] + [ANY] * 2 + [VMEM] * (3 + slots),
-        out_specs=[VMEM] * 2,
-        scratch_shapes=[pltpu.VMEM((table_rows * 16, width // 2), F32)] + index_scratch,
-        compiler_params=pltpu.CompilerParams(vmem_limit_bytes=24 << 20),
+        scratch_shapes=index_scratch,
+        cost_estimate=cost(held - FIRST_TARGETS),
+        compiler_params=pltpu.CompilerParams(vmem_limit_bytes=20 << 20),
+        name="more",
+    )(chunks, indices, table, factor)
+    keep, send, _ = pl.pallas_call(
+        functools.partial(
+            rest_kernel, (slots, cap_l, cap_p, 2 * held, chunk, CHUNKS, count)
+        ),
+        out_shape=[jax.ShapeDtypeStruct((held, rhs, width), BF16)] * 2 + [table_shape],
+        in_specs=[SMEM, ANY] + [VMEM] * (4 + slots),
+        out_specs=[VMEM] * 3,
+        scratch_shapes=index_scratch,
+        input_output_aliases={2: 2},
+        compiler_params=pltpu.CompilerParams(vmem_limit_bytes=20 << 20),
         name="rest",
-    )(chunks, source_rows, class_rows, rows, *near_own, *near_recv, translation, acc)
+    )(chunks, indices, table, factor, *near_own, *near_recv, acc_first, acc_last)
     arrived = swap_cores(send)
     return tuple(
         pl.pallas_call(

time: 84.9 us -> 80.9 us (0.953)
  local copies, waits for them, and re-layouts: 8.91 us -> 0.01 us
  Pallas kernels: 58.9 us -> 65.6 us
  waiting for transfers between devices: 4.95 us -> 3.47 us
    unnamed x26 -> x2, local copies, waits for them, and re-layouts: 7.96 us -> 0.01 us
    pallas_call x2 -> x3, Pallas kernels: 44.4 us -> 49.6 us  [the longest x1 23.7 us: shards(): pl.pallas_call(functools.partial(near_kernel, chunk, FIRST_TARGETS), out_...]
    ppermute x7, waiting for transfers between devices: 4.94 us -> 3.46 us  [swap_cores(): return lax.ppermute(value, 'rhs', [(0, 1), (1, 0)])]
    dynamic_slice x1 -> x0, local copies, waits for them, and re-layouts: 0.95 us -> none  [shards(): lax.dynamic_slice_in_dim(charges, other * leaves, leaves, 0)]
    pallas_call x1, Pallas kernels: 1.49 us -> 2.42 us  [shards(): pl.pallas_call(functools.partial(plan_kernel, 2 * held, chunk), out_shape...]
  transfers between devices with their start and end apart: 11 -> 11, of which waited for: 6 -> 2; matrix products, arithmetic and copies ran while one was open for 0% -> 0% of each run, Pallas kernels for 35% -> 42%
where the time goes in v4:
time: 80.9 us; the launch traced here: 80.7 us
  Pallas kernels  65.6 us (81%)
  starting transfers between devices  10.9 us (13%)
  waiting for transfers between devices  3.47 us (4%)
    pallas_call x1, Pallas kernels, shards(): pl.pallas_call(functools.partial(near_kernel, chunk, FIRST_TARGETS), out_...  23.7 us
    pallas_call x1, Pallas kernels, shards(): pl.pallas_call(functools.partial(rest_kernel, (slots, cap_l, cap_p, 2 * h...  17.9 us
    pallas_call x1, Pallas kernels, shards(): pl.pallas_call(upward_kernel, out_shape=jax.ShapeDtypeStruct((held, 2 * r...  11.3 us
    ppermute x4, starting transfers between devices, shards(): lax.ppermute(part, ('space', 'rhs'), slot_permutation(k))  9 us
    pallas_call x1, Pallas kernels, shards(): pl.pallas_call(functools.partial(more_kernel, chunk, FIRST_TARGETS, held)...  7.99 us
    ppermute x7, waiting for transfers between devices, swap_cores(): return lax.ppermute(value, 'rhs', [(0, 1), (1, 0)])  3.46 us
    pallas_call x1, Pallas kernels, shards(): pl.pallas_call(functools.partial(plan_kernel, 2 * held, chunk), out_shape...  2.42 us
    ppermute x7, starting transfers between devices, swap_cores(): return lax.ppermute(value, 'rhs', [(0, 1), (1, 0)])  1.86 us
  transfers between devices with their start and end apart: 11, of which 2 were waited for; matrix products, arithmetic and copies ran while one was open for 0% of the time, Pallas kernels for 42%

profile of v4, /device:TPU:0, one launch (start us, length us, event | category | flops | bytes accessed | tf_op | source)
XLA Modules:
  0.0 80.7 jit_solution(176041613109501672)
XLA Ops:
  0.6 0.5 collective-permute-start
  1.1 2.4 %plan.1 = (s32[576,128]{1,0:T(8,128)S(1)}, s32[1,256]{1,0:T(1,128)S(1)}, s32[8,48]{1,0:T(8,128)S(1)}, s32[8,16]{1,0:T(8,128)S(1)}, f32[316,256]{1,0:T(8,128)S(1)}) custom-call(s32[189,2,256]{2,1,0:T(2,128)} %bitcast.9, s32[32,2,189]{2,1,0:T(2,128)} %parent_hbm.1, s32[8,48]{1,0:T(8,128)} %bitcast.10, s32[8,16]{1,0:T(8,128)} %bitcast.11, f32[316,256]{1,0:T(8,128)} %trans_hbm.1), custom_call_target="tpu_custom_call" | custom-call | tf_op jit(solution)/shard_map/plan/pallas_call | solution.py:414
  3.6 11.3 %upward.1.own_ref = bf16[144,8,256]{2,1,0:T(8,128)(2,1)S(1)} custom-call(s32[256]{0:T(256)} %counts_hbm.1, s32[256]{0:T(256)} %octants_hbm.1, f32[3,128]{1,0:T(4,128)} %freq_hbm.1, f32[3,256,128]{2,1,0:T(8,128)} %bitcast.8, bf16[256,4,128]{2,1,0:T(4,128)(2,1)} %own_hbm.1, bf16[8,256,256]{2,1,0:T(8,128)(2,1)} %shift_hbm.1, bf16[256,256]{1,0:T(8,128)(2,1)} %wave_mat_hbm.1, ...), custom_call_target="tpu_custom_call" | custom-call | tf_op jit(solution)/shard_map/upward/pallas_call | solution.py:442
  14.9 0.1 collective-permute-start.1
  15.0 1.9 %collective-permute-done.1.recv_ref = bf16[144,8,256]{2,1,0:T(8,128)(2,1)S(1)} collective-permute-done((bf16[144,8,256]{2,1,0:T(8,128)(2,1)S(1)}, bf16[144,8,256]{2,1,0:T(8,128)(2,1)S(1)}, u32[]{:S(2)}, u32[]{:S(2)}) %collective-permute-start.1) | collective-permute-done | bytes 589856 | tf_op jit(solution)/shard_map/ppermute | solution.py:38
  16.9 1.0 %pack.1 = (bf16[288,8,256]{2,1,0:T(8,128)(2,1)S(1)}, bf16[64,8,256]{2,1,0:T(8,128)(2,1)S(1)}, bf16[64,8,256]{2,1,0:T(8,128)(2,1)S(1)}, bf16[64,8,256]{2,1,0:T(8,128)(2,1)S(1)}, bf16[64,8,256]{2,1,0:T(8,128)(2,1)S(1)}) custom-call(s32[8,48]{1,0:T(8,128)S(1)} %get-tuple-element.35.leaf_ids_ref, s32[8,16]{1,0:T(8,128)S(1)} %get-tuple-element.36.parent_ids_ref, ...), custom_call_target="tpu_custom_call" | custom-call | tf_op jit(solution)/shard_map/pack/pallas_call | solution.py:470
  17.9 4.8 %collective-permute-start.2 = (bf16[64,8,256]{2,1,0:T(8,128)(2,1)S(1)}, bf16[64,8,256]{2,1,0:T(8,128)(2,1)S(1)}, u32[]{:S(2)}, u32[]{:S(2)}) collective-permute-start(bf16[64,8,256]{2,1,0:T(8,128)(2,1)S(1)} %get-tuple-element.42), channel_id=1, source_target_pairs={{0,24},{2,26},{4,28},{6,30},{8,0},{10,2},{12,4},{14,6},{16,8},{18,... | collective-permute-start | bytes 786440 | tf_op jit(solution)/shard_map/ppermute | solution.py:486
  22.7 1.4 %collective-permute-start.3 = (bf16[64,8,256]{2,1,0:T(8,128)(2,1)S(1)}, bf16[64,8,256]{2,1,0:T(8,128)(2,1)S(1)}, u32[]{:S(2)}, u32[]{:S(2)}) collective-permute-start(bf16[64,8,256]{2,1,0:T(8,128)(2,1)S(1)} %get-tuple-element.43), channel_id=1, source_target_pairs={{0,26},{2,28},{4,30},{6,0},{8,2},{10,4},{12,6},{14,8},{16,10},{18,... | collective-permute-start | bytes 786440 | tf_op jit(solution)/shard_map/ppermute | solution.py:486
  24.1 1.4 %collective-permute-start.4 = (bf16[64,8,256]{2,1,0:T(8,128)(2,1)S(1)}, bf16[64,8,256]{2,1,0:T(8,128)(2,1)S(1)}, u32[]{:S(2)}, u32[]{:S(2)}) collective-permute-start(bf16[64,8,256]{2,1,0:T(8,128)(2,1)S(1)} %get-tuple-element.44), channel_id=1, source_target_pairs={{0,28},{2,30},{4,0},{6,2},{8,4},{10,6},{12,8},{14,10},{16,12},{18,... | collective-permute-start | bytes 786440 | tf_op jit(solution)/shard_map/ppermute | solution.py:486
  25.5 1.4 %collective-permute-start.5 = (bf16[64,8,256]{2,1,0:T(8,128)(2,1)S(1)}, bf16[64,8,256]{2,1,0:T(8,128)(2,1)S(1)}, u32[]{:S(2)}, u32[]{:S(2)}) collective-permute-start(bf16[64,8,256]{2,1,0:T(8,128)(2,1)S(1)} %get-tuple-element.45), channel_id=1, source_target_pairs={{0,30},{2,0},{4,2},{6,4},{8,6},{10,8},{12,10},{14,12},{16,14},{18,... | collective-permute-start | bytes 786440 | tf_op jit(solution)/shard_map/ppermute | solution.py:486
  26.9 23.7 %near.1 = (f32[12800,128]{1,0:T(8,128)S(1)}, f32[5056,128]{1,0:T(8,128)S(1)}, f32[112,16,128]{2,1,0:T(8,128)S(1)}) custom-call(s32[1,256]{1,0:T(1,128)S(1)} %get-tuple-element.33.chunks_ref, s32[73728]{0:T(1024)S(1)} %bitcast.5, bf16[288,8,256]{2,1,0:T(8,128)(2,1)S(1)} %get-tuple-element.38.rows_ref, f32[316,256]{1,0:T(8,128)S(1)} %get-tuple-element.39.trans_ref), custom_call_target="tpu_custom_call" | custom-call | flops 19040000000 | bytes 56000000 | tf_op jit(solution)/shard_map/near/pallas_call | solution.py:503
  50.7 0.0 collective-permute-done.2.refs_0_
  50.7 0.0 collective-permute-done.4.refs_2_
  50.7 0.0 collective-permute-done.5.refs_3_
  50.7 0.1 collective-permute-start.6
  50.8 0.5 collective-permute-start.7
  51.3 0.1 collective-permute-start.8
  51.4 0.4 collective-permute-start.9
  51.8 8.0 %more.1.refs_9_ = f32[32,16,128]{2,1,0:T(8,128)S(1)} custom-call(s32[1,256]{1,0:T(1,128)S(1)} %get-tuple-element.33.chunks_ref, s32[73728]{0:T(1024)S(1)} %bitcast.6, f32[12800,128]{1,0:T(8,128)S(1)} %get-tuple-element.40.table.table_in, f32[5056,128]{1,0:T(8,128)S(1)} %get-tuple-element.41.factor), custom_call_target="tpu_custom_call" | custom-call | flops 5440000000 | bytes 16000000 | tf_op jit(solution)/shard_map/more/pallas_call | solution.py:515
  59.8 0.0 copy-start
  59.8 17.9 %rest.1 = (bf16[144,4,256]{2,1,0:T(4,128)(2,1)S(1)}, bf16[144,4,256]{2,1,0:T(4,128)(2,1)S(1)}, f32[12800,128]{1,0:T(8,128)S(1)}) custom-call(s32[1,256]{1,0:T(1,128)S(1)} %get-tuple-element.33.chunks_ref, s32[73728]{0:T(1024)S(1)} %bitcast.7, f32[12800,128]{1,0:T(8,128)S(1)} %get-tuple-element.40.table.table_in, ...), custom_call_target="tpu_custom_call", output_to_operand_aliasing={{2}: (2, {})} | custom-call | tf_op jit(solution)/shard_map/rest/pallas_call | solution.py:525
  77.7 0.1 collective-permute-start.10
  77.9 1.5 %collective-permute-done.10.recv_ref = bf16[144,4,256]{2,1,0:T(4,128)(2,1)S(1)} collective-permute-done((bf16[144,4,256]{2,1,0:T(4,128)(2,1)S(1)}, bf16[144,4,256]{2,1,0:T(4,128)(2,1)S(1)}, u32[]{:S(2)}, u32[]{:S(2)}) %collective-permute-start.10) | collective-permute-done | bytes 294944 | tf_op jit(solution)/shard_map/ppermute | solution.py:38
  79.4 1.3 %local.1 = (f32[256,4,256]{2,1,0:T(4,128)}, f32[32,4,256]{2,1,0:T(4,128)}) custom-call(bf16[144,4,256]{2,1,0:T(4,128)(2,1)S(1)} %get-tuple-element.52.keep_ref, bf16[144,4,256]{2,1,0:T(4,128)(2,1)S(1)} %collective-permute-done.10.recv_ref, bf16[256,256]{1,0:T(8,128)(2,1)S(1)} %copy-done), custom_call_target="tpu_custom_call" | custom-call | tf_op jit(solution)/shard_map/local/pallas_call | solution.py:539
  (7 shorter events, 0.0 us)
Async XLA Ops:
  0.6 3.0 %collective-permute-start = (bf16[256,4,128]{2,1,0:T(4,128)(2,1)}, bf16[256,4,128]{2,1,0:T(4,128)(2,1)S(1)}, u32[]{:S(2)}, u32[]{:S(2)}) collective-permute-start(bf16[256,4,128]{2,1,0:T(4,128)(2,1)} %own_hbm.1), channel_id=1, source_target_pairs={{0,1},{1,0},{2,3},{3,2},{4,5},{5,4},{6,7},{7,6},{8,9},{9,8},{10,11... | collective-permute-start | bytes 786440 | tf_op jit(solution)/shard_map/ppermute | solution.py:38
  14.9 2.1 %collective-permute-start.1 = (bf16[144,8,256]{2,1,0:T(8,128)(2,1)S(1)}, bf16[144,8,256]{2,1,0:T(8,128)(2,1)S(1)}, u32[]{:S(2)}, u32[]{:S(2)}) collective-permute-start(bf16[144,8,256]{2,1,0:T(8,128)(2,1)S(1)} %upward.1.own_ref), channel_id=1, source_target_pairs={{0,1},{1,0},{2,3},{3,2},{4,5},{5,4},{6,7},{7,6},{8,9},{9,8},{10,11... | collective-permute-start | bytes 1769480 | tf_op jit(solution)/shard_map/ppermute | solution.py:38
  17.9 32.8 %collective-permute-start.2 = (bf16[64,8,256]{2,1,0:T(8,128)(2,1)S(1)}, bf16[64,8,256]{2,1,0:T(8,128)(2,1)S(1)}, u32[]{:S(2)}, u32[]{:S(2)}) collective-permute-start(bf16[64,8,256]{2,1,0:T(8,128)(2,1)S(1)} %get-tuple-element.42), channel_id=1, source_target_pairs={{0,24},{2,26},{4,28},{6,30},{8,0},{10,2},{12,4},{14,6},{16,8},{18,... | collective-permute-start | bytes 786440 | tf_op jit(solution)/shard_map/ppermute | solution.py:486
  22.7 28.0 %collective-permute-start.3 = (bf16[64,8,256]{2,1,0:T(8,128)(2,1)S(1)}, bf16[64,8,256]{2,1,0:T(8,128)(2,1)S(1)}, u32[]{:S(2)}, u32[]{:S(2)}) collective-permute-start(bf16[64,8,256]{2,1,0:T(8,128)(2,1)S(1)} %get-tuple-element.43), channel_id=1, source_target_pairs={{0,26},{2,28},{4,30},{6,0},{8,2},{10,4},{12,6},{14,8},{16,10},{18,... | collective-permute-start | bytes 786440 | tf_op jit(solution)/shard_map/ppermute | solution.py:486
  24.1 26.6 %collective-permute-start.4 = (bf16[64,8,256]{2,1,0:T(8,128)(2,1)S(1)}, bf16[64,8,256]{2,1,0:T(8,128)(2,1)S(1)}, u32[]{:S(2)}, u32[]{:S(2)}) collective-permute-start(bf16[64,8,256]{2,1,0:T(8,128)(2,1)S(1)} %get-tuple-element.44), channel_id=1, source_target_pairs={{0,28},{2,30},{4,0},{6,2},{8,4},{10,6},{12,8},{14,10},{16,12},{18,... | collective-permute-start | bytes 786440 | tf_op jit(solution)/shard_map/ppermute | solution.py:486
  25.5 25.2 %collective-permute-start.5 = (bf16[64,8,256]{2,1,0:T(8,128)(2,1)S(1)}, bf16[64,8,256]{2,1,0:T(8,128)(2,1)S(1)}, u32[]{:S(2)}, u32[]{:S(2)}) collective-permute-start(bf16[64,8,256]{2,1,0:T(8,128)(2,1)S(1)} %get-tuple-element.45), channel_id=1, source_target_pairs={{0,30},{2,0},{4,2},{6,4},{8,6},{10,8},{12,10},{14,12},{16,14},{18,... | collective-permute-start | bytes 786440 | tf_op jit(solution)/shard_map/ppermute | solution.py:486
  50.7 9.1 %collective-permute-start.6 = (bf16[64,8,256]{2,1,0:T(8,128)(2,1)S(1)}, bf16[64,8,256]{2,1,0:T(8,128)(2,1)S(1)}, u32[]{:S(2)}, u32[]{:S(2)}) collective-permute-start(bf16[64,8,256]{2,1,0:T(8,128)(2,1)S(1)} %collective-permute-done.2.refs_0_), channel_id=1, source_target_pairs={{0,1},{1,0},{2,3},{3,2},{4,5},{5,4},{6,7},{7,6},{8,9},{9,8},{10,11... | collective-permute-start | bytes 786440 | tf_op jit(solution)/shard_map/ppermute | solution.py:38
  50.8 9.0 %collective-permute-start.7 = (bf16[64,8,256]{2,1,0:T(8,128)(2,1)S(1)}, bf16[64,8,256]{2,1,0:T(8,128)(2,1)S(1)}, u32[]{:S(2)}, u32[]{:S(2)}) collective-permute-start(bf16[64,8,256]{2,1,0:T(8,128)(2,1)S(1)} %collective-permute-done.3.refs_1_), channel_id=1, source_target_pairs={{0,1},{1,0},{2,3},{3,2},{4,5},{5,4},{6,7},{7,6},{8,9},{9,8},{10,11... | collective-permute-start | bytes 786440 | tf_op jit(solution)/shard_map/ppermute | solution.py:38
  51.3 8.5 %collective-permute-start.8 = (bf16[64,8,256]{2,1,0:T(8,128)(2,1)S(1)}, bf16[64,8,256]{2,1,0:T(8,128)(2,1)S(1)}, u32[]{:S(2)}, u32[]{:S(2)}) collective-permute-start(bf16[64,8,256]{2,1,0:T(8,128)(2,1)S(1)} %collective-permute-done.4.refs_2_), channel_id=1, source_target_pairs={{0,1},{1,0},{2,3},{3,2},{4,5},{5,4},{6,7},{7,6},{8,9},{9,8},{10,11... | collective-permute-start | bytes 786440 | tf_op jit(solution)/shard_map/ppermute | solution.py:38
  51.4 8.5 %collective-permute-start.9 = (bf16[64,8,256]{2,1,0:T(8,128)(2,1)S(1)}, bf16[64,8,256]{2,1,0:T(8,128)(2,1)S(1)}, u32[]{:S(2)}, u32[]{:S(2)}) collective-permute-start(bf16[64,8,256]{2,1,0:T(8,128)(2,1)S(1)} %collective-permute-done.5.refs_3_), channel_id=1, source_target_pairs={{0,1},{1,0},{2,3},{3,2},{4,5},{5,4},{6,7},{7,6},{8,9},{9,8},{10,11... | collective-permute-start | bytes 786440 | tf_op jit(solution)/shard_map/ppermute | solution.py:38
  59.8 19.6 %copy-start = (bf16[256,256]{1,0:T(8,128)(2,1)S(1)}, bf16[256,256]{1,0:T(8,128)(2,1)}, u32[]{:S(2)}) copy-start(bf16[256,256]{1,0:T(8,128)(2,1)} %mat_ref.1) | copy-start | bytes 393220
  77.7 1.6 %collective-permute-start.10 = (bf16[144,4,256]{2,1,0:T(4,128)(2,1)S(1)}, bf16[144,4,256]{2,1,0:T(4,128)(2,1)S(1)}, u32[]{:S(2)}, u32[]{:S(2)}) collective-permute-start(bf16[144,4,256]{2,1,0:T(4,128)(2,1)S(1)} %get-tuple-element.53), channel_id=1, source_target_pairs={{0,1},{1,0},{2,3},{3,2},{4,5},{5,4},{6,7},{7,6},{8,9},{9,8},{10,11... | collective-permute-start | bytes 884744 | tf_op jit(solution)/shard_map/ppermute | solution.py:38

commit v5 on v4

--- a/solution.py
+++ b/solution.py
@@ -10,11 +10,9 @@
 
 F32 = jnp.float32
 BF16 = jnp.bfloat16
-CHUNKS = 3
 GROUP = 9
-LEAF_UNROLL = 8
+LEAF_UNROLL = 2
 TARGET_GROUP = 16
-FIRST_TARGETS = 112
 SIN_POLY = (4.44286790342698, -7.307443431653506, 3.594788153158899, -0.7843741906863176)
 COS_POLY = (
     1.4142134967586113,
@@ -63,7 +61,7 @@
 
 def upward_kernel(
     counts_hbm, octants_hbm, freq_hbm, pos_hbm, own_hbm, shift_hbm, wave_mat_hbm, recv_ref,
-    out_ref, freq_scr, mult_scr, child_scr,
+    out_ref, freq_scr, mult_scr, child_scr, basis_scr,
     counts_ref, octants_ref, freq_ref, pos_ref, own_ref, shift_ref, wave_mat_ref, sems,
 ):
     core = lax.axis_index("rhs")
@@ -90,28 +88,40 @@
         freq_scr[d] = jnp.broadcast_to(row, (slots, nodes)).T
     lane = lax.broadcasted_iota(jnp.int32, (2 * rhs_half, slots), 1)
 
-    def one_leaf(b):
+    def put_basis(b):
+        xs = [jnp.broadcast_to(pos_ref[d, pl.ds(b, 1), :], (nodes, slots)) for d in range(3)]
+        turns = freq_scr[0] * xs[0] + freq_scr[1] * xs[1] + freq_scr[2] * xs[2]
+        sin, cos = sin_cos_turns(turns)
+        basis_scr[b % (2 * LEAF_UNROLL), :nodes] = cos.astype(BF16)
+        basis_scr[b % (2 * LEAF_UNROLL), nodes:] = sin.astype(BF16)
+
+    def put_multipole(b):
         own, recv = own_ref[b].astype(F32), recv_ref[base + b].astype(F32)
         lower = jnp.where(core == 0, own, recv)
         upper = jnp.where(core == 0, recv, own)
         charge = jnp.concatenate([lower, upper], axis=0)
         charge = jnp.where(lane < counts_ref[base + b], charge, 0.0).astype(BF16)
-        xs = [jnp.broadcast_to(pos_ref[d, pl.ds(b, 1), :], (nodes, slots)) for d in range(3)]
-        turns = freq_scr[0] * xs[0] + freq_scr[1] * xs[1] + freq_scr[2] * xs[2]
-        sin, cos = sin_cos_turns(turns)
-        basis = jnp.concatenate([cos.astype(BF16), sin.astype(BF16)], axis=0)
         multipole = lax.dot_general(
-            charge, basis, (((1,), (1,)), ((), ())), preferred_element_type=F32
+            charge,
+            basis_scr[b % (2 * LEAF_UNROLL)],
+            (((1,), (1,)), ((), ())),
+            preferred_element_type=F32,
         ).astype(BF16)
         mult_scr[b] = multipole
         child_scr[octants_ref[base + b], b // 8] = multipole
 
     def step(g, carry):
         for k in range(LEAF_UNROLL):
-            one_leaf(g * LEAF_UNROLL + k)
+            put_multipole((g - 1) * LEAF_UNROLL + k)
+        for k in range(LEAF_UNROLL):
+            put_basis(g * LEAF_UNROLL + k)
         return carry
 
-    lax.fori_loop(0, leaves // LEAF_UNROLL, step, 0)
+    for k in range(LEAF_UNROLL):
+        put_basis(k)
+    lax.fori_loop(1, leaves // LEAF_UNROLL, step, 0)
+    for k in range(LEAF_UNROLL):
+        put_multipole(leaves - LEAF_UNROLL + k)
     for copy in copies[5:]:
         copy.wait()
     parents = leaves // 8
@@ -133,8 +143,8 @@
 
 
 def plan_kernel(
-    local_rows, chunk, leaf_hbm, parent_hbm, send_leaf_hbm, send_parent_hbm, trans_hbm,
-    index_out, chunks_out, send_leaf_out, send_parent_out, trans_out, leaf_ref, parent_ref, sems,
+    local_rows, split, leaf_hbm, parent_hbm, send_leaf_hbm, send_parent_hbm, trans_hbm,
+    first_out, second_out, send_leaf_out, send_parent_out, trans_out, leaf_ref, parent_ref, sems,
 ):
     core = lax.axis_index("rhs")
     list_len, _, leaves = leaf_ref.shape
@@ -192,12 +202,12 @@
     words = front + back
     sources = (words & 1023) * 16
     classes = (lax.shift_right_logical(words, 10) & 1023) * 16
+    ready = (total >= split).astype(jnp.int32)
     for h, values in enumerate((sources, classes)):
-        index_out[pl.ds(h, targets, stride=4), :] = values[:128].T[:targets]
-        tail = pltpu.roll(values, depth - 2 * chunk, 0)[:128].T[:targets]
-        index_out[pl.ds(2 + h, targets, stride=4), :] = tail
-    full = [(total >= n * chunk).astype(jnp.int32) for n in range(1, list_len // chunk + 1)]
-    chunks_out[...] = tree(full)
+        head = jnp.where(row[:128] == 127, ready, values[:128])
+        tail = jnp.where(row[:128] == 127, ready, pltpu.roll(values, depth - split, 0)[:128])
+        first_out[pl.ds(h, targets, stride=2), :] = head.T[:targets]
+        second_out[pl.ds(h, targets, stride=2), :] = tail.T[:targets]
     for copy in copies[2:]:
         copy.wait()
 
@@ -256,39 +266,40 @@
         put_factors(full, trans_ref[full:, :])
 
 
-def pair_sums(index_ref, table, factor, chunk):
-    def accumulate(b, c, total):
-        total_re, total_im = total
-        first = b * 512 + jnp.where(c == 2, 256, c * chunk)
-        reals, imags = [], []
-        for k in range(chunk):
-            if k % GROUP == 0:
-                span = min(GROUP, chunk - k)
-                sources = index_ref.at[pl.ds(first + k, span)]
-                classes = index_ref.at[pl.ds(first + 128 + k, span)]
-            s = pl.multiple_of(sources[k % GROUP], 8)
-            o = pl.multiple_of(classes[k % GROUP], 8)
-            wave, shift = table.at[pl.ds(s, 16)], factor.at[pl.ds(o, 16)]
-            wave_re, wave_im, shift_re, shift_im = wave[:8], wave[8:], shift[:8], shift[8:]
-            reals.append(shift_re * wave_re - shift_im * wave_im)
-            imags.append(shift_re * wave_im + shift_im * wave_re)
-            if len(reals) == 3 or k == chunk - 1:
-                total_re, total_im = total_re + tree(reals), total_im + tree(imags)
-                reals, imags = [], []
-        return total_re, total_im
-
-    return accumulate
+def pair_sums(index_ref, first, count, table, factor, total):
+    total_re, total_im = total
+    reals, imags = [], []
+    for k in range(count):
+        if k % GROUP == 0:
+            span = min(GROUP, count - k)
+            sources = index_ref.at[pl.ds(first + k, span)]
+            classes = index_ref.at[pl.ds(first + 128 + k, span)]
+        s = pl.multiple_of(sources[k % GROUP], 8)
+        o = pl.multiple_of(classes[k % GROUP], 8)
+        wave, shift = table.at[pl.ds(s, 16)], factor.at[pl.ds(o, 16)]
+        wave_re, wave_im, shift_re, shift_im = wave[:8], wave[8:], shift[:8], shift[8:]
+        reals.append(shift_re * wave_re - shift_im * wave_im)
+        imags.append(shift_re * wave_im + shift_im * wave_re)
+        if len(reals) == 3 or k == count - 1:
+            total_re, total_im = total_re + tree(reals), total_im + tree(imags)
+            reals, imags = [], []
+    return total_re, total_im
 
 
 def index_copy(index_hbm, index_scr, sems, group):
-    words = TARGET_GROUP * 512
+    words = TARGET_GROUP * 256
     span = pl.ds(pl.multiple_of(group * words, 1024), words)
     return pltpu.make_async_copy(index_hbm.at[span], index_scr.at[span], sems.at[group])
 
 
-def over_targets(index, first, last, one_target):
+def start_indices(index):
+    for group in range(2):
+        index_copy(*index, group).start()
+
+
+def over_targets(index, targets, one_target):
     def one_group(g, carry):
-        @pl.when(g + 2 < last // TARGET_GROUP)
+        @pl.when(g + 2 < targets // TARGET_GROUP)
         def _():
             index_copy(*index, g + 2).start()
 
@@ -297,58 +308,37 @@
             0, TARGET_GROUP, lambda t, c: one_target(g * TARGET_GROUP + t, c), carry
         )
 
-    lax.fori_loop(first // TARGET_GROUP, last // TARGET_GROUP, one_group, 0)
-
-
-def start_indices(index, first, last):
-    for group in range(first // TARGET_GROUP, min(first // TARGET_GROUP + 2, last // TARGET_GROUP)):
-        index_copy(*index, group).start()
-
-
-def near_targets(index, first, last, chunks_ref, table, factor, chunk, acc_ref):
-    accumulate = pair_sums(index[1], table, factor, chunk)
-
-    def one_target(b, carry):
-        zero = jnp.zeros((8, table.shape[1]), F32)
-        total = lax.fori_loop(
-            0, jnp.minimum(chunks_ref[0, b], 2), lambda c, t: accumulate(b, c, t), (zero, zero)
-        )
-        acc_ref[b - first, :8] = total[0]
-        acc_ref[b - first, 8:] = total[1]
-        return carry
-
-    over_targets(index, first, last, one_target)
-
-
-def near_kernel(
-    chunk, last, chunks_ref, index_hbm, rows_ref, trans_ref, table, factor, acc_ref, index_scr, sems
-):
+    lax.fori_loop(0, targets // TARGET_GROUP, one_group, 0)
+
+
+def near_kernel(split, index_hbm, rows_ref, trans_ref, table, factor, acc_ref, index_scr, sems):
     index = (index_hbm, index_scr, sems)
-    start_indices(index, 0, last)
+    start_indices(index)
     put_rows(table, rows_ref, 0, rows_ref.shape[0], 0)
     put_all_factors(factor, trans_ref)
-    near_targets(index, 0, last, chunks_ref, table, factor, chunk, acc_ref)
-
-
-def more_kernel(
-    chunk, first, last, chunks_ref, index_hbm, table, factor, acc_ref, index_scr, sems
-):
-    index = (index_hbm, index_scr, sems)
-    start_indices(index, first, last)
-    near_targets(index, first, last, chunks_ref, table, factor, chunk, acc_ref)
-
-
-def rest_kernel(dims, chunks_ref, index_hbm, table_in, factor, *refs):
-    slots, cap_l, cap_p, base, chunk, chunk_count, count = dims
+    zero = jnp.zeros((8, table.shape[1]), F32)
+
+    def one_target(b, carry):
+        @pl.when(index_scr[b * 256 + 127] > 0)
+        def _():
+            total = pair_sums(index_scr, b * 256, split, table, factor, (zero, zero))
+            acc_ref[b, :8] = total[0]
+            acc_ref[b, 8:] = total[1]
+
+        return carry
+
+    over_targets(index, acc_ref.shape[0], one_target)
+
+
+def rest_kernel(dims, first_hbm, second_hbm, table_in, factor, *refs):
+    slots, cap_l, cap_p, base, split, list_len, count = dims
     near = slots // 2
     near_own, near_recv = refs[:near], refs[near:slots]
-    acc_refs = refs[slots : slots + 2]
-    keep_ref, send_ref, table, index_scr, sems = refs[slots + 2 :]
+    acc_ref, keep_ref, send_ref, table, index_scr, late_scr, sems, late_sem = refs[slots + 1 :]
     core = lax.axis_index("rhs")
     device = lax.axis_index("space")
-    targets = keep_ref.shape[0]
-    index = (index_hbm, index_scr, sems)
-    start_indices(index, 0, targets)
+    index = (second_hbm, index_scr, sems)
+    start_indices(index)
     for k in range(near):
         for values, which in ((near_own[k], core), (near_recv[k], 1 - core)):
             slot = which * near + k
@@ -356,28 +346,29 @@
             valid = (sender >= 0) & (sender < count)
             put_rows(table, values, 0, cap_l, base + slot * cap_l, valid)
             put_rows(table, values, cap_l, cap_p, base + slots * cap_l + slot * cap_p, valid)
-    accumulate = pair_sums(index_scr, table, factor, chunk)
-    first = 0
-    for acc_ref in acc_refs:
-
-        def one_target(b, carry, acc_ref=acc_ref, first=first):
-            total = lax.fori_loop(
-                jnp.minimum(chunks_ref[0, b], 2),
-                chunk_count,
-                lambda c, t: accumulate(b, c, t),
-                (acc_ref[b - first, :8], acc_ref[b - first, 8:]),
-            )
-            incoming = jnp.concatenate(total, axis=1)
-            lower, upper = incoming[:4], incoming[4:]
-            keep_ref[b] = jnp.where(core == 0, lower, upper).astype(BF16)
-            send_ref[b] = jnp.where(core == 0, upper, lower).astype(BF16)
-            return carry
-
-        last = first + acc_ref.shape[0]
-        if first:
-            start_indices(index, first, last)
-        over_targets(index, first, last, one_target)
-        first = last
+    zero = jnp.zeros((8, table.shape[1]), F32)
+
+    def one_target(b, carry):
+        @pl.when(index_scr[b * 256 + 127] == 0)
+        def _():
+            span = pl.ds(pl.multiple_of(b * 256, 256), 256)
+            copy = pltpu.make_async_copy(first_hbm.at[span], late_scr, late_sem)
+            copy.start()
+            copy.wait()
+            total = pair_sums(late_scr, 0, split, table, factor, (zero, zero))
+            acc_ref[b, :8] = total[0]
+            acc_ref[b, 8:] = total[1]
+
+        total = pair_sums(
+            index_scr, b * 256, list_len - split, table, factor, (acc_ref[b, :8], acc_ref[b, 8:])
+        )
+        incoming = jnp.concatenate(total, axis=1)
+        lower, upper = incoming[:4], incoming[4:]
+        keep_ref[b] = jnp.where(core == 0, lower, upper).astype(BF16)
+        send_ref[b] = jnp.where(core == 0, upper, lower).astype(BF16)
+        return carry
+
+    over_targets(index, keep_ref.shape[0], one_target)
 
 
 def local_kernel(leaves, keep_ref, recv_ref, mat_ref, leaf_ref, parent_ref):
@@ -406,16 +397,17 @@
     near = slots // 2
     held = leaves + parents
     list_len = leaf_pairs.shape[2]
-    chunk = list_len // CHUNKS
+    split = list_len // 2
     cap_l, cap_p = send_leaf.shape[2], send_parent.shape[2]
     table_rows = 2 * held + slots * (cap_l + cap_p)
 
     arrived_charges = swap_cores(charges)
-    indices, chunks, leaf_ids, parent_ids, factors = pl.pallas_call(
-        functools.partial(plan_kernel, 2 * held, chunk),
+    index_shape = jax.ShapeDtypeStruct((2 * held, 128), jnp.int32)
+    first, second, leaf_ids, parent_ids, factors = pl.pallas_call(
+        functools.partial(plan_kernel, 2 * held, split),
         out_shape=[
-            jax.ShapeDtypeStruct((4 * held, 128), jnp.int32),
-            jax.ShapeDtypeStruct((1, 256), jnp.int32),
+            index_shape,
+            index_shape,
             jax.ShapeDtypeStruct(send_leaf.shape[1:], jnp.int32),
             jax.ShapeDtypeStruct(send_parent.shape[1:], jnp.int32),
             jax.ShapeDtypeStruct(translation.shape, F32),
@@ -435,10 +427,10 @@
             translation,
         )
     )
-    arrived_charges, indices, chunks, leaf_ids, parent_ids, factors = lax.optimization_barrier(
-        (arrived_charges, indices, chunks, leaf_ids, parent_ids, factors)
-    )
-    indices = indices.reshape(-1)
+    arrived_charges, first, second, leaf_ids, parent_ids, factors = lax.optimization_barrier(
+        (arrived_charges, first, second, leaf_ids, parent_ids, factors)
+    )
+    first, second = first.reshape(-1), second.reshape(-1)
     waves = pl.pallas_call(
         upward_kernel,
         out_shape=jax.ShapeDtypeStruct((held, 2 * rhs, width), BF16),
@@ -448,6 +440,7 @@
             pltpu.VMEM((3, width // 2, positions.shape[2]), F32),
             pltpu.VMEM((leaves, 2 * rhs, width), BF16),
             pltpu.VMEM((8, parents, 2 * rhs, width), BF16),
+            pltpu.VMEM((2 * LEAF_UNROLL, width, positions.shape[2]), BF16),
             pltpu.SMEM(point_counts.shape, jnp.int32),
             pltpu.SMEM(octants.shape, jnp.int32),
             pltpu.VMEM(frequencies.shape, F32),
@@ -485,55 +478,44 @@
     near_own = [
         lax.ppermute(part, ("space", "rhs"), slot_permutation(k)) for k, part in enumerate(sent)
     ]
-    index_scratch = [
-        pltpu.SMEM((held * 512,), jnp.int32),
-        pltpu.SemaphoreType.DMA((held // TARGET_GROUP,)),
-    ]
+    index_scr = pltpu.SMEM((held * 256,), jnp.int32)
+    index_sems = pltpu.SemaphoreType.DMA((held // TARGET_GROUP,))
     table_shape = jax.ShapeDtypeStruct((table_rows * 16, width // 2), F32)
     factor_shape = jax.ShapeDtypeStruct((translation.shape[0] * 16, width // 2), F32)
-
-    def acc_shape(targets):
-        return jax.ShapeDtypeStruct((targets, 16, width // 2), F32)
-
-    def cost(targets):
-        return pl.CostEstimate(
-            flops=targets * 170_000_000, bytes_accessed=targets * 500_000, transcendentals=0
-        )
-
-    table, factor, acc_first = pl.pallas_call(
-        functools.partial(near_kernel, chunk, FIRST_TARGETS),
-        out_shape=[table_shape, factor_shape, acc_shape(FIRST_TARGETS)],
-        in_specs=[SMEM, ANY, VMEM, VMEM],
+    acc_shape = jax.ShapeDtypeStruct((held, 16, width // 2), F32)
+    table, factor, acc = pl.pallas_call(
+        functools.partial(near_kernel, split),
+        out_shape=[table_shape, factor_shape, acc_shape],
+        in_specs=[ANY, VMEM, VMEM],
         out_specs=[VMEM] * 3,
-        scratch_shapes=index_scratch,
-        cost_estimate=cost(FIRST_TARGETS),
+        scratch_shapes=[index_scr, index_sems],
+        cost_estimate=pl.CostEstimate(
+            flops=20_000_000_000, bytes_accessed=60_000_000, transcendentals=0
+        ),
         compiler_params=pltpu.CompilerParams(vmem_limit_bytes=20 << 20),
         name="near",
-    )(chunks, indices, rows, factors)
-    *near_own, acc_first = lax.optimization_barrier((*near_own, acc_first))
+    )(first, rows, factors)
+    *near_own, acc = lax.optimization_barrier((*near_own, acc))
     near_recv = [swap_cores(part) for part in near_own]
-    acc_last = pl.pallas_call(
-        functools.partial(more_kernel, chunk, FIRST_TARGETS, held),
-        out_shape=acc_shape(held - FIRST_TARGETS),
-        in_specs=[SMEM, ANY, VMEM, VMEM],
-        out_specs=VMEM,
-        scratch_shapes=index_scratch,
-        cost_estimate=cost(held - FIRST_TARGETS),
-        compiler_params=pltpu.CompilerParams(vmem_limit_bytes=20 << 20),
-        name="more",
-    )(chunks, indices, table, factor)
-    keep, send, _ = pl.pallas_call(
+    _, keep, send, _ = pl.pallas_call(
         functools.partial(
-            rest_kernel, (slots, cap_l, cap_p, 2 * held, chunk, CHUNKS, count)
+            rest_kernel, (slots, cap_l, cap_p, 2 * held, split, list_len, count)
         ),
-        out_shape=[jax.ShapeDtypeStruct((held, rhs, width), BF16)] * 2 + [table_shape],
-        in_specs=[SMEM, ANY] + [VMEM] * (4 + slots),
-        out_specs=[VMEM] * 3,
-        scratch_shapes=index_scratch,
-        input_output_aliases={2: 2},
+        out_shape=[acc_shape]
+        + [jax.ShapeDtypeStruct((held, rhs, width), BF16)] * 2
+        + [table_shape],
+        in_specs=[ANY] * 2 + [VMEM] * (3 + slots),
+        out_specs=[VMEM] * 4,
+        scratch_shapes=[
+            index_scr,
+            pltpu.SMEM((256,), jnp.int32),
+            index_sems,
+            pltpu.SemaphoreType.DMA,
+        ],
+        input_output_aliases={2: 3, 4 + slots: 0},
         compiler_params=pltpu.CompilerParams(vmem_limit_bytes=20 << 20),
         name="rest",
-    )(chunks, indices, table, factor, *near_own, *near_recv, acc_first, acc_last)
+    )(first, second, table, factor, *near_own, *near_recv, acc)
     arrived = swap_cores(send)
     return tuple(
         pl.pallas_call(

time: 80.9 us -> 80.5 us (level)
  Pallas kernels: 65.6 us -> 63.6 us
  waiting for transfers between devices: 3.47 us -> 5.04 us
    pallas_call x3 -> x2, Pallas kernels: 34.2 us -> 23.1 us  [the longest x1 20.7 us: shards(): pl.pallas_call(functools.partial(near_kernel, split), out_shape=[table_sh...]
    pallas_call x1, Pallas kernels: 11.3 us -> 17.3 us  [shards(): pl.pallas_call(upward_kernel, out_shape=jax.ShapeDtypeStruct((held, 2 * r...]
    pallas_call x1, Pallas kernels: 17.9 us -> 21 us  [shards(): pl.pallas_call(functools.partial(rest_kernel, (slots, cap_l, cap_p, 2 * h...]
    ppermute x7, waiting for transfers between devices: 3.46 us -> 5.03 us  [swap_cores(): return lax.ppermute(value, 'rhs', [(0, 1), (1, 0)])]
  transfers between devices with their start and end apart: 11 -> 11, of which waited for: 2 -> 6; matrix products, arithmetic and copies ran while one was open for 0% -> 0% of each run, Pallas kernels for 42% -> 29%
where the time goes in v5:
time: 80.5 us; the launch traced here: 80.3 us
  Pallas kernels  63.6 us (79%)
  starting transfers between devices  10.9 us (14%)
  waiting for transfers between devices  5.04 us (6%)
    pallas_call x1, Pallas kernels, shards(): pl.pallas_call(functools.partial(rest_kernel, (slots, cap_l, cap_p, 2 * h...  21 us
    pallas_call x1, Pallas kernels, shards(): pl.pallas_call(functools.partial(near_kernel, split), out_shape=[table_sh...  20.7 us
    pallas_call x1, Pallas kernels, shards(): pl.pallas_call(upward_kernel, out_shape=jax.ShapeDtypeStruct((held, 2 * r...  17.3 us
    ppermute x4, starting transfers between devices, shards(): lax.ppermute(part, ('space', 'rhs'), slot_permutation(k))  9 us
    ppermute x7, waiting for transfers between devices, swap_cores(): return lax.ppermute(value, 'rhs', [(0, 1), (1, 0)])  5.03 us
    pallas_call x1, Pallas kernels, shards(): pl.pallas_call(functools.partial(plan_kernel, 2 * held, split), out_shape...  2.41 us
    ppermute x7, starting transfers between devices, swap_cores(): return lax.ppermute(value, 'rhs', [(0, 1), (1, 0)])  1.92 us
  transfers between devices with their start and end apart: 11, of which 6 were waited for; matrix products, arithmetic and copies ran while one was open for 0% of the time, Pallas kernels for 29%

profile of v5, /device:TPU:0, one launch (start us, length us, event | category | flops | bytes accessed | tf_op | source)
XLA Modules:
  0.0 80.3 jit_solution(2622670960672590624)
XLA Ops:
  0.6 0.5 collective-permute-start
  1.1 2.4 %plan.1 = (s32[288,128]{1,0:T(8,128)S(1)}, s32[288,128]{1,0:T(8,128)S(1)}, s32[8,48]{1,0:T(8,128)S(1)}, s32[8,16]{1,0:T(8,128)S(1)}, f32[316,256]{1,0:T(8,128)S(1)}) custom-call(s32[189,2,256]{2,1,0:T(2,128)} %bitcast.10, s32[32,2,189]{2,1,0:T(2,128)} %parent_hbm.1, s32[8,48]{1,0:T(8,128)} %bitcast.11, s32[8,16]{1,0:T(8,128)} %bitcast.12, f32[316,256]{1,0:T(8,128)} %trans_hbm.1), custom_call_target="tpu_custom_call" | custom-call | tf_op jit(solution)/shard_map/plan/pallas_call | solution.py:406
  3.6 17.3 %upward.1.own_ref = bf16[144,8,256]{2,1,0:T(8,128)(2,1)S(1)} custom-call(s32[256]{0:T(256)} %counts_hbm.1, s32[256]{0:T(256)} %octants_hbm.1, f32[3,128]{1,0:T(4,128)} %freq_hbm.1, f32[3,256,128]{2,1,0:T(8,128)} %bitcast.9, bf16[256,4,128]{2,1,0:T(4,128)(2,1)} %own_hbm.1, bf16[8,256,256]{2,1,0:T(8,128)(2,1)} %shift_hbm.1, bf16[256,256]{1,0:T(8,128)(2,1)} %wave_mat_hbm.1, ...), custom_call_target="tpu_custom_call" | custom-call | tf_op jit(solution)/shard_map/upward/pallas_call | solution.py:434
  20.9 0.1 collective-permute-start.1
  21.0 1.9 %collective-permute-done.1.recv_ref = bf16[144,8,256]{2,1,0:T(8,128)(2,1)S(1)} collective-permute-done((bf16[144,8,256]{2,1,0:T(8,128)(2,1)S(1)}, bf16[144,8,256]{2,1,0:T(8,128)(2,1)S(1)}, u32[]{:S(2)}, u32[]{:S(2)}) %collective-permute-start.1) | collective-permute-done | bytes 589856 | tf_op jit(solution)/shard_map/ppermute | solution.py:36
  22.9 1.0 %pack.1 = (bf16[288,8,256]{2,1,0:T(8,128)(2,1)S(1)}, bf16[64,8,256]{2,1,0:T(8,128)(2,1)S(1)}, bf16[64,8,256]{2,1,0:T(8,128)(2,1)S(1)}, bf16[64,8,256]{2,1,0:T(8,128)(2,1)S(1)}, bf16[64,8,256]{2,1,0:T(8,128)(2,1)S(1)}) custom-call(s32[8,48]{1,0:T(8,128)S(1)} %get-tuple-element.35.leaf_ids_ref, s32[8,16]{1,0:T(8,128)S(1)} %get-tuple-element.36.parent_ids_ref, ...), custom_call_target="tpu_custom_call" | custom-call | tf_op jit(solution)/shard_map/pack/pallas_call | solution.py:463
  23.9 4.8 %collective-permute-start.2 = (bf16[64,8,256]{2,1,0:T(8,128)(2,1)S(1)}, bf16[64,8,256]{2,1,0:T(8,128)(2,1)S(1)}, u32[]{:S(2)}, u32[]{:S(2)}) collective-permute-start(bf16[64,8,256]{2,1,0:T(8,128)(2,1)S(1)} %get-tuple-element.42), channel_id=1, source_target_pairs={{0,24},{2,26},{4,28},{6,30},{8,0},{10,2},{12,4},{14,6},{16,8},{18,... | collective-permute-start | bytes 786440 | tf_op jit(solution)/shard_map/ppermute | solution.py:479
  28.7 1.4 %collective-permute-start.3 = (bf16[64,8,256]{2,1,0:T(8,128)(2,1)S(1)}, bf16[64,8,256]{2,1,0:T(8,128)(2,1)S(1)}, u32[]{:S(2)}, u32[]{:S(2)}) collective-permute-start(bf16[64,8,256]{2,1,0:T(8,128)(2,1)S(1)} %get-tuple-element.43), channel_id=1, source_target_pairs={{0,26},{2,28},{4,30},{6,0},{8,2},{10,4},{12,6},{14,8},{16,10},{18,... | collective-permute-start | bytes 786440 | tf_op jit(solution)/shard_map/ppermute | solution.py:479
  30.1 1.4 %collective-permute-start.4 = (bf16[64,8,256]{2,1,0:T(8,128)(2,1)S(1)}, bf16[64,8,256]{2,1,0:T(8,128)(2,1)S(1)}, u32[]{:S(2)}, u32[]{:S(2)}) collective-permute-start(bf16[64,8,256]{2,1,0:T(8,128)(2,1)S(1)} %get-tuple-element.44), channel_id=1, source_target_pairs={{0,28},{2,30},{4,0},{6,2},{8,4},{10,6},{12,8},{14,10},{16,12},{18,... | collective-permute-start | bytes 786440 | tf_op jit(solution)/shard_map/ppermute | solution.py:479
  31.5 1.4 %collective-permute-start.5 = (bf16[64,8,256]{2,1,0:T(8,128)(2,1)S(1)}, bf16[64,8,256]{2,1,0:T(8,128)(2,1)S(1)}, u32[]{:S(2)}, u32[]{:S(2)}) collective-permute-start(bf16[64,8,256]{2,1,0:T(8,128)(2,1)S(1)} %get-tuple-element.45), channel_id=1, source_target_pairs={{0,30},{2,0},{4,2},{6,4},{8,6},{10,8},{12,10},{14,12},{16,14},{18,... | collective-permute-start | bytes 786440 | tf_op jit(solution)/shard_map/ppermute | solution.py:479
  32.9 20.7 %near.1 = (f32[12800,128]{1,0:T(8,128)S(1)}, f32[5056,128]{1,0:T(8,128)S(1)}, f32[144,16,128]{2,1,0:T(8,128)S(1)}) custom-call(s32[36864]{0:T(1024)S(1)} %bitcast.6, bf16[288,8,256]{2,1,0:T(8,128)(2,1)S(1)} %get-tuple-element.38.rows_ref, f32[316,256]{1,0:T(8,128)S(1)} %get-tuple-element.39.trans_ref), custom_call_target="tpu_custom_call" | custom-call | flops 20000000000 | bytes 60000000 | tf_op jit(solution)/shard_map/near/pallas_call | solution.py:486
  53.6 0.0 collective-permute-done.2.refs_0_
  53.6 0.1 collective-permute-start.6
  53.7 0.5 collective-permute-start.7
  54.2 0.1 collective-permute-start.8
  54.3 0.4 collective-permute-start.9
  54.7 0.5 collective-permute-done.6.refs_4_
  55.2 0.4 collective-permute-done.7.refs_5_
  55.6 0.4 collective-permute-done.8.refs_6_
  56.0 0.4 collective-permute-done.9.refs_7_
  56.4 21.0 %rest.1 = (f32[144,16,128]{2,1,0:T(8,128)S(1)}, bf16[144,4,256]{2,1,0:T(4,128)(2,1)S(1)}, bf16[144,4,256]{2,1,0:T(4,128)(2,1)S(1)}, f32[12800,128]{1,0:T(8,128)S(1)}) custom-call(s32[36864]{0:T(1024)S(1)} %bitcast.7, s32[36864]{0:T(1024)S(1)} %bitcast.8, f32[12800,128]{1,0:T(8,128)S(1)} %get-tuple-element.40.table_in, ...), custom_call_target="tpu_custom_call", output_to_operand_aliasing={{3}: (2, {}), {0}: (12, {})} | custom-call | tf_op jit(solution)/shard_map/rest/pallas_call | solution.py:500
  77.4 0.2 collective-permute-start.10
  77.6 1.4 %collective-permute-done.10.recv_ref = bf16[144,4,256]{2,1,0:T(4,128)(2,1)S(1)} collective-permute-done((bf16[144,4,256]{2,1,0:T(4,128)(2,1)S(1)}, bf16[144,4,256]{2,1,0:T(4,128)(2,1)S(1)}, u32[]{:S(2)}, u32[]{:S(2)}) %collective-permute-start.10) | collective-permute-done | bytes 294944 | tf_op jit(solution)/shard_map/ppermute | solution.py:36
  79.0 1.3 %local.1 = (f32[256,4,256]{2,1,0:T(4,128)}, f32[32,4,256]{2,1,0:T(4,128)}) custom-call(bf16[144,4,256]{2,1,0:T(4,128)(2,1)S(1)} %get-tuple-element.52.keep_ref, bf16[144,4,256]{2,1,0:T(4,128)(2,1)S(1)} %collective-permute-done.10.recv_ref, bf16[256,256]{1,0:T(8,128)(2,1)S(1)} %copy-done), custom_call_target="tpu_custom_call" | custom-call | tf_op jit(solution)/shard_map/local/pallas_call | solution.py:521
  (6 shorter events, 0.0 us)
Async XLA Ops:
  0.6 2.9 %collective-permute-start = (bf16[256,4,128]{2,1,0:T(4,128)(2,1)}, bf16[256,4,128]{2,1,0:T(4,128)(2,1)S(1)}, u32[]{:S(2)}, u32[]{:S(2)}) collective-permute-start(bf16[256,4,128]{2,1,0:T(4,128)(2,1)} %own_hbm.1), channel_id=1, source_target_pairs={{0,1},{1,0},{2,3},{3,2},{4,5},{5,4},{6,7},{7,6},{8,9},{9,8},{10,11... | collective-permute-start | bytes 786440 | tf_op jit(solution)/shard_map/ppermute | solution.py:36
  20.9 2.1 %collective-permute-start.1 = (bf16[144,8,256]{2,1,0:T(8,128)(2,1)S(1)}, bf16[144,8,256]{2,1,0:T(8,128)(2,1)S(1)}, u32[]{:S(2)}, u32[]{:S(2)}) collective-permute-start(bf16[144,8,256]{2,1,0:T(8,128)(2,1)S(1)} %upward.1.own_ref), channel_id=1, source_target_pairs={{0,1},{1,0},{2,3},{3,2},{4,5},{5,4},{6,7},{7,6},{8,9},{9,8},{10,11... | collective-permute-start | bytes 1769480 | tf_op jit(solution)/shard_map/ppermute | solution.py:36
  23.9 29.7 %collective-permute-start.2 = (bf16[64,8,256]{2,1,0:T(8,128)(2,1)S(1)}, bf16[64,8,256]{2,1,0:T(8,128)(2,1)S(1)}, u32[]{:S(2)}, u32[]{:S(2)}) collective-permute-start(bf16[64,8,256]{2,1,0:T(8,128)(2,1)S(1)} %get-tuple-element.42), channel_id=1, source_target_pairs={{0,24},{2,26},{4,28},{6,30},{8,0},{10,2},{12,4},{14,6},{16,8},{18,... | collective-permute-start | bytes 786440 | tf_op jit(solution)/shard_map/ppermute | solution.py:479
  28.7 24.9 %collective-permute-start.3 = (bf16[64,8,256]{2,1,0:T(8,128)(2,1)S(1)}, bf16[64,8,256]{2,1,0:T(8,128)(2,1)S(1)}, u32[]{:S(2)}, u32[]{:S(2)}) collective-permute-start(bf16[64,8,256]{2,1,0:T(8,128)(2,1)S(1)} %get-tuple-element.43), channel_id=1, source_target_pairs={{0,26},{2,28},{4,30},{6,0},{8,2},{10,4},{12,6},{14,8},{16,10},{18,... | collective-permute-start | bytes 786440 | tf_op jit(solution)/shard_map/ppermute | solution.py:479
  30.1 23.5 %collective-permute-start.4 = (bf16[64,8,256]{2,1,0:T(8,128)(2,1)S(1)}, bf16[64,8,256]{2,1,0:T(8,128)(2,1)S(1)}, u32[]{:S(2)}, u32[]{:S(2)}) collective-permute-start(bf16[64,8,256]{2,1,0:T(8,128)(2,1)S(1)} %get-tuple-element.44), channel_id=1, source_target_pairs={{0,28},{2,30},{4,0},{6,2},{8,4},{10,6},{12,8},{14,10},{16,12},{18,... | collective-permute-start | bytes 786440 | tf_op jit(solution)/shard_map/ppermute | solution.py:479
  31.5 22.1 %collective-permute-start.5 = (bf16[64,8,256]{2,1,0:T(8,128)(2,1)S(1)}, bf16[64,8,256]{2,1,0:T(8,128)(2,1)S(1)}, u32[]{:S(2)}, u32[]{:S(2)}) collective-permute-start(bf16[64,8,256]{2,1,0:T(8,128)(2,1)S(1)} %get-tuple-element.45), channel_id=1, source_target_pairs={{0,30},{2,0},{4,2},{6,4},{8,6},{10,8},{12,10},{14,12},{16,14},{18,... | collective-permute-start | bytes 786440 | tf_op jit(solution)/shard_map/ppermute | solution.py:479
  53.6 1.6 %collective-permute-start.6 = (bf16[64,8,256]{2,1,0:T(8,128)(2,1)S(1)}, bf16[64,8,256]{2,1,0:T(8,128)(2,1)S(1)}, u32[]{:S(2)}, u32[]{:S(2)}) collective-permute-start(bf16[64,8,256]{2,1,0:T(8,128)(2,1)S(1)} %collective-permute-done.2.refs_0_), channel_id=1, source_target_pairs={{0,1},{1,0},{2,3},{3,2},{4,5},{5,4},{6,7},{7,6},{8,9},{9,8},{10,11... | collective-permute-start | bytes 786440 | tf_op jit(solution)/shard_map/ppermute | solution.py:36
  53.7 1.9 %collective-permute-start.7 = (bf16[64,8,256]{2,1,0:T(8,128)(2,1)S(1)}, bf16[64,8,256]{2,1,0:T(8,128)(2,1)S(1)}, u32[]{:S(2)}, u32[]{:S(2)}) collective-permute-start(bf16[64,8,256]{2,1,0:T(8,128)(2,1)S(1)} %collective-permute-done.3.refs_1_), channel_id=1, source_target_pairs={{0,1},{1,0},{2,3},{3,2},{4,5},{5,4},{6,7},{7,6},{8,9},{9,8},{10,11... | collective-permute-start | bytes 786440 | tf_op jit(solution)/shard_map/ppermute | solution.py:36
  54.2 1.8 %collective-permute-start.8 = (bf16[64,8,256]{2,1,0:T(8,128)(2,1)S(1)}, bf16[64,8,256]{2,1,0:T(8,128)(2,1)S(1)}, u32[]{:S(2)}, u32[]{:S(2)}) collective-permute-start(bf16[64,8,256]{2,1,0:T(8,128)(2,1)S(1)} %collective-permute-done.4.refs_2_), channel_id=1, source_target_pairs={{0,1},{1,0},{2,3},{3,2},{4,5},{5,4},{6,7},{7,6},{8,9},{9,8},{10,11... | collective-permute-start | bytes 786440 | tf_op jit(solution)/shard_map/ppermute | solution.py:36
  54.3 2.1 %collective-permute-start.9 = (bf16[64,8,256]{2,1,0:T(8,128)(2,1)S(1)}, bf16[64,8,256]{2,1,0:T(8,128)(2,1)S(1)}, u32[]{:S(2)}, u32[]{:S(2)}) collective-permute-start(bf16[64,8,256]{2,1,0:T(8,128)(2,1)S(1)} %collective-permute-done.5.refs_3_), channel_id=1, source_target_pairs={{0,1},{1,0},{2,3},{3,2},{4,5},{5,4},{6,7},{7,6},{8,9},{9,8},{10,11... | collective-permute-start | bytes 786440 | tf_op jit(solution)/shard_map/ppermute | solution.py:36
  56.4 22.6 %copy-start = (bf16[256,256]{1,0:T(8,128)(2,1)S(1)}, bf16[256,256]{1,0:T(8,128)(2,1)}, u32[]{:S(2)}) copy-start(bf16[256,256]{1,0:T(8,128)(2,1)} %mat_ref.1) | copy-start | bytes 393220
  77.4 1.6 %collective-permute-start.10 = (bf16[144,4,256]{2,1,0:T(4,128)(2,1)S(1)}, bf16[144,4,256]{2,1,0:T(4,128)(2,1)S(1)}, u32[]{:S(2)}, u32[]{:S(2)}) collective-permute-start(bf16[144,4,256]{2,1,0:T(4,128)(2,1)S(1)} %get-tuple-element.53), channel_id=1, source_target_pairs={{0,1},{1,0},{2,3},{3,2},{4,5},{5,4},{6,7},{7,6},{8,9},{9,8},{10,11... | collective-permute-start | bytes 884744 | tf_op jit(solution)/shard_map/ppermute | solution.py:36

commit v6 on v5

--- a/solution.py
+++ b/solution.py
@@ -11,7 +11,7 @@
 F32 = jnp.float32
 BF16 = jnp.bfloat16
 GROUP = 9
-LEAF_UNROLL = 2
+LEAF_UNROLL = 16
 TARGET_GROUP = 16
 SIN_POLY = (4.44286790342698, -7.307443431653506, 3.594788153158899, -0.7843741906863176)
 COS_POLY = (
@@ -60,69 +60,47 @@
 
 
 def upward_kernel(
-    counts_hbm, octants_hbm, freq_hbm, pos_hbm, own_hbm, shift_hbm, wave_mat_hbm, recv_ref,
-    out_ref, freq_scr, mult_scr, child_scr, basis_scr,
-    counts_ref, octants_ref, freq_ref, pos_ref, own_ref, shift_ref, wave_mat_ref, sems,
+    counts_ref, octants_ref, freq_ref, pos_ref, own_ref, recv_ref, shift_hbm, wave_mat_hbm,
+    out_ref, freq_scr, mult_scr, child_scr, shift_ref, wave_mat_ref, sems,
 ):
     core = lax.axis_index("rhs")
     leaves, rhs_half, slots = own_ref.shape
     nodes = freq_ref.shape[1]
     base = core * leaves
-    half = pl.ds(pl.multiple_of(base, leaves), leaves)
-    moves = (
-        (counts_hbm, counts_ref),
-        (octants_hbm, octants_ref),
-        (freq_hbm, freq_ref),
-        (pos_hbm.at[:, half, :], pos_ref),
-        (own_hbm.at[half], own_ref),
-        (wave_mat_hbm, wave_mat_ref),
-        (shift_hbm, shift_ref),
-    )
-    copies = [pltpu.make_async_copy(a, b, sems.at[i]) for i, (a, b) in enumerate(moves)]
+    copies = [
+        pltpu.make_async_copy(wave_mat_hbm, wave_mat_ref, sems.at[0]),
+        pltpu.make_async_copy(shift_hbm, shift_ref, sems.at[1]),
+    ]
     for copy in copies:
         copy.start()
-    for copy in copies[:5]:
-        copy.wait()
     for d in range(3):
         row = freq_ref[d : d + 1, :] * (1.0 / (2.0 * math.pi))
         freq_scr[d] = jnp.broadcast_to(row, (slots, nodes)).T
     lane = lax.broadcasted_iota(jnp.int32, (2 * rhs_half, slots), 1)
 
-    def put_basis(b):
-        xs = [jnp.broadcast_to(pos_ref[d, pl.ds(b, 1), :], (nodes, slots)) for d in range(3)]
-        turns = freq_scr[0] * xs[0] + freq_scr[1] * xs[1] + freq_scr[2] * xs[2]
-        sin, cos = sin_cos_turns(turns)
-        basis_scr[b % (2 * LEAF_UNROLL), :nodes] = cos.astype(BF16)
-        basis_scr[b % (2 * LEAF_UNROLL), nodes:] = sin.astype(BF16)
-
-    def put_multipole(b):
+    def one_leaf(b):
         own, recv = own_ref[b].astype(F32), recv_ref[base + b].astype(F32)
         lower = jnp.where(core == 0, own, recv)
         upper = jnp.where(core == 0, recv, own)
         charge = jnp.concatenate([lower, upper], axis=0)
         charge = jnp.where(lane < counts_ref[base + b], charge, 0.0).astype(BF16)
+        xs = [jnp.broadcast_to(pos_ref[d, pl.ds(b, 1), :], (nodes, slots)) for d in range(3)]
+        turns = freq_scr[0] * xs[0] + freq_scr[1] * xs[1] + freq_scr[2] * xs[2]
+        sin, cos = sin_cos_turns(turns)
+        basis = jnp.concatenate([cos.astype(BF16), sin.astype(BF16)], axis=0)
         multipole = lax.dot_general(
-            charge,
-            basis_scr[b % (2 * LEAF_UNROLL)],
-            (((1,), (1,)), ((), ())),
-            preferred_element_type=F32,
+            charge, basis, (((1,), (1,)), ((), ())), preferred_element_type=F32
         ).astype(BF16)
         mult_scr[b] = multipole
         child_scr[octants_ref[base + b], b // 8] = multipole
 
     def step(g, carry):
         for k in range(LEAF_UNROLL):
-            put_multipole((g - 1) * LEAF_UNROLL + k)
-        for k in range(LEAF_UNROLL):
-            put_basis(g * LEAF_UNROLL + k)
+            one_leaf(g * LEAF_UNROLL + k)
         return carry
 
-    for k in range(LEAF_UNROLL):
-        put_basis(k)
-    lax.fori_loop(1, leaves // LEAF_UNROLL, step, 0)
-    for k in range(LEAF_UNROLL):
-        put_multipole(leaves - LEAF_UNROLL + k)
-    for copy in copies[5:]:
+    lax.fori_loop(0, leaves // LEAF_UNROLL, step, 0)
+    for copy in copies:
         copy.wait()
     parents = leaves // 8
     rhs, width = mult_scr.shape[1:]
@@ -144,7 +122,9 @@
 
 def plan_kernel(
     local_rows, split, leaf_hbm, parent_hbm, send_leaf_hbm, send_parent_hbm, trans_hbm,
-    first_out, second_out, send_leaf_out, send_parent_out, trans_out, leaf_ref, parent_ref, sems,
+    counts_hbm, octants_hbm, freq_hbm, pos_hbm, own_hbm,
+    first_out, second_out, send_leaf_out, send_parent_out, trans_out,
+    counts_out, octants_out, freq_out, pos_out, own_out, leaf_ref, parent_ref, sems,
 ):
     core = lax.axis_index("rhs")
     list_len, _, leaves = leaf_ref.shape
@@ -157,6 +137,11 @@
         pltpu.make_async_copy(send_leaf_hbm, send_leaf_out, sems.at[2]),
         pltpu.make_async_copy(send_parent_hbm, send_parent_out, sems.at[3]),
         pltpu.make_async_copy(trans_hbm, trans_out, sems.at[4]),
+        pltpu.make_async_copy(counts_hbm, counts_out, sems.at[5]),
+        pltpu.make_async_copy(octants_hbm, octants_out, sems.at[6]),
+        pltpu.make_async_copy(freq_hbm, freq_out, sems.at[7]),
+        pltpu.make_async_copy(pos_hbm.at[:, lanes, :], pos_out, sems.at[8]),
+        pltpu.make_async_copy(own_hbm.at[lanes], own_out, sems.at[9]),
     ]
     for copy in copies:
         copy.start()
@@ -403,7 +388,7 @@
 
     arrived_charges = swap_cores(charges)
     index_shape = jax.ShapeDtypeStruct((2 * held, 128), jnp.int32)
-    first, second, leaf_ids, parent_ids, factors = pl.pallas_call(
+    first, second, leaf_ids, parent_ids, factors, *early = pl.pallas_call(
         functools.partial(plan_kernel, 2 * held, split),
         out_shape=[
             index_shape,
@@ -411,53 +396,46 @@
             jax.ShapeDtypeStruct(send_leaf.shape[1:], jnp.int32),
             jax.ShapeDtypeStruct(send_parent.shape[1:], jnp.int32),
             jax.ShapeDtypeStruct(translation.shape, F32),
+            jax.ShapeDtypeStruct(point_counts.shape, jnp.int32),
+            jax.ShapeDtypeStruct(octants.shape, jnp.int32),
+            jax.ShapeDtypeStruct(frequencies.shape, F32),
+            jax.ShapeDtypeStruct((3, leaves, positions.shape[2]), F32),
+            jax.ShapeDtypeStruct((leaves,) + charges.shape[1:], BF16),
         ],
-        in_specs=[HBM] * 5,
-        out_specs=[VMEM] * 5,
+        in_specs=[HBM] * 10,
+        out_specs=[VMEM] * 10,
         scratch_shapes=[
             pltpu.VMEM((list_len, 2, leaves), jnp.int32),
             pltpu.VMEM((parents, 2, list_len), jnp.int32),
-            pltpu.SemaphoreType.DMA((5,)),
+            pltpu.SemaphoreType.DMA((10,)),
         ],
         compiler_params=pltpu.CompilerParams(vmem_limit_bytes=12 << 20),
         name="plan",
     )(
         *in_hbm(
             jnp.transpose(leaf_pairs, (2, 1, 0)), parent_pairs, send_leaf[0], send_parent[0],
-            translation,
+            translation, point_counts, octants, frequencies,
+            jnp.transpose(positions, (1, 0, 2)), charges,
         )
-    )
-    arrived_charges, first, second, leaf_ids, parent_ids, factors = lax.optimization_barrier(
-        (arrived_charges, first, second, leaf_ids, parent_ids, factors)
     )
     first, second = first.reshape(-1), second.reshape(-1)
     waves = pl.pallas_call(
         upward_kernel,
         out_shape=jax.ShapeDtypeStruct((held, 2 * rhs, width), BF16),
-        in_specs=[HBM] * 7 + [VMEM],
+        in_specs=[SMEM] * 2 + [VMEM] * 4 + [HBM] * 2,
         out_specs=VMEM,
         scratch_shapes=[
             pltpu.VMEM((3, width // 2, positions.shape[2]), F32),
             pltpu.VMEM((leaves, 2 * rhs, width), BF16),
             pltpu.VMEM((8, parents, 2 * rhs, width), BF16),
-            pltpu.VMEM((2 * LEAF_UNROLL, width, positions.shape[2]), BF16),
-            pltpu.SMEM(point_counts.shape, jnp.int32),
-            pltpu.SMEM(octants.shape, jnp.int32),
-            pltpu.VMEM(frequencies.shape, F32),
-            pltpu.VMEM((3, leaves, positions.shape[2]), F32),
-            pltpu.VMEM((leaves,) + charges.shape[1:], BF16),
             pltpu.VMEM(child_shift.shape, BF16),
             pltpu.VMEM(to_wave.shape, BF16),
-            pltpu.SemaphoreType.DMA((7,)),
+            pltpu.SemaphoreType.DMA((2,)),
         ],
         compiler_params=pltpu.CompilerParams(vmem_limit_bytes=12 << 20),
         name="upward",
     )(
-        *in_hbm(
-            point_counts, octants, frequencies, jnp.transpose(positions, (1, 0, 2)), charges,
-            child_shift, to_wave,
-        ),
-        arrived_charges,
+        *early, arrived_charges, *in_hbm(child_shift, to_wave)
     )
     arrived_waves = swap_cores(waves)
     rows, *sent = pl.pallas_call(

time: 80.5 us -> 73 us (0.907)
  Pallas kernels: 63.6 us -> 56.2 us
    pallas_call x1, Pallas kernels: 17.3 us -> 9.78 us  [shards(): pl.pallas_call(upward_kernel, out_shape=jax.ShapeDtypeStruct((held, 2 * r...]
  transfers between devices with their start and end apart: 11 -> 11, of which waited for: 6 -> 6; matrix products, arithmetic and copies ran while one was open for 0% -> 0% of each run, Pallas kernels for 29% -> 32%
where the time goes in v6:
time: 73 us; the launch traced here: 72.9 us
  Pallas kernels  56.2 us (77%)
  starting transfers between devices  10.9 us (15%)
  waiting for transfers between devices  5.04 us (7%)
  between operations  0.73 us (1%)
    pallas_call x1, Pallas kernels, shards(): pl.pallas_call(functools.partial(rest_kernel, (slots, cap_l, cap_p, 2 * h...  21 us
    pallas_call x1, Pallas kernels, shards(): pl.pallas_call(functools.partial(near_kernel, split), out_shape=[table_sh...  20.7 us
    pallas_call x1, Pallas kernels, shards(): pl.pallas_call(upward_kernel, out_shape=jax.ShapeDtypeStruct((held, 2 * r...  9.78 us
    ppermute x4, starting transfers between devices, shards(): lax.ppermute(part, ('space', 'rhs'), slot_permutation(k))  9 us
    ppermute x7, waiting for transfers between devices, swap_cores(): return lax.ppermute(value, 'rhs', [(0, 1), (1, 0)])  5.03 us
    pallas_call x1, Pallas kernels, shards(): pl.pallas_call(functools.partial(plan_kernel, 2 * held, split), out_shape...  2.47 us
    ppermute x7, starting transfers between devices, swap_cores(): return lax.ppermute(value, 'rhs', [(0, 1), (1, 0)])  1.92 us
  transfers between devices with their start and end apart: 11, of which 6 were waited for; matrix products, arithmetic and copies ran while one was open for 0% of the time, Pallas kernels for 32%

profile of v6, /device:TPU:0, one launch (start us, length us, event | category | flops | bytes accessed | tf_op | source)
XLA Modules:
  0.0 72.9 jit_solution(4559263848085826891)
XLA Ops:
  0.6 0.5 collective-permute-start
  1.2 2.5 %plan.1 = (s32[288,128]{1,0:T(8,128)S(1)}, s32[288,128]{1,0:T(8,128)S(1)}, s32[8,48]{1,0:T(8,128)S(1)}, s32[8,16]{1,0:T(8,128)S(1)}, f32[316,256]{1,0:T(8,128)S(...) custom-call(s32[189,2,256]{2,1,0:T(2,128)} %bitcast.10, ...), custom_call_target="tpu_custom_call" | custom-call | tf_op jit(solution)/shard_map/plan/pallas_call | solution.py:391
  3.6 0.0 collective-permute-done.recv_ref
  3.6 9.8 %upward.1.own_ref = bf16[144,8,256]{2,1,0:T(8,128)(2,1)S(1)} custom-call(s32[256]{0:T(256)S(1)} %get-tuple-element.31.counts_ref, s32[256]{0:T(256)S(1)} %get-tuple-element.32.octants_ref, f32[3,128]{1,0:T(4,128)S(1)} %get-tuple-element.33.freq_ref, f32[3,128,128]{2,1,0:T(8,128)S(1)} %get-tuple-element.34.pos_ref, ...), custom_call_target="tpu_custom_call" | custom-call | tf_op jit(solution)/shard_map/upward/pallas_call | solution.py:422
  13.4 0.1 collective-permute-start.1
  13.6 1.9 %collective-permute-done.1.recv_ref = bf16[144,8,256]{2,1,0:T(8,128)(2,1)S(1)} collective-permute-done((bf16[144,8,256]{2,1,0:T(8,128)(2,1)S(1)}, bf16[144,8,256]{2,1,0:T(8,128)(2,1)S(1)}, u32[]{:S(2)}, u32[]{:S(2)}) %collective-permute-start.1) | collective-permute-done | bytes 589856 | tf_op jit(solution)/shard_map/ppermute | solution.py:36
  15.5 1.0 %pack.1 = (bf16[288,8,256]{2,1,0:T(8,128)(2,1)S(1)}, bf16[64,8,256]{2,1,0:T(8,128)(2,1)S(1)}, bf16[64,8,256]{2,1,0:T(8,128)(2,1)S(1)}, bf16[64,8,256]{2,1,0:T(8,128)(2,1)S(1)}, bf16[64,8,256]{2,1,0:T(8,128)(2,1)S(1)}) custom-call(s32[8,48]{1,0:T(8,128)S(1)} %get-tuple-element.29.leaf_ids_ref, s32[8,16]{1,0:T(8,128)S(1)} %get-tuple-element.30.parent_ids_ref, ...), custom_call_target="tpu_custom_call" | custom-call | tf_op jit(solution)/shard_map/pack/pallas_call | solution.py:441
  16.5 4.8 %collective-permute-start.2 = (bf16[64,8,256]{2,1,0:T(8,128)(2,1)S(1)}, bf16[64,8,256]{2,1,0:T(8,128)(2,1)S(1)}, u32[]{:S(2)}, u32[]{:S(2)}) collective-permute-start(bf16[64,8,256]{2,1,0:T(8,128)(2,1)S(1)} %get-tuple-element.40), channel_id=1, source_target_pairs={{0,24},{2,26},{4,28},{6,30},{8,0},{10,2},{12,4},{14,6},{16,8},{18,... | collective-permute-start | bytes 786440 | tf_op jit(solution)/shard_map/ppermute | solution.py:457
  21.3 1.4 %collective-permute-start.3 = (bf16[64,8,256]{2,1,0:T(8,128)(2,1)S(1)}, bf16[64,8,256]{2,1,0:T(8,128)(2,1)S(1)}, u32[]{:S(2)}, u32[]{:S(2)}) collective-permute-start(bf16[64,8,256]{2,1,0:T(8,128)(2,1)S(1)} %get-tuple-element.41), channel_id=1, source_target_pairs={{0,26},{2,28},{4,30},{6,0},{8,2},{10,4},{12,6},{14,8},{16,10},{18,... | collective-permute-start | bytes 786440 | tf_op jit(solution)/shard_map/ppermute | solution.py:457
  22.6 1.4 %collective-permute-start.4 = (bf16[64,8,256]{2,1,0:T(8,128)(2,1)S(1)}, bf16[64,8,256]{2,1,0:T(8,128)(2,1)S(1)}, u32[]{:S(2)}, u32[]{:S(2)}) collective-permute-start(bf16[64,8,256]{2,1,0:T(8,128)(2,1)S(1)} %get-tuple-element.42), channel_id=1, source_target_pairs={{0,28},{2,30},{4,0},{6,2},{8,4},{10,6},{12,8},{14,10},{16,12},{18,... | collective-permute-start | bytes 786440 | tf_op jit(solution)/shard_map/ppermute | solution.py:457
  24.1 1.4 %collective-permute-start.5 = (bf16[64,8,256]{2,1,0:T(8,128)(2,1)S(1)}, bf16[64,8,256]{2,1,0:T(8,128)(2,1)S(1)}, u32[]{:S(2)}, u32[]{:S(2)}) collective-permute-start(bf16[64,8,256]{2,1,0:T(8,128)(2,1)S(1)} %get-tuple-element.43), channel_id=1, source_target_pairs={{0,30},{2,0},{4,2},{6,4},{8,6},{10,8},{12,10},{14,12},{16,14},{18,... | collective-permute-start | bytes 786440 | tf_op jit(solution)/shard_map/ppermute | solution.py:457
  25.5 20.7 %near.1 = (f32[12800,128]{1,0:T(8,128)S(1)}, f32[5056,128]{1,0:T(8,128)S(1)}, f32[144,16,128]{2,1,0:T(8,128)S(1)}) custom-call(s32[36864]{0:T(1024)S(1)} %bitcast.6, bf16[288,8,256]{2,1,0:T(8,128)(2,1)S(1)} %get-tuple-element.36.rows_ref, f32[316,256]{1,0:T(8,128)S(1)} %get-tuple-element.37.trans_ref), custom_call_target="tpu_custom_call" | custom-call | flops 20000000000 | bytes 60000000 | tf_op jit(solution)/shard_map/near/pallas_call | solution.py:464
  46.2 0.1 collective-permute-start.6
  46.3 0.5 collective-permute-start.7
  46.8 0.1 collective-permute-start.8
  46.9 0.4 collective-permute-start.9
  47.3 0.5 collective-permute-done.6.refs_4_
  47.8 0.4 collective-permute-done.7.refs_5_
  48.2 0.4 collective-permute-done.8.refs_6_
  48.6 0.4 collective-permute-done.9.refs_7_
  48.9 21.0 %rest.1 = (f32[144,16,128]{2,1,0:T(8,128)S(1)}, bf16[144,4,256]{2,1,0:T(4,128)(2,1)S(1)}, bf16[144,4,256]{2,1,0:T(4,128)(2,1)S(1)}, f32[12800,128]{1,0:T(8,128)S(1)}) custom-call(s32[36864]{0:T(1024)S(1)} %bitcast.7, s32[36864]{0:T(1024)S(1)} %bitcast.8, f32[12800,128]{1,0:T(8,128)S(1)} %get-tuple-element.38.table_in, ...), custom_call_target="tpu_custom_call", output_to_operand_aliasing={{3}: (2, {}), {0}: (12, {})} | custom-call | tf_op jit(solution)/shard_map/rest/pallas_call | solution.py:478
  69.9 0.2 collective-permute-start.10
  70.1 1.4 %collective-permute-done.10.recv_ref = bf16[144,4,256]{2,1,0:T(4,128)(2,1)S(1)} collective-permute-done((bf16[144,4,256]{2,1,0:T(4,128)(2,1)S(1)}, bf16[144,4,256]{2,1,0:T(4,128)(2,1)S(1)}, u32[]{:S(2)}, u32[]{:S(2)}) %collective-permute-start.10) | collective-permute-done | bytes 294944 | tf_op jit(solution)/shard_map/ppermute | solution.py:36
  71.6 1.3 %local.1 = (f32[256,4,256]{2,1,0:T(4,128)}, f32[32,4,256]{2,1,0:T(4,128)}) custom-call(bf16[144,4,256]{2,1,0:T(4,128)(2,1)S(1)} %get-tuple-element.50.keep_ref, bf16[144,4,256]{2,1,0:T(4,128)(2,1)S(1)} %collective-permute-done.10.recv_ref, bf16[256,256]{1,0:T(8,128)(2,1)S(1)} %copy-done), custom_call_target="tpu_custom_call" | custom-call | tf_op jit(solution)/shard_map/local/pallas_call | solution.py:499
  (6 shorter events, 0.0 us)
Async XLA Ops:
  0.6 3.0 %collective-permute-start = (bf16[256,4,128]{2,1,0:T(4,128)(2,1)}, bf16[256,4,128]{2,1,0:T(4,128)(2,1)S(1)}, u32[]{:S(2)}, u32[]{:S(2)}) collective-permute-start(bf16[256,4,128]{2,1,0:T(4,128)(2,1)} %own_hbm.1), channel_id=1, source_target_pairs={{0,1},{1,0},{2,3},{3,2},{4,5},{5,4},{6,7},{7,6},{8,9},{9,8},{10,11... | collective-permute-start | bytes 786440 | tf_op jit(solution)/shard_map/ppermute | solution.py:36
  13.4 2.1 %collective-permute-start.1 = (bf16[144,8,256]{2,1,0:T(8,128)(2,1)S(1)}, bf16[144,8,256]{2,1,0:T(8,128)(2,1)S(1)}, u32[]{:S(2)}, u32[]{:S(2)}) collective-permute-start(bf16[144,8,256]{2,1,0:T(8,128)(2,1)S(1)} %upward.1.own_ref), channel_id=1, source_target_pairs={{0,1},{1,0},{2,3},{3,2},{4,5},{5,4},{6,7},{7,6},{8,9},{9,8},{10,11... | collective-permute-start | bytes 1769480 | tf_op jit(solution)/shard_map/ppermute | solution.py:36
  16.5 29.7 %collective-permute-start.2 = (bf16[64,8,256]{2,1,0:T(8,128)(2,1)S(1)}, bf16[64,8,256]{2,1,0:T(8,128)(2,1)S(1)}, u32[]{:S(2)}, u32[]{:S(2)}) collective-permute-start(bf16[64,8,256]{2,1,0:T(8,128)(2,1)S(1)} %get-tuple-element.40), channel_id=1, source_target_pairs={{0,24},{2,26},{4,28},{6,30},{8,0},{10,2},{12,4},{14,6},{16,8},{18,... | collective-permute-start | bytes 786440 | tf_op jit(solution)/shard_map/ppermute | solution.py:457
  21.3 24.9 %collective-permute-start.3 = (bf16[64,8,256]{2,1,0:T(8,128)(2,1)S(1)}, bf16[64,8,256]{2,1,0:T(8,128)(2,1)S(1)}, u32[]{:S(2)}, u32[]{:S(2)}) collective-permute-start(bf16[64,8,256]{2,1,0:T(8,128)(2,1)S(1)} %get-tuple-element.41), channel_id=1, source_target_pairs={{0,26},{2,28},{4,30},{6,0},{8,2},{10,4},{12,6},{14,8},{16,10},{18,... | collective-permute-start | bytes 786440 | tf_op jit(solution)/shard_map/ppermute | solution.py:457
  22.6 23.5 %collective-permute-start.4 = (bf16[64,8,256]{2,1,0:T(8,128)(2,1)S(1)}, bf16[64,8,256]{2,1,0:T(8,128)(2,1)S(1)}, u32[]{:S(2)}, u32[]{:S(2)}) collective-permute-start(bf16[64,8,256]{2,1,0:T(8,128)(2,1)S(1)} %get-tuple-element.42), channel_id=1, source_target_pairs={{0,28},{2,30},{4,0},{6,2},{8,4},{10,6},{12,8},{14,10},{16,12},{18,... | collective-permute-start | bytes 786440 | tf_op jit(solution)/shard_map/ppermute | solution.py:457
  24.1 22.1 %collective-permute-start.5 = (bf16[64,8,256]{2,1,0:T(8,128)(2,1)S(1)}, bf16[64,8,256]{2,1,0:T(8,128)(2,1)S(1)}, u32[]{:S(2)}, u32[]{:S(2)}) collective-permute-start(bf16[64,8,256]{2,1,0:T(8,128)(2,1)S(1)} %get-tuple-element.43), channel_id=1, source_target_pairs={{0,30},{2,0},{4,2},{6,4},{8,6},{10,8},{12,10},{14,12},{16,14},{18,... | collective-permute-start | bytes 786440 | tf_op jit(solution)/shard_map/ppermute | solution.py:457
  46.2 1.6 %collective-permute-start.6 = (bf16[64,8,256]{2,1,0:T(8,128)(2,1)S(1)}, bf16[64,8,256]{2,1,0:T(8,128)(2,1)S(1)}, u32[]{:S(2)}, u32[]{:S(2)}) collective-permute-start(bf16[64,8,256]{2,1,0:T(8,128)(2,1)S(1)} %collective-permute-done.2.refs_0_), channel_id=1, source_target_pairs={{0,1},{1,0},{2,3},{3,2},{4,5},{5,4},{6,7},{7,6},{8,9},{9,8},{10,11... | collective-permute-start | bytes 786440 | tf_op jit(solution)/shard_map/ppermute | solution.py:36
  46.3 1.9 %collective-permute-start.7 = (bf16[64,8,256]{2,1,0:T(8,128)(2,1)S(1)}, bf16[64,8,256]{2,1,0:T(8,128)(2,1)S(1)}, u32[]{:S(2)}, u32[]{:S(2)}) collective-permute-start(bf16[64,8,256]{2,1,0:T(8,128)(2,1)S(1)} %collective-permute-done.3.refs_1_), channel_id=1, source_target_pairs={{0,1},{1,0},{2,3},{3,2},{4,5},{5,4},{6,7},{7,6},{8,9},{9,8},{10,11... | collective-permute-start | bytes 786440 | tf_op jit(solution)/shard_map/ppermute | solution.py:36
  46.8 1.8 %collective-permute-start.8 = (bf16[64,8,256]{2,1,0:T(8,128)(2,1)S(1)}, bf16[64,8,256]{2,1,0:T(8,128)(2,1)S(1)}, u32[]{:S(2)}, u32[]{:S(2)}) collective-permute-start(bf16[64,8,256]{2,1,0:T(8,128)(2,1)S(1)} %collective-permute-done.4.refs_2_), channel_id=1, source_target_pairs={{0,1},{1,0},{2,3},{3,2},{4,5},{5,4},{6,7},{7,6},{8,9},{9,8},{10,11... | collective-permute-start | bytes 786440 | tf_op jit(solution)/shard_map/ppermute | solution.py:36
  46.9 2.1 %collective-permute-start.9 = (bf16[64,8,256]{2,1,0:T(8,128)(2,1)S(1)}, bf16[64,8,256]{2,1,0:T(8,128)(2,1)S(1)}, u32[]{:S(2)}, u32[]{:S(2)}) collective-permute-start(bf16[64,8,256]{2,1,0:T(8,128)(2,1)S(1)} %collective-permute-done.5.refs_3_), channel_id=1, source_target_pairs={{0,1},{1,0},{2,3},{3,2},{4,5},{5,4},{6,7},{7,6},{8,9},{9,8},{10,11... | collective-permute-start | bytes 786440 | tf_op jit(solution)/shard_map/ppermute | solution.py:36
  48.9 22.6 %copy-start = (bf16[256,256]{1,0:T(8,128)(2,1)S(1)}, bf16[256,256]{1,0:T(8,128)(2,1)}, u32[]{:S(2)}) copy-start(bf16[256,256]{1,0:T(8,128)(2,1)} %mat_ref.1) | copy-start | bytes 393220
  69.9 1.6 %collective-permute-start.10 = (bf16[144,4,256]{2,1,0:T(4,128)(2,1)S(1)}, bf16[144,4,256]{2,1,0:T(4,128)(2,1)S(1)}, u32[]{:S(2)}, u32[]{:S(2)}) collective-permute-start(bf16[144,4,256]{2,1,0:T(4,128)(2,1)S(1)} %get-tuple-element.51), channel_id=1, source_target_pairs={{0,1},{1,0},{2,3},{3,2},{4,5},{5,4},{6,7},{7,6},{8,9},{9,8},{10,11... | collective-permute-start | bytes 884744 | tf_op jit(solution)/shard_map/ppermute | solution.py:36

commit v7 on v6

--- a/solution.py
+++ b/solution.py
@@ -11,7 +11,7 @@
 F32 = jnp.float32
 BF16 = jnp.bfloat16
 GROUP = 9
-LEAF_UNROLL = 16
+LEAF_UNROLL = 32
 TARGET_GROUP = 16
 SIN_POLY = (4.44286790342698, -7.307443431653506, 3.594788153158899, -0.7843741906863176)
 COS_POLY = (
@@ -120,33 +120,33 @@
     out_ref[leaves:] = parent_waves.astype(BF16).reshape(parents, rhs, width)
 
 
-def plan_kernel(
-    local_rows, split, leaf_hbm, parent_hbm, send_leaf_hbm, send_parent_hbm, trans_hbm,
-    counts_hbm, octants_hbm, freq_hbm, pos_hbm, own_hbm,
-    first_out, second_out, send_leaf_out, send_parent_out, trans_out,
-    counts_out, octants_out, freq_out, pos_out, own_out, leaf_ref, parent_ref, sems,
-):
+def fetch_kernel(*refs):
+    count = (len(refs) - 1) // 2
+    sources, targets, sems = refs[:count], refs[count:-1], refs[-1]
     core = lax.axis_index("rhs")
+    leaves, parents = targets[0].shape[2], targets[1].shape[0]
+    half = pl.ds(pl.multiple_of(core * leaves, leaves), leaves)
+    views = [
+        sources[0].at[:, :, half],
+        sources[1].at[pl.ds(core * parents, parents)],
+        sources[2].at[:, half, :],
+        sources[3].at[half],
+        *sources[4:],
+    ]
+    copies = [
+        pltpu.make_async_copy(view, target, sems.at[i])
+        for i, (view, target) in enumerate(zip(views, targets))
+    ]
+    for copy in copies:
+        copy.start()
+    for copy in copies:
+        copy.wait()
+
+
+def plan_kernel(local_rows, split, leaf_ref, parent_ref, first_out, second_out):
     list_len, _, leaves = leaf_ref.shape
     parents = parent_ref.shape[0]
     targets = leaves + parents
-    lanes = pl.ds(pl.multiple_of(core * leaves, leaves), leaves)
-    copies = [
-        pltpu.make_async_copy(leaf_hbm.at[:, :, lanes], leaf_ref, sems.at[0]),
-        pltpu.make_async_copy(parent_hbm.at[pl.ds(core * parents, parents)], parent_ref, sems.at[1]),
-        pltpu.make_async_copy(send_leaf_hbm, send_leaf_out, sems.at[2]),
-        pltpu.make_async_copy(send_parent_hbm, send_parent_out, sems.at[3]),
-        pltpu.make_async_copy(trans_hbm, trans_out, sems.at[4]),
-        pltpu.make_async_copy(counts_hbm, counts_out, sems.at[5]),
-        pltpu.make_async_copy(octants_hbm, octants_out, sems.at[6]),
-        pltpu.make_async_copy(freq_hbm, freq_out, sems.at[7]),
-        pltpu.make_async_copy(pos_hbm.at[:, lanes, :], pos_out, sems.at[8]),
-        pltpu.make_async_copy(own_hbm.at[lanes], own_out, sems.at[9]),
-    ]
-    for copy in copies:
-        copy.start()
-    for copy in copies[:2]:
-        copy.wait()
     depth = -(-list_len // 8) * 8
 
     def packed(source, shift):
@@ -193,8 +193,6 @@
         tail = jnp.where(row[:128] == 127, ready, pltpu.roll(values, depth - split, 0)[:128])
         first_out[pl.ds(h, targets, stride=2), :] = head.T[:targets]
         second_out[pl.ds(h, targets, stride=2), :] = tail.T[:targets]
-    for copy in copies[2:]:
-        copy.wait()
 
 
 def pack_kernel(leaf_ids_ref, parent_ids_ref, own_ref, recv_ref, *refs):
@@ -387,38 +385,23 @@
     table_rows = 2 * held + slots * (cap_l + cap_p)
 
     arrived_charges = swap_cores(charges)
-    index_shape = jax.ShapeDtypeStruct((2 * held, 128), jnp.int32)
-    first, second, leaf_ids, parent_ids, factors, *early = pl.pallas_call(
-        functools.partial(plan_kernel, 2 * held, split),
-        out_shape=[
-            index_shape,
-            index_shape,
-            jax.ShapeDtypeStruct(send_leaf.shape[1:], jnp.int32),
-            jax.ShapeDtypeStruct(send_parent.shape[1:], jnp.int32),
-            jax.ShapeDtypeStruct(translation.shape, F32),
-            jax.ShapeDtypeStruct(point_counts.shape, jnp.int32),
-            jax.ShapeDtypeStruct(octants.shape, jnp.int32),
-            jax.ShapeDtypeStruct(frequencies.shape, F32),
-            jax.ShapeDtypeStruct((3, leaves, positions.shape[2]), F32),
-            jax.ShapeDtypeStruct((leaves,) + charges.shape[1:], BF16),
-        ],
-        in_specs=[HBM] * 10,
-        out_specs=[VMEM] * 10,
-        scratch_shapes=[
-            pltpu.VMEM((list_len, 2, leaves), jnp.int32),
-            pltpu.VMEM((parents, 2, list_len), jnp.int32),
-            pltpu.SemaphoreType.DMA((10,)),
-        ],
+    fetched = [
+        (jnp.transpose(leaf_pairs, (2, 1, 0)), (list_len, 2, leaves)),
+        (parent_pairs, (parents, 2, list_len)),
+        (jnp.transpose(positions, (1, 0, 2)), (3, leaves, positions.shape[2])),
+        (charges, (leaves,) + charges.shape[1:]),
+    ]
+    whole = (send_leaf[0], send_parent[0], translation, point_counts, octants, frequencies)
+    fetched += [(value, value.shape) for value in whole]
+    leaf_half, parent_half, pos_half, own_half, leaf_ids, parent_ids, factors, *early = pl.pallas_call(
+        fetch_kernel,
+        out_shape=[jax.ShapeDtypeStruct(shape, value.dtype) for value, shape in fetched],
+        in_specs=[HBM] * len(fetched),
+        out_specs=[VMEM] * len(fetched),
+        scratch_shapes=[pltpu.SemaphoreType.DMA((len(fetched),))],
         compiler_params=pltpu.CompilerParams(vmem_limit_bytes=12 << 20),
-        name="plan",
-    )(
-        *in_hbm(
-            jnp.transpose(leaf_pairs, (2, 1, 0)), parent_pairs, send_leaf[0], send_parent[0],
-            translation, point_counts, octants, frequencies,
-            jnp.transpose(positions, (1, 0, 2)), charges,
-        )
-    )
-    first, second = first.reshape(-1), second.reshape(-1)
+        name="fetch",
+    )(*in_hbm(*(value for value, _ in fetched)))
     waves = pl.pallas_call(
         upward_kernel,
         out_shape=jax.ShapeDtypeStruct((held, 2 * rhs, width), BF16),
@@ -435,9 +418,21 @@
         compiler_params=pltpu.CompilerParams(vmem_limit_bytes=12 << 20),
         name="upward",
     )(
-        *early, arrived_charges, *in_hbm(child_shift, to_wave)
+        *early, pos_half, own_half, arrived_charges, *in_hbm(child_shift, to_wave)
     )
     arrived_waves = swap_cores(waves)
+    waves, leaf_half, parent_half = lax.optimization_barrier((waves, leaf_half, parent_half))
+    index_shape = jax.ShapeDtypeStruct((2 * held, 128), jnp.int32)
+    first, second = pl.pallas_call(
+        functools.partial(plan_kernel, 2 * held, split),
+        out_shape=[index_shape] * 2,
+        in_specs=[VMEM] * 2,
+        out_specs=[VMEM] * 2,
+        compiler_params=pltpu.CompilerParams(vmem_limit_bytes=12 << 20),
+        name="plan",
+    )(leaf_half, parent_half)
+    arrived_waves, first, second = lax.optimization_barrier((arrived_waves, first, second))
+    first, second = first.reshape(-1), second.reshape(-1)
     rows, *sent = pl.pallas_call(
         pack_kernel,
         out_shape=[jax.ShapeDtypeStruct((2 * held, 2 * rhs, width), BF16)]

time: 73 us -> 71.6 us (0.981)
  waiting for transfers between devices: 5.04 us -> 3.31 us
    ppermute x7, waiting for transfers between devices: 5.03 us -> 3.3 us  [swap_cores(): return lax.ppermute(value, 'rhs', [(0, 1), (1, 0)])]
    pallas_call x0 -> x1, Pallas kernels: none -> 1.38 us  [shards(): pl.pallas_call(fetch_kernel, out_shape=[jax.ShapeDtypeStruct(shape, value...]
    pallas_call x1, Pallas kernels: 2.47 us -> 1.43 us  [shards(): pl.pallas_call(functools.partial(plan_kernel, 2 * held, split), out_shape...]
  transfers between devices with their start and end apart: 11 -> 11, of which waited for: 6 -> 6; matrix products, arithmetic and copies ran while one was open for 0% -> 0% of each run, Pallas kernels for 32% -> 33%
where the time goes in v7:
time: 71.6 us; the launch traced here: 71.5 us
  Pallas kernels  56 us (78%)
  starting transfers between devices  11.4 us (16%)
  waiting for transfers between devices  3.31 us (5%)
  between operations  0.74 us (1%)
    pallas_call x1, Pallas kernels, shards(): pl.pallas_call(functools.partial(rest_kernel, (slots, cap_l, cap_p, 2 * h...  21 us
    pallas_call x1, Pallas kernels, shards(): pl.pallas_call(functools.partial(near_kernel, split), out_shape=[table_sh...  20.7 us
    pallas_call x1, Pallas kernels, shards(): pl.pallas_call(upward_kernel, out_shape=jax.ShapeDtypeStruct((held, 2 * r...  9.26 us
    ppermute x4, starting transfers between devices, shards(): lax.ppermute(part, ('space', 'rhs'), slot_permutation(k))  9.21 us
    ppermute x7, waiting for transfers between devices, swap_cores(): return lax.ppermute(value, 'rhs', [(0, 1), (1, 0)])  3.3 us
    ppermute x7, starting transfers between devices, swap_cores(): return lax.ppermute(value, 'rhs', [(0, 1), (1, 0)])  2.21 us
  transfers between devices with their start and end apart: 11, of which 6 were waited for; matrix products, arithmetic and copies ran while one was open for 0% of the time, Pallas kernels for 33%

profile of v7, /device:TPU:0, one launch (start us, length us, event | category | flops | bytes accessed | tf_op | source)
XLA Modules:
  0.0 71.5 jit_solution(9231728745066715007)
XLA Ops:
  0.6 0.5 collective-permute-start
  1.2 1.4 %fetch.1 = (s32[189,2,128]{2,1,0:T(2,128)S(1)}, s32[16,2,189]{2,1,0:T(2,128)S(1)}, f32[3,128,128]{2,1,0:T(8,128)S(1)}, bf16[128,4,128]{2,1,0:T(4,128)(2,1)S(1)},...) custom-call(s32[189,2,256]{2,1,0:T(2,128)} %bitcast.10, ...), custom_call_target="tpu_custom_call" | custom-call | tf_op jit(solution)/shard_map/fetch/pallas_call | solution.py:396
  2.5 9.3 %upward.1.own_ref = bf16[144,8,256]{2,1,0:T(8,128)(2,1)S(1)} custom-call(s32[256]{0:T(256)S(1)} %get-tuple-element.35.counts_ref, s32[256]{0:T(256)S(1)} %get-tuple-element.36.octants_ref, f32[3,128]{1,0:T(4,128)S(1)} %get-tuple-element.37.freq_ref, f32[3,128,128]{2,1,0:T(8,128)S(1)} %get-tuple-element.38.pos_ref, ...), custom_call_target="tpu_custom_call" | custom-call | tf_op jit(solution)/shard_map/upward/pallas_call | solution.py:405
  11.8 0.4 collective-permute-start.1
  12.2 1.4 %plan.1 = (s32[288,128]{1,0:T(8,128)S(1)}, s32[288,128]{1,0:T(8,128)S(1)}) custom-call(s32[189,2,128]{2,1,0:T(2,128)S(1)} %get-tuple-element.42.leaf_ref, s32[16,2,189]{2,1,0:T(2,128)S(1)} %get-tuple-element.43.parent_ref), custom_call_target="tpu_custom_call" | custom-call | tf_op jit(solution)/shard_map/plan/pallas_call | solution.py:426
  13.7 0.2 collective-permute-done.1.recv_ref
  13.9 1.0 %pack.1 = (bf16[288,8,256]{2,1,0:T(8,128)(2,1)S(1)}, bf16[64,8,256]{2,1,0:T(8,128)(2,1)S(1)}, bf16[64,8,256]{2,1,0:T(8,128)(2,1)S(1)}, bf16[64,8,256]{2,1,0:T(8,128)(2,1)S(1)}, bf16[64,8,256]{2,1,0:T(8,128)(2,1)S(1)}) custom-call(s32[8,48]{1,0:T(8,128)S(1)} %get-tuple-element.48.leaf_ids_ref, s32[8,16]{1,0:T(8,128)S(1)} %get-tuple-element.49.parent_ids_ref, ...), custom_call_target="tpu_custom_call" | custom-call | tf_op jit(solution)/shard_map/pack/pallas_call | solution.py:436
  14.9 5.0 %collective-permute-start.2 = (bf16[64,8,256]{2,1,0:T(8,128)(2,1)S(1)}, bf16[64,8,256]{2,1,0:T(8,128)(2,1)S(1)}, u32[]{:S(2)}, u32[]{:S(2)}) collective-permute-start(bf16[64,8,256]{2,1,0:T(8,128)(2,1)S(1)} %get-tuple-element.56), channel_id=1, source_target_pairs={{0,24},{2,26},{4,28},{6,30},{8,0},{10,2},{12,4},{14,6},{16,8},{18,... | collective-permute-start | bytes 786440 | tf_op jit(solution)/shard_map/ppermute | solution.py:452
  19.9 1.4 %collective-permute-start.3 = (bf16[64,8,256]{2,1,0:T(8,128)(2,1)S(1)}, bf16[64,8,256]{2,1,0:T(8,128)(2,1)S(1)}, u32[]{:S(2)}, u32[]{:S(2)}) collective-permute-start(bf16[64,8,256]{2,1,0:T(8,128)(2,1)S(1)} %get-tuple-element.57), channel_id=1, source_target_pairs={{0,26},{2,28},{4,30},{6,0},{8,2},{10,4},{12,6},{14,8},{16,10},{18,... | collective-permute-start | bytes 786440 | tf_op jit(solution)/shard_map/ppermute | solution.py:452
  21.3 1.4 %collective-permute-start.4 = (bf16[64,8,256]{2,1,0:T(8,128)(2,1)S(1)}, bf16[64,8,256]{2,1,0:T(8,128)(2,1)S(1)}, u32[]{:S(2)}, u32[]{:S(2)}) collective-permute-start(bf16[64,8,256]{2,1,0:T(8,128)(2,1)S(1)} %get-tuple-element.58), channel_id=1, source_target_pairs={{0,28},{2,30},{4,0},{6,2},{8,4},{10,6},{12,8},{14,10},{16,12},{18,... | collective-permute-start | bytes 786440 | tf_op jit(solution)/shard_map/ppermute | solution.py:452
  22.7 1.4 %collective-permute-start.5 = (bf16[64,8,256]{2,1,0:T(8,128)(2,1)S(1)}, bf16[64,8,256]{2,1,0:T(8,128)(2,1)S(1)}, u32[]{:S(2)}, u32[]{:S(2)}) collective-permute-start(bf16[64,8,256]{2,1,0:T(8,128)(2,1)S(1)} %get-tuple-element.59), channel_id=1, source_target_pairs={{0,30},{2,0},{4,2},{6,4},{8,6},{10,8},{12,10},{14,12},{16,14},{18,... | collective-permute-start | bytes 786440 | tf_op jit(solution)/shard_map/ppermute | solution.py:452
  24.1 20.7 %near.1 = (f32[12800,128]{1,0:T(8,128)S(1)}, f32[5056,128]{1,0:T(8,128)S(1)}, f32[144,16,128]{2,1,0:T(8,128)S(1)}) custom-call(s32[36864]{0:T(1024)S(1)} %bitcast.6, bf16[288,8,256]{2,1,0:T(8,128)(2,1)S(1)} %get-tuple-element.52.rows_ref, f32[316,256]{1,0:T(8,128)S(1)} %get-tuple-element.53.trans_ref), custom_call_target="tpu_custom_call" | custom-call | flops 20000000000 | bytes 60000000 | tf_op jit(solution)/shard_map/near/pallas_call | solution.py:459
  44.8 0.1 collective-permute-start.6
  44.9 0.5 collective-permute-start.7
  45.4 0.1 collective-permute-start.8
  45.5 0.4 collective-permute-start.9
  45.9 0.5 collective-permute-done.6.refs_4_
  46.4 0.4 collective-permute-done.7.refs_5_
  46.8 0.4 collective-permute-done.8.refs_6_
  47.2 0.4 collective-permute-done.9.refs_7_
  47.5 21.0 %rest.1 = (f32[144,16,128]{2,1,0:T(8,128)S(1)}, bf16[144,4,256]{2,1,0:T(4,128)(2,1)S(1)}, bf16[144,4,256]{2,1,0:T(4,128)(2,1)S(1)}, f32[12800,128]{1,0:T(8,128)S(1)}) custom-call(s32[36864]{0:T(1024)S(1)} %bitcast.7, s32[36864]{0:T(1024)S(1)} %bitcast.8, f32[12800,128]{1,0:T(8,128)S(1)} %get-tuple-element.54.table_in, ...), custom_call_target="tpu_custom_call", output_to_operand_aliasing={{3}: (2, {}), {0}: (12, {})} | custom-call | tf_op jit(solution)/shard_map/rest/pallas_call | solution.py:473
  68.5 0.2 collective-permute-start.10
  68.7 1.4 %collective-permute-done.10.recv_ref = bf16[144,4,256]{2,1,0:T(4,128)(2,1)S(1)} collective-permute-done((bf16[144,4,256]{2,1,0:T(4,128)(2,1)S(1)}, bf16[144,4,256]{2,1,0:T(4,128)(2,1)S(1)}, u32[]{:S(2)}, u32[]{:S(2)}) %collective-permute-start.10) | collective-permute-done | bytes 294944 | tf_op jit(solution)/shard_map/ppermute | solution.py:36
  70.2 1.3 %local.1 = (f32[256,4,256]{2,1,0:T(4,128)}, f32[32,4,256]{2,1,0:T(4,128)}) custom-call(bf16[144,4,256]{2,1,0:T(4,128)(2,1)S(1)} %get-tuple-element.66.keep_ref, bf16[144,4,256]{2,1,0:T(4,128)(2,1)S(1)} %collective-permute-done.10.recv_ref, bf16[256,256]{1,0:T(8,128)(2,1)S(1)} %copy-done), custom_call_target="tpu_custom_call" | custom-call | tf_op jit(solution)/shard_map/local/pallas_call | solution.py:494
  (7 shorter events, 0.0 us)
Async XLA Ops:
  0.6 1.9 %collective-permute-start = (bf16[256,4,128]{2,1,0:T(4,128)(2,1)}, bf16[256,4,128]{2,1,0:T(4,128)(2,1)S(1)}, u32[]{:S(2)}, u32[]{:S(2)}) collective-permute-start(bf16[256,4,128]{2,1,0:T(4,128)(2,1)} %refs_3_.1), channel_id=1, source_target_pairs={{0,1},{1,0},{2,3},{3,2},{4,5},{5,4},{6,7},{7,6},{8,9},{9,8},{10,11... | collective-permute-start | bytes 786440 | tf_op jit(solution)/shard_map/ppermute | solution.py:36
  11.8 2.1 %collective-permute-start.1 = (bf16[144,8,256]{2,1,0:T(8,128)(2,1)S(1)}, bf16[144,8,256]{2,1,0:T(8,128)(2,1)S(1)}, u32[]{:S(2)}, u32[]{:S(2)}) collective-permute-start(bf16[144,8,256]{2,1,0:T(8,128)(2,1)S(1)} %upward.1.own_ref), channel_id=1, source_target_pairs={{0,1},{1,0},{2,3},{3,2},{4,5},{5,4},{6,7},{7,6},{8,9},{9,8},{10,11... | collective-permute-start | bytes 1769480 | tf_op jit(solution)/shard_map/ppermute | solution.py:36
  14.9 29.9 %collective-permute-start.2 = (bf16[64,8,256]{2,1,0:T(8,128)(2,1)S(1)}, bf16[64,8,256]{2,1,0:T(8,128)(2,1)S(1)}, u32[]{:S(2)}, u32[]{:S(2)}) collective-permute-start(bf16[64,8,256]{2,1,0:T(8,128)(2,1)S(1)} %get-tuple-element.56), channel_id=1, source_target_pairs={{0,24},{2,26},{4,28},{6,30},{8,0},{10,2},{12,4},{14,6},{16,8},{18,... | collective-permute-start | bytes 786440 | tf_op jit(solution)/shard_map/ppermute | solution.py:452
  19.9 24.9 %collective-permute-start.3 = (bf16[64,8,256]{2,1,0:T(8,128)(2,1)S(1)}, bf16[64,8,256]{2,1,0:T(8,128)(2,1)S(1)}, u32[]{:S(2)}, u32[]{:S(2)}) collective-permute-start(bf16[64,8,256]{2,1,0:T(8,128)(2,1)S(1)} %get-tuple-element.57), channel_id=1, source_target_pairs={{0,26},{2,28},{4,30},{6,0},{8,2},{10,4},{12,6},{14,8},{16,10},{18,... | collective-permute-start | bytes 786440 | tf_op jit(solution)/shard_map/ppermute | solution.py:452
  21.3 23.5 %collective-permute-start.4 = (bf16[64,8,256]{2,1,0:T(8,128)(2,1)S(1)}, bf16[64,8,256]{2,1,0:T(8,128)(2,1)S(1)}, u32[]{:S(2)}, u32[]{:S(2)}) collective-permute-start(bf16[64,8,256]{2,1,0:T(8,128)(2,1)S(1)} %get-tuple-element.58), channel_id=1, source_target_pairs={{0,28},{2,30},{4,0},{6,2},{8,4},{10,6},{12,8},{14,10},{16,12},{18,... | collective-permute-start | bytes 786440 | tf_op jit(solution)/shard_map/ppermute | solution.py:452
  22.7 22.1 %collective-permute-start.5 = (bf16[64,8,256]{2,1,0:T(8,128)(2,1)S(1)}, bf16[64,8,256]{2,1,0:T(8,128)(2,1)S(1)}, u32[]{:S(2)}, u32[]{:S(2)}) collective-permute-start(bf16[64,8,256]{2,1,0:T(8,128)(2,1)S(1)} %get-tuple-element.59), channel_id=1, source_target_pairs={{0,30},{2,0},{4,2},{6,4},{8,6},{10,8},{12,10},{14,12},{16,14},{18,... | collective-permute-start | bytes 786440 | tf_op jit(solution)/shard_map/ppermute | solution.py:452
  44.8 1.6 %collective-permute-start.6 = (bf16[64,8,256]{2,1,0:T(8,128)(2,1)S(1)}, bf16[64,8,256]{2,1,0:T(8,128)(2,1)S(1)}, u32[]{:S(2)}, u32[]{:S(2)}) collective-permute-start(bf16[64,8,256]{2,1,0:T(8,128)(2,1)S(1)} %collective-permute-done.2.refs_0_), channel_id=1, source_target_pairs={{0,1},{1,0},{2,3},{3,2},{4,5},{5,4},{6,7},{7,6},{8,9},{9,8},{10,11... | collective-permute-start | bytes 786440 | tf_op jit(solution)/shard_map/ppermute | solution.py:36
  44.9 1.9 %collective-permute-start.7 = (bf16[64,8,256]{2,1,0:T(8,128)(2,1)S(1)}, bf16[64,8,256]{2,1,0:T(8,128)(2,1)S(1)}, u32[]{:S(2)}, u32[]{:S(2)}) collective-permute-start(bf16[64,8,256]{2,1,0:T(8,128)(2,1)S(1)} %collective-permute-done.3.refs_1_), channel_id=1, source_target_pairs={{0,1},{1,0},{2,3},{3,2},{4,5},{5,4},{6,7},{7,6},{8,9},{9,8},{10,11... | collective-permute-start | bytes 786440 | tf_op jit(solution)/shard_map/ppermute | solution.py:36
  45.4 1.8 %collective-permute-start.8 = (bf16[64,8,256]{2,1,0:T(8,128)(2,1)S(1)}, bf16[64,8,256]{2,1,0:T(8,128)(2,1)S(1)}, u32[]{:S(2)}, u32[]{:S(2)}) collective-permute-start(bf16[64,8,256]{2,1,0:T(8,128)(2,1)S(1)} %collective-permute-done.4.refs_2_), channel_id=1, source_target_pairs={{0,1},{1,0},{2,3},{3,2},{4,5},{5,4},{6,7},{7,6},{8,9},{9,8},{10,11... | collective-permute-start | bytes 786440 | tf_op jit(solution)/shard_map/ppermute | solution.py:36
  45.5 2.1 %collective-permute-start.9 = (bf16[64,8,256]{2,1,0:T(8,128)(2,1)S(1)}, bf16[64,8,256]{2,1,0:T(8,128)(2,1)S(1)}, u32[]{:S(2)}, u32[]{:S(2)}) collective-permute-start(bf16[64,8,256]{2,1,0:T(8,128)(2,1)S(1)} %collective-permute-done.5.refs_3_), channel_id=1, source_target_pairs={{0,1},{1,0},{2,3},{3,2},{4,5},{5,4},{6,7},{7,6},{8,9},{9,8},{10,11... | collective-permute-start | bytes 786440 | tf_op jit(solution)/shard_map/ppermute | solution.py:36
  47.5 22.6 %copy-start = (bf16[256,256]{1,0:T(8,128)(2,1)S(1)}, bf16[256,256]{1,0:T(8,128)(2,1)}, u32[]{:S(2)}) copy-start(bf16[256,256]{1,0:T(8,128)(2,1)} %mat_ref.1) | copy-start | bytes 393220
  68.5 1.6 %collective-permute-start.10 = (bf16[144,4,256]{2,1,0:T(4,128)(2,1)S(1)}, bf16[144,4,256]{2,1,0:T(4,128)(2,1)S(1)}, u32[]{:S(2)}, u32[]{:S(2)}) collective-permute-start(bf16[144,4,256]{2,1,0:T(4,128)(2,1)S(1)} %get-tuple-element.67), channel_id=1, source_target_pairs={{0,1},{1,0},{2,3},{3,2},{4,5},{5,4},{6,7},{7,6},{8,9},{9,8},{10,11... | collective-permute-start | bytes 884744 | tf_op jit(solution)/shard_map/ppermute | solution.py:36

commit v8 on v7

--- a/solution.py
+++ b/solution.py
@@ -188,9 +188,11 @@
     sources = (words & 1023) * 16
     classes = (lax.shift_right_logical(words, 10) & 1023) * 16
     ready = (total >= split).astype(jnp.int32)
+    lane = lax.broadcasted_iota(jnp.int32, ready.shape, 1)
+    late = jnp.max(jnp.where(lane < targets, 1 - ready, 0), axis=1, keepdims=True)
     for h, values in enumerate((sources, classes)):
         head = jnp.where(row[:128] == 127, ready, values[:128])
-        tail = jnp.where(row[:128] == 127, ready, pltpu.roll(values, depth - split, 0)[:128])
+        tail = jnp.where(row[:128] == 127, late, pltpu.roll(values, depth - split, 0)[:128])
         first_out[pl.ds(h, targets, stride=2), :] = head.T[:targets]
         second_out[pl.ds(h, targets, stride=2), :] = tail.T[:targets]
 
@@ -286,7 +288,10 @@
         def _():
             index_copy(*index, g + 2).start()
 
-        index_copy(*index, g).wait()
+        @pl.when(g > 0)
+        def _():
+            index_copy(*index, g).wait()
+
         return lax.fori_loop(
             0, TARGET_GROUP, lambda t, c: one_target(g * TARGET_GROUP + t, c), carry
         )
@@ -302,14 +307,12 @@
     zero = jnp.zeros((8, table.shape[1]), F32)
 
     def one_target(b, carry):
-        @pl.when(index_scr[b * 256 + 127] > 0)
-        def _():
-            total = pair_sums(index_scr, b * 256, split, table, factor, (zero, zero))
-            acc_ref[b, :8] = total[0]
-            acc_ref[b, 8:] = total[1]
-
+        total = pair_sums(index_scr, b * 256, split, table, factor, (zero, zero))
+        acc_ref[b, :8] = total[0]
+        acc_ref[b, 8:] = total[1]
         return carry
 
+    index_copy(*index, 0).wait()
     over_targets(index, acc_ref.shape[0], one_target)
 
 
@@ -331,17 +334,27 @@
             put_rows(table, values, cap_l, cap_p, base + slots * cap_l + slot * cap_p, valid)
     zero = jnp.zeros((8, table.shape[1]), F32)
 
-    def one_target(b, carry):
-        @pl.when(index_scr[b * 256 + 127] == 0)
-        def _():
+    index_copy(*index, 0).wait()
+
+    @pl.when(index_scr[127] > 0)
+    def _():
+        def redo(b, carry):
             span = pl.ds(pl.multiple_of(b * 256, 256), 256)
             copy = pltpu.make_async_copy(first_hbm.at[span], late_scr, late_sem)
             copy.start()
             copy.wait()
-            total = pair_sums(late_scr, 0, split, table, factor, (zero, zero))
-            acc_ref[b, :8] = total[0]
-            acc_ref[b, 8:] = total[1]
-
+
+            @pl.when(late_scr[127] == 0)
+            def _():
+                total = pair_sums(late_scr, 0, split, table, factor, (zero, zero))
+                acc_ref[b, :8] = total[0]
+                acc_ref[b, 8:] = total[1]
+
+            return carry
+
+        lax.fori_loop(0, keep_ref.shape[0], redo, 0)
+
+    def one_target(b, carry):
         total = pair_sums(
             index_scr, b * 256, list_len - split, table, factor, (acc_ref[b, :8], acc_ref[b, 8:])
         )

time: 71.6 us -> 69.5 us (0.971)
  Pallas kernels: 56 us -> 53.9 us
    pallas_call x1, Pallas kernels: 20.7 us -> 19.5 us  [shards(): pl.pallas_call(functools.partial(near_kernel, split), out_shape=[table_sh...]
    pallas_call x1, Pallas kernels: 21 us -> 19.9 us  [shards(): pl.pallas_call(functools.partial(rest_kernel, (slots, cap_l, cap_p, 2 * h...]
  transfers between devices with their start and end apart: 11 -> 11, of which waited for: 6 -> 6; matrix products, arithmetic and copies ran while one was open for 0% -> 0% of each run, Pallas kernels for 33% -> 32%
where the time goes in v8:
time: 69.5 us; the launch traced here: 69.3 us
  Pallas kernels  53.9 us (78%)
  starting transfers between devices  11.4 us (16%)
  waiting for transfers between devices  3.27 us (5%)
  between operations  0.74 us (1%)
    pallas_call x1, Pallas kernels, shards(): pl.pallas_call(functools.partial(rest_kernel, (slots, cap_l, cap_p, 2 * h...  19.9 us
    pallas_call x1, Pallas kernels, shards(): pl.pallas_call(functools.partial(near_kernel, split), out_shape=[table_sh...  19.5 us
    pallas_call x1, Pallas kernels, shards(): pl.pallas_call(upward_kernel, out_shape=jax.ShapeDtypeStruct((held, 2 * r...  9.26 us
    ppermute x4, starting transfers between devices, shards(): lax.ppermute(part, ('space', 'rhs'), slot_permutation(k))  9.21 us
    ppermute x7, waiting for transfers between devices, swap_cores(): return lax.ppermute(value, 'rhs', [(0, 1), (1, 0)])  3.26 us
    ppermute x7, starting transfers between devices, swap_cores(): return lax.ppermute(value, 'rhs', [(0, 1), (1, 0)])  2.21 us
    pallas_call x1, Pallas kernels, shards(): pl.pallas_call(functools.partial(plan_kernel, 2 * held, split), out_shape...  1.47 us
  transfers between devices with their start and end apart: 11, of which 6 were waited for; matrix products, arithmetic and copies ran while one was open for 0% of the time, Pallas kernels for 32%

profile of v8, /device:TPU:0, one launch (start us, length us, event | category | flops | bytes accessed | tf_op | source)
XLA Modules:
  0.0 69.3 jit_solution(7924902216936863143)
XLA Ops:
  0.6 0.5 collective-permute-start
  1.2 1.4 %fetch.1 = (s32[189,2,128]{2,1,0:T(2,128)S(1)}, s32[16,2,189]{2,1,0:T(2,128)S(1)}, f32[3,128,128]{2,1,0:T(8,128)S(1)}, bf16[128,4,128]{2,1,0:T(4,128)(2,1)S(1)},...) custom-call(s32[189,2,256]{2,1,0:T(2,128)} %bitcast.10, ...), custom_call_target="tpu_custom_call" | custom-call | tf_op jit(solution)/shard_map/fetch/pallas_call | solution.py:409
  2.5 9.3 %upward.1.own_ref = bf16[144,8,256]{2,1,0:T(8,128)(2,1)S(1)} custom-call(s32[256]{0:T(256)S(1)} %get-tuple-element.35.counts_ref, s32[256]{0:T(256)S(1)} %get-tuple-element.36.octants_ref, f32[3,128]{1,0:T(4,128)S(1)} %get-tuple-element.37.freq_ref, f32[3,128,128]{2,1,0:T(8,128)S(1)} %get-tuple-element.38.pos_ref, ...), custom_call_target="tpu_custom_call" | custom-call | tf_op jit(solution)/shard_map/upward/pallas_call | solution.py:418
  11.8 0.4 collective-permute-start.1
  12.2 1.5 %plan.1 = (s32[288,128]{1,0:T(8,128)S(1)}, s32[288,128]{1,0:T(8,128)S(1)}) custom-call(s32[189,2,128]{2,1,0:T(2,128)S(1)} %get-tuple-element.42.leaf_ref, s32[16,2,189]{2,1,0:T(2,128)S(1)} %get-tuple-element.43.parent_ref), custom_call_target="tpu_custom_call" | custom-call | tf_op jit(solution)/shard_map/plan/pallas_call | solution.py:439
  13.7 0.2 collective-permute-done.1.recv_ref
  13.9 1.0 %pack.1 = (bf16[288,8,256]{2,1,0:T(8,128)(2,1)S(1)}, bf16[64,8,256]{2,1,0:T(8,128)(2,1)S(1)}, bf16[64,8,256]{2,1,0:T(8,128)(2,1)S(1)}, bf16[64,8,256]{2,1,0:T(8,128)(2,1)S(1)}, bf16[64,8,256]{2,1,0:T(8,128)(2,1)S(1)}) custom-call(s32[8,48]{1,0:T(8,128)S(1)} %get-tuple-element.48.leaf_ids_ref, s32[8,16]{1,0:T(8,128)S(1)} %get-tuple-element.49.parent_ids_ref, ...), custom_call_target="tpu_custom_call" | custom-call | tf_op jit(solution)/shard_map/pack/pallas_call | solution.py:449
  14.9 5.0 %collective-permute-start.2 = (bf16[64,8,256]{2,1,0:T(8,128)(2,1)S(1)}, bf16[64,8,256]{2,1,0:T(8,128)(2,1)S(1)}, u32[]{:S(2)}, u32[]{:S(2)}) collective-permute-start(bf16[64,8,256]{2,1,0:T(8,128)(2,1)S(1)} %get-tuple-element.56), channel_id=1, source_target_pairs={{0,24},{2,26},{4,28},{6,30},{8,0},{10,2},{12,4},{14,6},{16,8},{18,... | collective-permute-start | bytes 786440 | tf_op jit(solution)/shard_map/ppermute | solution.py:465
  19.9 1.4 %collective-permute-start.3 = (bf16[64,8,256]{2,1,0:T(8,128)(2,1)S(1)}, bf16[64,8,256]{2,1,0:T(8,128)(2,1)S(1)}, u32[]{:S(2)}, u32[]{:S(2)}) collective-permute-start(bf16[64,8,256]{2,1,0:T(8,128)(2,1)S(1)} %get-tuple-element.57), channel_id=1, source_target_pairs={{0,26},{2,28},{4,30},{6,0},{8,2},{10,4},{12,6},{14,8},{16,10},{18,... | collective-permute-start | bytes 786440 | tf_op jit(solution)/shard_map/ppermute | solution.py:465
  21.3 1.4 %collective-permute-start.4 = (bf16[64,8,256]{2,1,0:T(8,128)(2,1)S(1)}, bf16[64,8,256]{2,1,0:T(8,128)(2,1)S(1)}, u32[]{:S(2)}, u32[]{:S(2)}) collective-permute-start(bf16[64,8,256]{2,1,0:T(8,128)(2,1)S(1)} %get-tuple-element.58), channel_id=1, source_target_pairs={{0,28},{2,30},{4,0},{6,2},{8,4},{10,6},{12,8},{14,10},{16,12},{18,... | collective-permute-start | bytes 786440 | tf_op jit(solution)/shard_map/ppermute | solution.py:465
  22.7 1.4 %collective-permute-start.5 = (bf16[64,8,256]{2,1,0:T(8,128)(2,1)S(1)}, bf16[64,8,256]{2,1,0:T(8,128)(2,1)S(1)}, u32[]{:S(2)}, u32[]{:S(2)}) collective-permute-start(bf16[64,8,256]{2,1,0:T(8,128)(2,1)S(1)} %get-tuple-element.59), channel_id=1, source_target_pairs={{0,30},{2,0},{4,2},{6,4},{8,6},{10,8},{12,10},{14,12},{16,14},{18,... | collective-permute-start | bytes 786440 | tf_op jit(solution)/shard_map/ppermute | solution.py:465
  24.1 19.5 %near.1 = (f32[12800,128]{1,0:T(8,128)S(1)}, f32[5056,128]{1,0:T(8,128)S(1)}, f32[144,16,128]{2,1,0:T(8,128)S(1)}) custom-call(s32[36864]{0:T(1024)S(1)} %bitcast.6, bf16[288,8,256]{2,1,0:T(8,128)(2,1)S(1)} %get-tuple-element.52.rows_ref, f32[316,256]{1,0:T(8,128)S(1)} %get-tuple-element.53.trans_ref), custom_call_target="tpu_custom_call" | custom-call | flops 20000000000 | bytes 60000000 | tf_op jit(solution)/shard_map/near/pallas_call | solution.py:472
  43.7 0.1 collective-permute-start.6
  43.8 0.5 collective-permute-start.7
  44.3 0.1 collective-permute-start.8
  44.3 0.4 collective-permute-start.9
  44.8 0.5 collective-permute-done.6.refs_4_
  45.3 0.4 collective-permute-done.7.refs_5_
  45.7 0.4 collective-permute-done.8.refs_6_
  46.0 0.4 collective-permute-done.9.refs_7_
  46.4 19.9 %rest.1 = (f32[144,16,128]{2,1,0:T(8,128)S(1)}, bf16[144,4,256]{2,1,0:T(4,128)(2,1)S(1)}, bf16[144,4,256]{2,1,0:T(4,128)(2,1)S(1)}, f32[12800,128]{1,0:T(8,128)S(1)}) custom-call(s32[36864]{0:T(1024)S(1)} %bitcast.7, s32[36864]{0:T(1024)S(1)} %bitcast.8, f32[12800,128]{1,0:T(8,128)S(1)} %get-tuple-element.54.table_in, ...), custom_call_target="tpu_custom_call", output_to_operand_aliasing={{3}: (2, {}), {0}: (12, {})} | custom-call | tf_op jit(solution)/shard_map/rest/pallas_call | solution.py:486
  66.4 0.2 collective-permute-start.10
  66.6 1.4 %collective-permute-done.10.recv_ref = bf16[144,4,256]{2,1,0:T(4,128)(2,1)S(1)} collective-permute-done((bf16[144,4,256]{2,1,0:T(4,128)(2,1)S(1)}, bf16[144,4,256]{2,1,0:T(4,128)(2,1)S(1)}, u32[]{:S(2)}, u32[]{:S(2)}) %collective-permute-start.10) | collective-permute-done | bytes 294944 | tf_op jit(solution)/shard_map/ppermute | solution.py:36
  68.0 1.3 %local.1 = (f32[256,4,256]{2,1,0:T(4,128)}, f32[32,4,256]{2,1,0:T(4,128)}) custom-call(bf16[144,4,256]{2,1,0:T(4,128)(2,1)S(1)} %get-tuple-element.66.keep_ref, bf16[144,4,256]{2,1,0:T(4,128)(2,1)S(1)} %collective-permute-done.10.recv_ref, bf16[256,256]{1,0:T(8,128)(2,1)S(1)} %copy-done), custom_call_target="tpu_custom_call" | custom-call | tf_op jit(solution)/shard_map/local/pallas_call | solution.py:507
  (7 shorter events, 0.0 us)
Async XLA Ops:
  0.6 1.9 %collective-permute-start = (bf16[256,4,128]{2,1,0:T(4,128)(2,1)}, bf16[256,4,128]{2,1,0:T(4,128)(2,1)S(1)}, u32[]{:S(2)}, u32[]{:S(2)}) collective-permute-start(bf16[256,4,128]{2,1,0:T(4,128)(2,1)} %refs_3_.1), channel_id=1, source_target_pairs={{0,1},{1,0},{2,3},{3,2},{4,5},{5,4},{6,7},{7,6},{8,9},{9,8},{10,11... | collective-permute-start | bytes 786440 | tf_op jit(solution)/shard_map/ppermute | solution.py:36
  11.8 2.1 %collective-permute-start.1 = (bf16[144,8,256]{2,1,0:T(8,128)(2,1)S(1)}, bf16[144,8,256]{2,1,0:T(8,128)(2,1)S(1)}, u32[]{:S(2)}, u32[]{:S(2)}) collective-permute-start(bf16[144,8,256]{2,1,0:T(8,128)(2,1)S(1)} %upward.1.own_ref), channel_id=1, source_target_pairs={{0,1},{1,0},{2,3},{3,2},{4,5},{5,4},{6,7},{7,6},{8,9},{9,8},{10,11... | collective-permute-start | bytes 1769480 | tf_op jit(solution)/shard_map/ppermute | solution.py:36
  14.9 28.8 %collective-permute-start.2 = (bf16[64,8,256]{2,1,0:T(8,128)(2,1)S(1)}, bf16[64,8,256]{2,1,0:T(8,128)(2,1)S(1)}, u32[]{:S(2)}, u32[]{:S(2)}) collective-permute-start(bf16[64,8,256]{2,1,0:T(8,128)(2,1)S(1)} %get-tuple-element.56), channel_id=1, source_target_pairs={{0,24},{2,26},{4,28},{6,30},{8,0},{10,2},{12,4},{14,6},{16,8},{18,... | collective-permute-start | bytes 786440 | tf_op jit(solution)/shard_map/ppermute | solution.py:465
  19.9 23.8 %collective-permute-start.3 = (bf16[64,8,256]{2,1,0:T(8,128)(2,1)S(1)}, bf16[64,8,256]{2,1,0:T(8,128)(2,1)S(1)}, u32[]{:S(2)}, u32[]{:S(2)}) collective-permute-start(bf16[64,8,256]{2,1,0:T(8,128)(2,1)S(1)} %get-tuple-element.57), channel_id=1, source_target_pairs={{0,26},{2,28},{4,30},{6,0},{8,2},{10,4},{12,6},{14,8},{16,10},{18,... | collective-permute-start | bytes 786440 | tf_op jit(solution)/shard_map/ppermute | solution.py:465
  21.3 22.4 %collective-permute-start.4 = (bf16[64,8,256]{2,1,0:T(8,128)(2,1)S(1)}, bf16[64,8,256]{2,1,0:T(8,128)(2,1)S(1)}, u32[]{:S(2)}, u32[]{:S(2)}) collective-permute-start(bf16[64,8,256]{2,1,0:T(8,128)(2,1)S(1)} %get-tuple-element.58), channel_id=1, source_target_pairs={{0,28},{2,30},{4,0},{6,2},{8,4},{10,6},{12,8},{14,10},{16,12},{18,... | collective-permute-start | bytes 786440 | tf_op jit(solution)/shard_map/ppermute | solution.py:465
  22.7 21.0 %collective-permute-start.5 = (bf16[64,8,256]{2,1,0:T(8,128)(2,1)S(1)}, bf16[64,8,256]{2,1,0:T(8,128)(2,1)S(1)}, u32[]{:S(2)}, u32[]{:S(2)}) collective-permute-start(bf16[64,8,256]{2,1,0:T(8,128)(2,1)S(1)} %get-tuple-element.59), channel_id=1, source_target_pairs={{0,30},{2,0},{4,2},{6,4},{8,6},{10,8},{12,10},{14,12},{16,14},{18,... | collective-permute-start | bytes 786440 | tf_op jit(solution)/shard_map/ppermute | solution.py:465
  43.7 1.6 %collective-permute-start.6 = (bf16[64,8,256]{2,1,0:T(8,128)(2,1)S(1)}, bf16[64,8,256]{2,1,0:T(8,128)(2,1)S(1)}, u32[]{:S(2)}, u32[]{:S(2)}) collective-permute-start(bf16[64,8,256]{2,1,0:T(8,128)(2,1)S(1)} %collective-permute-done.2.refs_0_), channel_id=1, source_target_pairs={{0,1},{1,0},{2,3},{3,2},{4,5},{5,4},{6,7},{7,6},{8,9},{9,8},{10,11... | collective-permute-start | bytes 786440 | tf_op jit(solution)/shard_map/ppermute | solution.py:36
  43.8 1.9 %collective-permute-start.7 = (bf16[64,8,256]{2,1,0:T(8,128)(2,1)S(1)}, bf16[64,8,256]{2,1,0:T(8,128)(2,1)S(1)}, u32[]{:S(2)}, u32[]{:S(2)}) collective-permute-start(bf16[64,8,256]{2,1,0:T(8,128)(2,1)S(1)} %collective-permute-done.3.refs_1_), channel_id=1, source_target_pairs={{0,1},{1,0},{2,3},{3,2},{4,5},{5,4},{6,7},{7,6},{8,9},{9,8},{10,11... | collective-permute-start | bytes 786440 | tf_op jit(solution)/shard_map/ppermute | solution.py:36
  44.3 1.8 %collective-permute-start.8 = (bf16[64,8,256]{2,1,0:T(8,128)(2,1)S(1)}, bf16[64,8,256]{2,1,0:T(8,128)(2,1)S(1)}, u32[]{:S(2)}, u32[]{:S(2)}) collective-permute-start(bf16[64,8,256]{2,1,0:T(8,128)(2,1)S(1)} %collective-permute-done.4.refs_2_), channel_id=1, source_target_pairs={{0,1},{1,0},{2,3},{3,2},{4,5},{5,4},{6,7},{7,6},{8,9},{9,8},{10,11... | collective-permute-start | bytes 786440 | tf_op jit(solution)/shard_map/ppermute | solution.py:36
  44.3 2.1 %collective-permute-start.9 = (bf16[64,8,256]{2,1,0:T(8,128)(2,1)S(1)}, bf16[64,8,256]{2,1,0:T(8,128)(2,1)S(1)}, u32[]{:S(2)}, u32[]{:S(2)}) collective-permute-start(bf16[64,8,256]{2,1,0:T(8,128)(2,1)S(1)} %collective-permute-done.5.refs_3_), channel_id=1, source_target_pairs={{0,1},{1,0},{2,3},{3,2},{4,5},{5,4},{6,7},{7,6},{8,9},{9,8},{10,11... | collective-permute-start | bytes 786440 | tf_op jit(solution)/shard_map/ppermute | solution.py:36
  46.4 21.6 %copy-start = (bf16[256,256]{1,0:T(8,128)(2,1)S(1)}, bf16[256,256]{1,0:T(8,128)(2,1)}, u32[]{:S(2)}) copy-start(bf16[256,256]{1,0:T(8,128)(2,1)} %mat_ref.1) | copy-start | bytes 393220
  66.4 1.6 %collective-permute-start.10 = (bf16[144,4,256]{2,1,0:T(4,128)(2,1)S(1)}, bf16[144,4,256]{2,1,0:T(4,128)(2,1)S(1)}, u32[]{:S(2)}, u32[]{:S(2)}) collective-permute-start(bf16[144,4,256]{2,1,0:T(4,128)(2,1)S(1)} %get-tuple-element.67), channel_id=1, source_target_pairs={{0,1},{1,0},{2,3},{3,2},{4,5},{5,4},{6,7},{7,6},{8,9},{9,8},{10,11... | collective-permute-start | bytes 884744 | tf_op jit(solution)/shard_map/ppermute | solution.py:36

commit v9 on v8

--- a/solution.py
+++ b/solution.py
@@ -12,7 +12,7 @@
 BF16 = jnp.bfloat16
 GROUP = 9
 LEAF_UNROLL = 32
-TARGET_GROUP = 16
+TARGET_GROUP = 24
 SIN_POLY = (4.44286790342698, -7.307443431653506, 3.594788153158899, -0.7843741906863176)
 COS_POLY = (
     1.4142134967586113,
@@ -265,7 +265,7 @@
         wave_re, wave_im, shift_re, shift_im = wave[:8], wave[8:], shift[:8], shift[8:]
         reals.append(shift_re * wave_re - shift_im * wave_im)
         imags.append(shift_re * wave_im + shift_im * wave_re)
-        if len(reals) == 3 or k == count - 1:
+        if len(reals) == 1 or k == count - 1:
             total_re, total_im = total_re + tree(reals), total_im + tree(imags)
             reals, imags = [], []
     return total_re, total_im

time: 69.5 us -> 69.5 us (level)
  no operation moved by 1% of the time
where the time goes in v9:
time: 69.5 us; the launch traced here: 69.3 us
  Pallas kernels  53.9 us (78%)
  starting transfers between devices  11.4 us (16%)
  waiting for transfers between devices  3.27 us (5%)
  between operations  0.74 us (1%)
    pallas_call x1, Pallas kernels, shards(): pl.pallas_call(functools.partial(rest_kernel, (slots, cap_l, cap_p, 2 * h...  19.9 us
    pallas_call x1, Pallas kernels, shards(): pl.pallas_call(functools.partial(near_kernel, split), out_shape=[table_sh...  19.6 us
    pallas_call x1, Pallas kernels, shards(): pl.pallas_call(upward_kernel, out_shape=jax.ShapeDtypeStruct((held, 2 * r...  9.26 us
    ppermute x4, starting transfers between devices, shards(): lax.ppermute(part, ('space', 'rhs'), slot_permutation(k))  9.21 us
    ppermute x7, waiting for transfers between devices, swap_cores(): return lax.ppermute(value, 'rhs', [(0, 1), (1, 0)])  3.26 us
    ppermute x7, starting transfers between devices, swap_cores(): return lax.ppermute(value, 'rhs', [(0, 1), (1, 0)])  2.21 us
    pallas_call x1, Pallas kernels, shards(): pl.pallas_call(functools.partial(plan_kernel, 2 * held, split), out_shape...  1.47 us
  transfers between devices with their start and end apart: 11, of which 6 were waited for; matrix products, arithmetic and copies ran while one was open for 0% of the time, Pallas kernels for 32%

profile of v9, /device:TPU:0, one launch (start us, length us, event | category | flops | bytes accessed | tf_op | source)
XLA Modules:
  0.0 69.3 jit_solution(3710723585991818020)
XLA Ops:
  0.6 0.5 collective-permute-start
  1.2 1.4 %fetch.1 = (s32[189,2,128]{2,1,0:T(2,128)S(1)}, s32[16,2,189]{2,1,0:T(2,128)S(1)}, f32[3,128,128]{2,1,0:T(8,128)S(1)}, bf16[128,4,128]{2,1,0:T(4,128)(2,1)S(1)},...) custom-call(s32[189,2,256]{2,1,0:T(2,128)} %bitcast.10, ...), custom_call_target="tpu_custom_call" | custom-call | tf_op jit(solution)/shard_map/fetch/pallas_call | solution.py:409
  2.5 9.3 %upward.1.own_ref = bf16[144,8,256]{2,1,0:T(8,128)(2,1)S(1)} custom-call(s32[256]{0:T(256)S(1)} %get-tuple-element.35.counts_ref, s32[256]{0:T(256)S(1)} %get-tuple-element.36.octants_ref, f32[3,128]{1,0:T(4,128)S(1)} %get-tuple-element.37.freq_ref, f32[3,128,128]{2,1,0:T(8,128)S(1)} %get-tuple-element.38.pos_ref, ...), custom_call_target="tpu_custom_call" | custom-call | tf_op jit(solution)/shard_map/upward/pallas_call | solution.py:418
  11.8 0.4 collective-permute-start.1
  12.2 1.5 %plan.1 = (s32[288,128]{1,0:T(8,128)S(1)}, s32[288,128]{1,0:T(8,128)S(1)}) custom-call(s32[189,2,128]{2,1,0:T(2,128)S(1)} %get-tuple-element.42.leaf_ref, s32[16,2,189]{2,1,0:T(2,128)S(1)} %get-tuple-element.43.parent_ref), custom_call_target="tpu_custom_call" | custom-call | tf_op jit(solution)/shard_map/plan/pallas_call | solution.py:439
  13.7 0.2 collective-permute-done.1.recv_ref
  13.9 1.0 %pack.1 = (bf16[288,8,256]{2,1,0:T(8,128)(2,1)S(1)}, bf16[64,8,256]{2,1,0:T(8,128)(2,1)S(1)}, bf16[64,8,256]{2,1,0:T(8,128)(2,1)S(1)}, bf16[64,8,256]{2,1,0:T(8,128)(2,1)S(1)}, bf16[64,8,256]{2,1,0:T(8,128)(2,1)S(1)}) custom-call(s32[8,48]{1,0:T(8,128)S(1)} %get-tuple-element.48.leaf_ids_ref, s32[8,16]{1,0:T(8,128)S(1)} %get-tuple-element.49.parent_ids_ref, ...), custom_call_target="tpu_custom_call" | custom-call | tf_op jit(solution)/shard_map/pack/pallas_call | solution.py:449
  14.9 5.0 %collective-permute-start.2 = (bf16[64,8,256]{2,1,0:T(8,128)(2,1)S(1)}, bf16[64,8,256]{2,1,0:T(8,128)(2,1)S(1)}, u32[]{:S(2)}, u32[]{:S(2)}) collective-permute-start(bf16[64,8,256]{2,1,0:T(8,128)(2,1)S(1)} %get-tuple-element.56), channel_id=1, source_target_pairs={{0,24},{2,26},{4,28},{6,30},{8,0},{10,2},{12,4},{14,6},{16,8},{18,... | collective-permute-start | bytes 786440 | tf_op jit(solution)/shard_map/ppermute | solution.py:465
  19.9 1.4 %collective-permute-start.3 = (bf16[64,8,256]{2,1,0:T(8,128)(2,1)S(1)}, bf16[64,8,256]{2,1,0:T(8,128)(2,1)S(1)}, u32[]{:S(2)}, u32[]{:S(2)}) collective-permute-start(bf16[64,8,256]{2,1,0:T(8,128)(2,1)S(1)} %get-tuple-element.57), channel_id=1, source_target_pairs={{0,26},{2,28},{4,30},{6,0},{8,2},{10,4},{12,6},{14,8},{16,10},{18,... | collective-permute-start | bytes 786440 | tf_op jit(solution)/shard_map/ppermute | solution.py:465
  21.3 1.4 %collective-permute-start.4 = (bf16[64,8,256]{2,1,0:T(8,128)(2,1)S(1)}, bf16[64,8,256]{2,1,0:T(8,128)(2,1)S(1)}, u32[]{:S(2)}, u32[]{:S(2)}) collective-permute-start(bf16[64,8,256]{2,1,0:T(8,128)(2,1)S(1)} %get-tuple-element.58), channel_id=1, source_target_pairs={{0,28},{2,30},{4,0},{6,2},{8,4},{10,6},{12,8},{14,10},{16,12},{18,... | collective-permute-start | bytes 786440 | tf_op jit(solution)/shard_map/ppermute | solution.py:465
  22.7 1.4 %collective-permute-start.5 = (bf16[64,8,256]{2,1,0:T(8,128)(2,1)S(1)}, bf16[64,8,256]{2,1,0:T(8,128)(2,1)S(1)}, u32[]{:S(2)}, u32[]{:S(2)}) collective-permute-start(bf16[64,8,256]{2,1,0:T(8,128)(2,1)S(1)} %get-tuple-element.59), channel_id=1, source_target_pairs={{0,30},{2,0},{4,2},{6,4},{8,6},{10,8},{12,10},{14,12},{16,14},{18,... | collective-permute-start | bytes 786440 | tf_op jit(solution)/shard_map/ppermute | solution.py:465
  24.1 19.6 %near.1 = (f32[12800,128]{1,0:T(8,128)S(1)}, f32[5056,128]{1,0:T(8,128)S(1)}, f32[144,16,128]{2,1,0:T(8,128)S(1)}) custom-call(s32[36864]{0:T(1024)S(1)} %bitcast.6, bf16[288,8,256]{2,1,0:T(8,128)(2,1)S(1)} %get-tuple-element.52.rows_ref, f32[316,256]{1,0:T(8,128)S(1)} %get-tuple-element.53.trans_ref), custom_call_target="tpu_custom_call" | custom-call | flops 20000000000 | bytes 60000000 | tf_op jit(solution)/shard_map/near/pallas_call | solution.py:472
  43.7 0.1 collective-permute-start.6
  43.8 0.5 collective-permute-start.7
  44.3 0.1 collective-permute-start.8
  44.4 0.4 collective-permute-start.9
  44.8 0.5 collective-permute-done.6.refs_4_
  45.3 0.4 collective-permute-done.7.refs_5_
  45.7 0.4 collective-permute-done.8.refs_6_
  46.1 0.4 collective-permute-done.9.refs_7_
  46.5 19.9 %rest.1 = (f32[144,16,128]{2,1,0:T(8,128)S(1)}, bf16[144,4,256]{2,1,0:T(4,128)(2,1)S(1)}, bf16[144,4,256]{2,1,0:T(4,128)(2,1)S(1)}, f32[12800,128]{1,0:T(8,128)S(1)}) custom-call(s32[36864]{0:T(1024)S(1)} %bitcast.7, s32[36864]{0:T(1024)S(1)} %bitcast.8, f32[12800,128]{1,0:T(8,128)S(1)} %get-tuple-element.54.table_in, ...), custom_call_target="tpu_custom_call", output_to_operand_aliasing={{3}: (2, {}), {0}: (12, {})} | custom-call | tf_op jit(solution)/shard_map/rest/pallas_call | solution.py:486
  66.4 0.2 collective-permute-start.10
  66.6 1.4 %collective-permute-done.10.recv_ref = bf16[144,4,256]{2,1,0:T(4,128)(2,1)S(1)} collective-permute-done((bf16[144,4,256]{2,1,0:T(4,128)(2,1)S(1)}, bf16[144,4,256]{2,1,0:T(4,128)(2,1)S(1)}, u32[]{:S(2)}, u32[]{:S(2)}) %collective-permute-start.10) | collective-permute-done | bytes 294944 | tf_op jit(solution)/shard_map/ppermute | solution.py:36
  68.0 1.3 %local.1 = (f32[256,4,256]{2,1,0:T(4,128)}, f32[32,4,256]{2,1,0:T(4,128)}) custom-call(bf16[144,4,256]{2,1,0:T(4,128)(2,1)S(1)} %get-tuple-element.66.keep_ref, bf16[144,4,256]{2,1,0:T(4,128)(2,1)S(1)} %collective-permute-done.10.recv_ref, bf16[256,256]{1,0:T(8,128)(2,1)S(1)} %copy-done), custom_call_target="tpu_custom_call" | custom-call | tf_op jit(solution)/shard_map/local/pallas_call | solution.py:507
  (7 shorter events, 0.0 us)
Async XLA Ops:
  0.6 1.9 %collective-permute-start = (bf16[256,4,128]{2,1,0:T(4,128)(2,1)}, bf16[256,4,128]{2,1,0:T(4,128)(2,1)S(1)}, u32[]{:S(2)}, u32[]{:S(2)}) collective-permute-start(bf16[256,4,128]{2,1,0:T(4,128)(2,1)} %refs_3_.1), channel_id=1, source_target_pairs={{0,1},{1,0},{2,3},{3,2},{4,5},{5,4},{6,7},{7,6},{8,9},{9,8},{10,11... | collective-permute-start | bytes 786440 | tf_op jit(solution)/shard_map/ppermute | solution.py:36
  11.8 2.1 %collective-permute-start.1 = (bf16[144,8,256]{2,1,0:T(8,128)(2,1)S(1)}, bf16[144,8,256]{2,1,0:T(8,128)(2,1)S(1)}, u32[]{:S(2)}, u32[]{:S(2)}) collective-permute-start(bf16[144,8,256]{2,1,0:T(8,128)(2,1)S(1)} %upward.1.own_ref), channel_id=1, source_target_pairs={{0,1},{1,0},{2,3},{3,2},{4,5},{5,4},{6,7},{7,6},{8,9},{9,8},{10,11... | collective-permute-start | bytes 1769480 | tf_op jit(solution)/shard_map/ppermute | solution.py:36
  14.9 28.8 %collective-permute-start.2 = (bf16[64,8,256]{2,1,0:T(8,128)(2,1)S(1)}, bf16[64,8,256]{2,1,0:T(8,128)(2,1)S(1)}, u32[]{:S(2)}, u32[]{:S(2)}) collective-permute-start(bf16[64,8,256]{2,1,0:T(8,128)(2,1)S(1)} %get-tuple-element.56), channel_id=1, source_target_pairs={{0,24},{2,26},{4,28},{6,30},{8,0},{10,2},{12,4},{14,6},{16,8},{18,... | collective-permute-start | bytes 786440 | tf_op jit(solution)/shard_map/ppermute | solution.py:465
  19.9 23.8 %collective-permute-start.3 = (bf16[64,8,256]{2,1,0:T(8,128)(2,1)S(1)}, bf16[64,8,256]{2,1,0:T(8,128)(2,1)S(1)}, u32[]{:S(2)}, u32[]{:S(2)}) collective-permute-start(bf16[64,8,256]{2,1,0:T(8,128)(2,1)S(1)} %get-tuple-element.57), channel_id=1, source_target_pairs={{0,26},{2,28},{4,30},{6,0},{8,2},{10,4},{12,6},{14,8},{16,10},{18,... | collective-permute-start | bytes 786440 | tf_op jit(solution)/shard_map/ppermute | solution.py:465
  21.3 22.5 %collective-permute-start.4 = (bf16[64,8,256]{2,1,0:T(8,128)(2,1)S(1)}, bf16[64,8,256]{2,1,0:T(8,128)(2,1)S(1)}, u32[]{:S(2)}, u32[]{:S(2)}) collective-permute-start(bf16[64,8,256]{2,1,0:T(8,128)(2,1)S(1)} %get-tuple-element.58), channel_id=1, source_target_pairs={{0,28},{2,30},{4,0},{6,2},{8,4},{10,6},{12,8},{14,10},{16,12},{18,... | collective-permute-start | bytes 786440 | tf_op jit(solution)/shard_map/ppermute | solution.py:465
  22.7 21.1 %collective-permute-start.5 = (bf16[64,8,256]{2,1,0:T(8,128)(2,1)S(1)}, bf16[64,8,256]{2,1,0:T(8,128)(2,1)S(1)}, u32[]{:S(2)}, u32[]{:S(2)}) collective-permute-start(bf16[64,8,256]{2,1,0:T(8,128)(2,1)S(1)} %get-tuple-element.59), channel_id=1, source_target_pairs={{0,30},{2,0},{4,2},{6,4},{8,6},{10,8},{12,10},{14,12},{16,14},{18,... | collective-permute-start | bytes 786440 | tf_op jit(solution)/shard_map/ppermute | solution.py:465
  43.7 1.6 %collective-permute-start.6 = (bf16[64,8,256]{2,1,0:T(8,128)(2,1)S(1)}, bf16[64,8,256]{2,1,0:T(8,128)(2,1)S(1)}, u32[]{:S(2)}, u32[]{:S(2)}) collective-permute-start(bf16[64,8,256]{2,1,0:T(8,128)(2,1)S(1)} %collective-permute-done.2.refs_0_), channel_id=1, source_target_pairs={{0,1},{1,0},{2,3},{3,2},{4,5},{5,4},{6,7},{7,6},{8,9},{9,8},{10,11... | collective-permute-start | bytes 786440 | tf_op jit(solution)/shard_map/ppermute | solution.py:36
  43.8 1.9 %collective-permute-start.7 = (bf16[64,8,256]{2,1,0:T(8,128)(2,1)S(1)}, bf16[64,8,256]{2,1,0:T(8,128)(2,1)S(1)}, u32[]{:S(2)}, u32[]{:S(2)}) collective-permute-start(bf16[64,8,256]{2,1,0:T(8,128)(2,1)S(1)} %collective-permute-done.3.refs_1_), channel_id=1, source_target_pairs={{0,1},{1,0},{2,3},{3,2},{4,5},{5,4},{6,7},{7,6},{8,9},{9,8},{10,11... | collective-permute-start | bytes 786440 | tf_op jit(solution)/shard_map/ppermute | solution.py:36
  44.3 1.8 %collective-permute-start.8 = (bf16[64,8,256]{2,1,0:T(8,128)(2,1)S(1)}, bf16[64,8,256]{2,1,0:T(8,128)(2,1)S(1)}, u32[]{:S(2)}, u32[]{:S(2)}) collective-permute-start(bf16[64,8,256]{2,1,0:T(8,128)(2,1)S(1)} %collective-permute-done.4.refs_2_), channel_id=1, source_target_pairs={{0,1},{1,0},{2,3},{3,2},{4,5},{5,4},{6,7},{7,6},{8,9},{9,8},{10,11... | collective-permute-start | bytes 786440 | tf_op jit(solution)/shard_map/ppermute | solution.py:36
  44.4 2.1 %collective-permute-start.9 = (bf16[64,8,256]{2,1,0:T(8,128)(2,1)S(1)}, bf16[64,8,256]{2,1,0:T(8,128)(2,1)S(1)}, u32[]{:S(2)}, u32[]{:S(2)}) collective-permute-start(bf16[64,8,256]{2,1,0:T(8,128)(2,1)S(1)} %collective-permute-done.5.refs_3_), channel_id=1, source_target_pairs={{0,1},{1,0},{2,3},{3,2},{4,5},{5,4},{6,7},{7,6},{8,9},{9,8},{10,11... | collective-permute-start | bytes 786440 | tf_op jit(solution)/shard_map/ppermute | solution.py:36
  46.5 21.6 %copy-start = (bf16[256,256]{1,0:T(8,128)(2,1)S(1)}, bf16[256,256]{1,0:T(8,128)(2,1)}, u32[]{:S(2)}) copy-start(bf16[256,256]{1,0:T(8,128)(2,1)} %mat_ref.1) | copy-start | bytes 393220
  66.4 1.6 %collective-permute-start.10 = (bf16[144,4,256]{2,1,0:T(4,128)(2,1)S(1)}, bf16[144,4,256]{2,1,0:T(4,128)(2,1)S(1)}, u32[]{:S(2)}, u32[]{:S(2)}) collective-permute-start(bf16[144,4,256]{2,1,0:T(4,128)(2,1)S(1)} %get-tuple-element.67), channel_id=1, source_target_pairs={{0,1},{1,0},{2,3},{3,2},{4,5},{5,4},{6,7},{7,6},{8,9},{9,8},{10,11... | collective-permute-start | bytes 884744 | tf_op jit(solution)/shard_map/ppermute | solution.py:36
